TPU v7x, 256 devices: a whole 4x4x8 slice. The times are simulated.
256 devices in a mesh: row: 8 (over z), col: 32 (over y, x, core).
Axes of the slice: x: 4, y: 4, z: 8, core: 2. Of those that a mesh axis runs over, the one named last changes fastest.
Arguments:
- amps: bfloat16 [384, 131072], P('row', 'col'), may hold values from -6 to 6
- integrals: bfloat16 [131072, 8192], P('col', 'row'), may hold values from -0.046875 to 0.046875
- cd_first: int32 [131072], P('col'), may hold values from 0 to 2399
- cd_second: int32 [131072], P('col'), may hold values from 0 to 2399
- ab_first: int32 [8192], P('row'), may hold values from 0 to 2399
- ab_second: int32 [8192], P('row'), may hold values from 0 to 2399
- occ_first: int32 [384], P('col'), may hold values from 0 to 199
- occ_second: int32 [384], P('col'), may hold values from 0 to 199
- virt_irrep: int32 [2400], replicated, may hold values from 0 to 7
- occ_energy: float32 [200], replicated, may hold values from -2 to -0.5
- virt_energy: float32 [2400], replicated, may hold values from 0.2 to 3
Outputs:
- update: float32 [384, 8192], P('col', 'row')
All inputs are finite; a program needn't handle non-finite values.
Results may differ from a plain program's by a relative error of at most 0.0003.
Values may be sent and summed in bfloat16 or wider, within the bound.
No kernel may reach another device: no remote copies, remote signals or barrier semaphores. Data moves between devices by JAX's collectives and lax.ppermute only.
A program may use at most 64 MiB of HBM per device.

v0:
```python
import jax
import jax.numpy as jnp
from jax import lax
from jax.sharding import PartitionSpec as P


def table_lookup(values_table, positions):
    row_width = 64
    row_count = -(-values_table.shape[0] // row_width)
    padded_table = jnp.pad(
        values_table, (0, row_count * row_width - values_table.shape[0])
    ).reshape(row_count, row_width)
    high_hot = (
        (positions // row_width)[:, None] == jnp.arange(row_count, dtype=jnp.int32)[None, :]
    ).astype(jnp.float32)
    low_hot = (
        (positions % row_width)[:, None] == jnp.arange(row_width, dtype=jnp.int32)[None, :]
    ).astype(jnp.float32)
    picked = jnp.dot(
        high_hot, padded_table, precision=lax.Precision.HIGHEST, preferred_element_type=jnp.float32
    )
    return jnp.sum(picked * low_hot, axis=1)


def irrep_of(labels_float, first_orb, second_orb):
    first_label = table_lookup(labels_float, first_orb).astype(jnp.int32)
    second_label = table_lookup(labels_float, second_orb).astype(jnp.int32)
    return jnp.bitwise_xor(first_label, second_label)


def on_device(
    amps,
    integrals,
    cd_first,
    cd_second,
    ab_first,
    ab_second,
    occ_first,
    occ_second,
    virt_irrep,
    occ_energy,
    virt_energy,
):
    labels_float = virt_irrep.astype(jnp.float32)
    irrep_cd = irrep_of(labels_float, cd_first, cd_second)
    irrep_ab = irrep_of(labels_float, ab_first, ab_second)
    masked = jnp.where(irrep_cd[:, None] == irrep_ab[None, :], integrals, jnp.zeros_like(integrals))
    partial_sums = jnp.dot(
        lax.all_gather(amps, "row", axis=0, tiled=True), masked, preferred_element_type=jnp.float32
    )
    own_rows = occ_first.shape[0]
    summed = lax.psum(partial_sums, "col")
    ladder = lax.dynamic_slice_in_dim(summed, lax.axis_index("col") * own_rows, own_rows, 0)
    virt_part = table_lookup(virt_energy, ab_first) + table_lookup(virt_energy, ab_second)
    occ_part = table_lookup(occ_energy, occ_first) + table_lookup(occ_energy, occ_second)
    denom = virt_part[None, :] - occ_part[:, None]
    return ladder / denom


def solution(mesh):
    in_specs = (
        P("row", "col"),
        P("col", "row"),
        P("col"),
        P("col"),
        P("row"),
        P("row"),
        P("col"),
        P("col"),
        P(),
        P(),
        P(),
    )
    out_specs = P("col", "row")
    return jax.shard_map(
        on_device, mesh=mesh, in_specs=in_specs, out_specs=out_specs, check_vma=False
    )
```

profile of v0, /device:TPU:1, one launch (start us, length us, event | category | flops | bytes accessed | tf_op | source)
XLA Modules:
  0.0 190.4 jit_solution(7204045527473177920)
XLA Ops:
  6.5 0.7 all-gather.2.cloned.1.call-update
  7.3 0.0 all-reduce.5.cloned.1.call-start
  7.3 0.7 convert_element_type.57
  8.0 0.1 reshape.50
  8.1 0.7 add_select_fusion.5
  8.8 0.6 fusion.8
  9.4 0.7 add_select_fusion.7
  10.1 0.6 fusion.7
  10.7 0.7 add_select_fusion.2
  11.4 0.7 fusion.5
  12.1 0.7 add_select_fusion
  12.8 0.7 fusion.6
  13.6 0.0 copy-start
  13.6 44.1 %all-gather.2.cloned.1.call-done = bf16[384,4096]{1,0:T(8,128)(2,1)} async-done(((bf16[48,4096]{1,0:T(8,128)(2,1)}), bf16[384,4096]{1,0:T(8,128)(2,1)}) %all-gather.2.cloned.1.call-update) | async-done | bytes 3145744 | tf_op jit(solution)/shard_map/all_gather | solution.py:49
  57.7 9.0 %fusion.4 = f32[384,1024]{1,0:T(8,128)} fusion(bf16[384,4096]{1,0:T(8,128)(2,1)} %all-gather.2.cloned.1.call-done, bf16[4096,1024]{1,0:T(8,128)(2,1)} %param.12, s32[1024]{0:T(1024)S(1)} %convert_xor_fusion.1, s32[4096]{0:T(1024)S(1)} %convert_xor_fusion), kind=kOutput, calls=%fused_computation.7 | convolution fusion | flops 3229614080 | bytes 13127680 | tf_op jit(solution)/shard_map/dot_general | solution.py:48
  66.7 0.0 all-reduce.5.cloned.1.call-update
  66.8 0.1 reshape.52
  66.9 0.1 reshape.51
  67.0 0.3 fusion.11
  67.3 0.3 fusion.12
  67.6 0.6 fusion.10
  68.2 0.6 fusion.9
  68.8 113.1 %all-reduce.5.cloned.1.call-done = f32[384,1024]{1,0:T(8,128)} async-done(((f32[384,1024]{1,0:T(8,128)}), f32[384,1024]{1,0:T(8,128)}) %all-reduce.5.cloned.1.call-update) | async-done | bytes 1572880 | tf_op jit(solution)/shard_map/psum | solution.py:52
  181.9 1.6 subtract_divide_fusion
  (17 shorter events, 0.1 us)
Async XLA Ops:
  6.5 51.2 %all-gather.2.cloned.1.call-start = ((), (), s32[]{:S(2)}) async-start(), calls=%async_computation | async-start | bytes 3538944 | tf_op jit(solution)/shard_map/all_gather | solution.py:49
  7.3 174.7 %all-reduce.5.cloned.1.call-start = ((), (), s32[]{:S(2)}) async-start(), calls=%async_computation.1 | async-start | bytes 3145728 | tf_op jit(solution)/shard_map/psum | solution.py:52
  13.5 53.2 %copy-start.2 = (s32[12]{0:T(128)S(1)}, s32[12]{0:T(128)}, u32[]{:S(2)}) copy-start(s32[12]{0:T(128)} %param.17) | copy-start | bytes 148
  13.6 53.2 %copy-start.1 = (f32[200]{0:T(256)S(1)}, f32[200]{0:T(256)}, u32[]{:S(2)}) copy-start(f32[200]{0:T(256)} %param.20) | copy-start | bytes 2404
  13.6 53.3 %copy-start = (f32[2400]{0:T(1024)S(1)}, f32[2400]{0:T(1024)}, u32[]{:S(2)}) copy-start(f32[2400]{0:T(1024)} %param.21) | copy-start | bytes 28804
  13.6 53.7 %copy-start.3 = (s32[12]{0:T(128)S(1)}, s32[12]{0:T(128)}, u32[]{:S(2)}) copy-start(s32[12]{0:T(128)} %param.18) | copy-start | bytes 148
Sparse Core Ops, SparseCore 0:
  9.1 48.5 all-gather.1
  66.9 114.9 all-reduce.4
where the time goes:
time: 191 us; the launch traced here: 190 us
  waiting for transfers between devices  158 us (83%)
  between operations  13.5 us (7%)
  matrix products  13.3 us (7%)
  other arithmetic  5.24 us (3%)
    psum x1, waiting for transfers between devices, on_device(): summed = lax.psum(partial_sums, 'col')  113 us
    all_gather x1, waiting for transfers between devices, on_device(): lax.all_gather(amps, 'row', axis=0, tiled=True)  44.1 us
    dot_general x1, matrix products, on_device(): jnp.dot(lax.all_gather(amps, 'row', axis=0, tiled=True), masked, preferre...  9 us
    dot_general x8, matrix products, table_lookup(): jnp.dot(high_hot, padded_table, precision=lax.Precision.HIGHEST, preferre...  4.28 us
  transfers between devices with their start and end apart: 2, of which 2 were waited for; matrix products, arithmetic and copies ran while one was open for 4% of the time, Pallas kernels for 0%

commit v1 on v0

v1 whole, which is shorter than its diff:
```python
import jax
import jax.numpy as jnp
from jax import lax
from jax.experimental import pallas as pl
from jax.experimental.pallas import tpu as pltpu
from jax.sharding import Mesh, PartitionSpec as P

LANES = 128
K_BLOCK = 512
ORDER = (0, -1, 1, -2, 2, -3, 3, 4)


def lookup(table_ref, rows, index):
    high = index // LANES
    low = index % LANES
    picked = jnp.zeros(index.shape, table_ref.dtype)
    for row in range(rows):
        line = jnp.broadcast_to(table_ref[row : row + 1, :], index.shape)
        value = jnp.take_along_axis(line, low, axis=1, mode="promise_in_bounds")
        picked = jnp.where(high == row, value, picked)
    return picked


def tables_kernel(cd1, cd2, ab1, ab2, occ, irrep, virt, occ_energy, cd_out, ab_out, virt_out, occ_out):
    rows = irrep.shape[0]
    for tile in range(cd1.shape[0] // 8):
        part = slice(8 * tile, 8 * tile + 8)
        label = lookup(irrep, rows, cd1[part, :]) ^ lookup(irrep, rows, cd2[part, :])
        cd_out[part, :] = label.astype(jnp.float32)
    label = lookup(irrep, rows, ab1[...]) ^ lookup(irrep, rows, ab2[...])
    ab_out[...] = label.astype(jnp.float32)
    virt_out[...] = lookup(virt, rows, ab1[...]) + lookup(virt, rows, ab2[...])
    picked = lookup(occ_energy, occ_energy.shape[0], occ[...])
    both = picked[0:1, :] + picked[1:2, :]
    column = jnp.broadcast_to(both, (LANES, LANES)).T
    occ_out[...] = column[: occ_out.shape[0], :]


def ladder_kernel(where, cd, ab, values, own, *refs):
    pieces = refs[:14]
    keep, send, total, masked = refs[14:]
    step = pl.program_id(0)
    steps = pl.num_programs(0)

    @pl.when(step == 0)
    def _():
        total[...] = jnp.zeros_like(total)

    for part in range(K_BLOCK // LANES):
        line = cd[pl.ds(step * (K_BLOCK // LANES) + part, 1), :]
        label = jnp.broadcast_to(line, (LANES, LANES)).T.astype(jnp.bfloat16)
        down = slice(part * LANES, part * LANES + LANES)
        for lane in range(values.shape[1] // LANES):
            across = slice(lane * LANES, lane * LANES + LANES)
            other = jnp.broadcast_to(ab[lane : lane + 1, :], (LANES, LANES)).astype(jnp.bfloat16)
            block = values[down, across]
            masked[down, across] = jnp.where(label == other, block, jnp.zeros_like(block))

    def accumulate(half):
        offset = pl.multiple_of((step - half * (steps // 2)) * K_BLOCK, K_BLOCK)
        left = [own[:, pl.ds(pl.multiple_of(step * K_BLOCK, K_BLOCK), K_BLOCK)]]
        left += [pieces[2 * i + half][:, pl.ds(offset, K_BLOCK)] for i in range(7)]
        total[...] += jnp.dot(
            jnp.concatenate(left, axis=0), masked[...], preferred_element_type=jnp.float32
        )

    @pl.when(step < steps // 2)
    def _():
        accumulate(0)

    @pl.when(step >= steps // 2)
    def _():
        accumulate(1)

    @pl.when(step == steps - 1)
    def _():
        layer = where[0]
        first_core = where[1] == 0
        rows = own.shape[0] // 4
        for place, shift in enumerate(ORDER):
            shard = lax.rem(layer + (shift + 8), 8)
            for high in range(2):
                at = place * own.shape[0] + 2 * high * rows
                even = total[at : at + rows, :]
                odd = total[at + rows : at + 2 * rows, :]
                kept = jnp.where(first_core, even, odd)
                sent = jnp.where(first_core, odd, even)
                for lane in range(kept.shape[1] // LANES):
                    across = slice(lane * LANES, lane * LANES + LANES)
                    down = slice(lane * rows, lane * rows + rows)
                    keep[2 * shard + high, down, :] = kept[:, across]
                    send[2 * shard + high, down, :] = sent[:, across]


def finish_kernel(parts, virt, occ, out):
    rows = out.shape[0]
    summed = jnp.sum(parts[...], axis=0)
    for lane in range(out.shape[1] // LANES):
        ladder = summed[lane * rows : lane * rows + rows, :]
        denom = virt[lane : lane + 1, :] - occ[:rows, :]
        out[:, lane * LANES : lane * LANES + LANES] = ladder / denom


def as_table(values):
    size = -(-values.shape[0] // 1024) * 1024
    return jnp.pad(values, (0, size - values.shape[0])).reshape(size // LANES, LANES)


def on_device(amps, integrals, cd1, cd2, ab1, ab2, occ1, occ2, irrep, occ_energy, virt_energy):
    depth = amps.shape[1]
    width = integrals.shape[1]
    rows = occ1.shape[0]
    forward = [(i, (i + 1) % 8) for i in range(8)]
    backward = [(i, (i - 1) % 8) for i in range(8)]
    up = [amps[:, : depth // 2], amps[:, depth // 2 :]]
    down = list(up)
    pieces = []
    for _ in range(3):
        up[0] = lax.ppermute(up[0], "z", forward)
        up[1] = lax.ppermute(up[1], "z", forward)
        down[0] = lax.ppermute(down[0], "z", backward)
        down[1] = lax.ppermute(down[1], "z", backward)
        pieces += up + down
    pieces += [lax.ppermute(up[0], "z", forward), lax.ppermute(down[1], "z", backward)]

    vmem = pl.BlockSpec(memory_space=pltpu.VMEM)
    occ = jnp.zeros((8, LANES), jnp.int32)
    occ = occ.at[0, :rows].set(occ1).at[1, :rows].set(occ2)
    square = lambda x: x.reshape(x.shape[0] // LANES, LANES)
    cd, ab, virt, occ_part = pl.pallas_call(
        tables_kernel,
        out_shape=(
            jax.ShapeDtypeStruct((depth // LANES, LANES), jnp.float32),
            jax.ShapeDtypeStruct((width // LANES, LANES), jnp.float32),
            jax.ShapeDtypeStruct((width // LANES, LANES), jnp.float32),
            jax.ShapeDtypeStruct((16, LANES), jnp.float32),
        ),
        in_specs=[vmem] * 8,
        out_specs=(vmem,) * 4,
    )(
        square(cd1), square(cd2), square(ab1), square(ab2), occ,
        as_table(irrep), as_table(virt_energy), as_table(occ_energy),
    )

    where = jnp.stack([lax.axis_index("z"), lax.axis_index("core")]).astype(jnp.int32)
    block = jax.ShapeDtypeStruct((16, rows * width // LANES, LANES), jnp.float32)
    keep, send = pl.pallas_call(
        ladder_kernel,
        out_shape=(block, block),
        grid_spec=pltpu.PrefetchScalarGridSpec(
            num_scalar_prefetch=1,
            grid=(depth // K_BLOCK,),
            in_specs=[vmem, vmem, pl.BlockSpec((K_BLOCK, width), lambda k, where: (k, 0)), vmem]
            + [vmem] * 14,
            out_specs=(vmem, vmem),
            scratch_shapes=[
                pltpu.VMEM((8 * amps.shape[0], width), jnp.float32),
                pltpu.VMEM((K_BLOCK, width), jnp.bfloat16),
            ],
        ),
        compiler_params=pltpu.CompilerParams(vmem_limit_bytes=32 * 1024 * 1024),
    )(where, cd, ab, integrals, amps, *pieces)

    both = keep + lax.ppermute(send, "core", [(0, 1), (1, 0)])
    parts = lax.all_to_all(both, ("y", "x"), 0, 0, tiled=True)
    return pl.pallas_call(
        finish_kernel,
        out_shape=jax.ShapeDtypeStruct((rows, width), jnp.float32),
        in_specs=[vmem] * 3,
        out_specs=vmem,
    )(parts, virt, occ_part)


def solution(mesh):
    fine = Mesh(mesh.devices.reshape(8, 4, 4, 2), ("z", "y", "x", "core"))
    col = ("y", "x", "core")
    in_specs = (
        P("z", col), P(col, "z"), P(col), P(col), P("z"), P("z"), P(col), P(col), P(), P(), P(),
    )
    return jax.shard_map(
        on_device, mesh=fine, in_specs=in_specs, out_specs=P(col, "z"), check_vma=False
    )
```

time: 191 us -> 80.7 us (0.42)
  waiting for transfers between devices: 158 us -> 11.9 us
  starting transfers between devices: 0.04 us -> 23.9 us
  blocking collectives: 0 us -> 20.5 us
  between operations: 13.5 us -> 0.05 us
  matrix products: 13.3 us -> 0 us
  local copies, waits for them, and re-layouts: 0.27 us -> 12.1 us
  Pallas kernels: 0 us -> 11.5 us
  other arithmetic: 5.24 us -> 0.16 us
    psum x1 -> x0, waiting for transfers between devices: 113 us -> none  [on_device(): summed = lax.psum(partial_sums, 'col')]
    all_gather x1 -> x0, waiting for transfers between devices: 44.1 us -> none  [on_device(): lax.all_gather(amps, 'row', axis=0, tiled=True)]
    ppermute x0 -> x15, starting transfers between devices: none -> 23.9 us  [the longest x3 11.1 us: on_device(): down[1] = lax.ppermute(down[1], 'z', backward)]
    all_to_all x0 -> x1, blocking collectives: none -> 20.5 us  [on_device(): parts = lax.all_to_all(both, ('y', 'x'), 0, 0, tiled=True)]
    dot_general x9 -> x0, matrix products: 13.3 us -> none  [the longest x1 9 us: on_device(): jnp.dot(lax.all_gather(amps, 'row', axis=0, tiled=True), masked, preferre...]
    ppermute x0 -> x15, waiting for transfers between devices: none -> 11.9 us  [the longest x3 4.25 us: on_device(): up[1] = lax.ppermute(up[1], 'z', forward)]
    pallas_call x0 -> x3, Pallas kernels: none -> 11.5 us  [the longest x1 7.84 us: on_device(): pl.pallas_call(ladder_kernel, out_shape=(block, block), grid_spec=pltpu.P...]
    unnamed x8 -> x10, local copies, waits for them, and re-layouts: 0.03 us -> 5.77 us
  transfers between devices with their start and end apart: 2 -> 15, of which waited for: 2 -> 8; matrix products, arithmetic and copies ran while one was open for 4% -> 7% of each run, Pallas kernels for 0% -> 2%
where the time goes in v1:
time: 80.7 us; the launch traced here: 80.2 us
  starting transfers between devices  23.9 us (30%)
  blocking collectives  20.5 us (25%)
  local copies, waits for them, and re-layouts  12.1 us (15%)
  waiting for transfers between devices  11.9 us (15%)
  Pallas kernels  11.5 us (14%)
    all_to_all x1, blocking collectives, on_device(): parts = lax.all_to_all(both, ('y', 'x'), 0, 0, tiled=True)  20.5 us
    ppermute x3, starting transfers between devices, on_device(): down[1] = lax.ppermute(down[1], 'z', backward)  11.1 us
    ppermute x3, starting transfers between devices, on_device(): down[0] = lax.ppermute(down[0], 'z', backward)  8.05 us
    pallas_call x1, Pallas kernels, on_device(): pl.pallas_call(ladder_kernel, out_shape=(block, block), grid_spec=pltpu.P...  7.84 us
    unnamed x10, local copies, waits for them, and re-layouts  5.77 us
    ppermute x3, waiting for transfers between devices, on_device(): up[1] = lax.ppermute(up[1], 'z', forward)  4.25 us
    ppermute x1, starting transfers between devices, on_device(): both = keep + lax.ppermute(send, 'core', [(0, 1), (1, 0)])  3.95 us
    reshape x3, local copies, waits for them, and re-layouts, as_table(): jnp.pad(values, (0, size - values.shape[0])).reshape(size // LANES, LANES)  3.89 us
  transfers between devices with their start and end apart: 15, of which 8 were waited for; matrix products, arithmetic and copies ran while one was open for 7% of the time, Pallas kernels for 2%

profile of v1, /device:TPU:1, one launch (start us, length us, event | category | flops | bytes accessed | tf_op | source)
XLA Modules:
  0.0 80.2 jit_solution(5343384930927657000)
XLA Ops:
  0.0 1.0 %fusion = (bf16[48,2048]{1,0:T(8,128)(2,1)S(1)}, bf16[48,2048]{1,0:T(8,128)(2,1)S(1)}) fusion(bf16[48,4096]{1,0:T(8,128)(2,1)} %own.1), kind=kLoop, calls=%fused_computation.4 | loop fusion | bytes 786432 | tf_op jit(solution)/shard_map/slice | solution.py:115
  1.1 6.5 %collective-permute-start.3 = (bf16[48,2048]{1,0:T(8,128)(2,1)S(1)}, bf16[48,2048]{1,0:T(8,128)(2,1)S(1)}, u32[]{:S(2)}, u32[]{:S(2)}) collective-permute-start(bf16[48,2048]{1,0:T(8,128)(2,1)S(1)} %get-tuple-element.41), channel_id=1, source_target_pairs={{0,224},{32,0},{64,32},{96,64},{128,96},{160,128},{192,160},{224,1... | collective-permute-start | bytes 589832 | tf_op jit(solution)/shard_map/ppermute | solution.py:122
  7.5 2.7 %collective-permute-start.2 = (bf16[48,2048]{1,0:T(8,128)(2,1)S(1)}, bf16[48,2048]{1,0:T(8,128)(2,1)S(1)}, u32[]{:S(2)}, u32[]{:S(2)}) collective-permute-start(bf16[48,2048]{1,0:T(8,128)(2,1)S(1)} %get-tuple-element.42), channel_id=1, source_target_pairs={{0,224},{32,0},{64,32},{96,64},{128,96},{160,128},{192,160},{224,1... | collective-permute-start | bytes 589832 | tf_op jit(solution)/shard_map/ppermute | solution.py:121
  10.2 0.9 %collective-permute-done.3.refs_3_ = bf16[48,2048]{1,0:T(8,128)(2,1)S(1)} collective-permute-done((bf16[48,2048]{1,0:T(8,128)(2,1)S(1)}, bf16[48,2048]{1,0:T(8,128)(2,1)S(1)}, u32[]{:S(2)}, u32[]{:S(2)}) %collective-permute-start.3) | collective-permute-done | bytes 196640 | tf_op jit(solution)/shard_map/ppermute | solution.py:122
  11.1 3.4 %collective-permute-start.7 = (bf16[48,2048]{1,0:T(8,128)(2,1)S(1)}, bf16[48,2048]{1,0:T(8,128)(2,1)S(1)}, u32[]{:S(2)}, u32[]{:S(2)}) collective-permute-start(bf16[48,2048]{1,0:T(8,128)(2,1)S(1)} %collective-permute-done.3.refs_3_), channel_id=1, source_target_pairs={{0,224},{32,0},{64,32},{96,64},{128,96},{160,128},{192,160},{224,1... | collective-permute-start | bytes 589832 | tf_op jit(solution)/shard_map/ppermute | solution.py:122
  15.2 0.7 scatter.9.occ
  15.9 2.5 %collective-permute-done.1.refs_1_ = bf16[48,2048]{1,0:T(8,128)(2,1)S(1)} collective-permute-done((bf16[48,2048]{1,0:T(8,128)(2,1)S(1)}, bf16[48,2048]{1,0:T(8,128)(2,1)S(1)}, u32[]{:S(2)}, u32[]{:S(2)}) %collective-permute-start.1) | collective-permute-done | bytes 196640 | tf_op jit(solution)/shard_map/ppermute | solution.py:120
  18.4 2.7 %collective-permute-start.6 = (bf16[48,2048]{1,0:T(8,128)(2,1)S(1)}, bf16[48,2048]{1,0:T(8,128)(2,1)S(1)}, u32[]{:S(2)}, u32[]{:S(2)}) collective-permute-start(bf16[48,2048]{1,0:T(8,128)(2,1)S(1)} %collective-permute-done.2.refs_2_), channel_id=1, source_target_pairs={{0,224},{32,0},{64,32},{96,64},{128,96},{160,128},{192,160},{224,1... | collective-permute-start | bytes 589832 | tf_op jit(solution)/shard_map/ppermute | solution.py:121
  21.1 1.2 %collective-permute-start.11 = (bf16[48,2048]{1,0:T(8,128)(2,1)S(1)}, bf16[48,2048]{1,0:T(8,128)(2,1)S(1)}, u32[]{:S(2)}, u32[]{:S(2)}) collective-permute-start(bf16[48,2048]{1,0:T(8,128)(2,1)S(1)} %collective-permute-done.7.refs_7_), channel_id=1, source_target_pairs={{0,224},{32,0},{64,32},{96,64},{128,96},{160,128},{192,160},{224,1... | collective-permute-start | bytes 589832 | tf_op jit(solution)/shard_map/ppermute | solution.py:122
  22.6 1.3 %pad_bitcast_fusion.1.irrep = s32[24,128]{1,0:T(8,128)} fusion(s32[2400]{0:T(1024)} %param.23), kind=kLoop, calls=%fused_computation.1 | loop fusion | bytes 21888 | tf_op jit(solution)/shard_map/reshape | solution.py:106
  23.9 1.3 %pad_bitcast_fusion.virt = f32[24,128]{1,0:T(8,128)} fusion(f32[2400]{0:T(1024)} %param.25), kind=kLoop, calls=%fused_computation | loop fusion | bytes 21888 | tf_op jit(solution)/shard_map/reshape | solution.py:106
  25.2 1.1 %collective-permute-done.5.refs_5_ = bf16[48,2048]{1,0:T(8,128)(2,1)S(1)} collective-permute-done((bf16[48,2048]{1,0:T(8,128)(2,1)S(1)}, bf16[48,2048]{1,0:T(8,128)(2,1)S(1)}, u32[]{:S(2)}, u32[]{:S(2)}) %collective-permute-start.5) | collective-permute-done | bytes 196640 | tf_op jit(solution)/shard_map/ppermute | solution.py:120
  26.3 2.7 %collective-permute-start.10 = (bf16[48,2048]{1,0:T(8,128)(2,1)S(1)}, bf16[48,2048]{1,0:T(8,128)(2,1)S(1)}, u32[]{:S(2)}, u32[]{:S(2)}) collective-permute-start(bf16[48,2048]{1,0:T(8,128)(2,1)S(1)} %collective-permute-done.6.refs_6_), channel_id=1, source_target_pairs={{0,224},{32,0},{64,32},{96,64},{128,96},{160,128},{192,160},{224,1... | collective-permute-start | bytes 589832 | tf_op jit(solution)/shard_map/ppermute | solution.py:121
  29.4 0.9 %collective-permute-done.8.refs_8_ = bf16[48,2048]{1,0:T(8,128)(2,1)S(1)} collective-permute-done((bf16[48,2048]{1,0:T(8,128)(2,1)S(1)}, bf16[48,2048]{1,0:T(8,128)(2,1)S(1)}, u32[]{:S(2)}, u32[]{:S(2)}) %collective-permute-start.8) | collective-permute-done | bytes 196640 | tf_op jit(solution)/shard_map/ppermute | solution.py:119
  30.5 1.3 %pad_bitcast_fusion.2.occ_energy = f32[8,128]{1,0:T(8,128)} fusion(f32[200]{0:T(256)} %param.24), kind=kLoop, calls=%fused_computation.2 | loop fusion | bytes 4896 | tf_op jit(solution)/shard_map/reshape | solution.py:106
  31.7 1.9 %shard_map.109 = (f32[32,128]{1,0:T(8,128)}, f32[8,128]{1,0:T(8,128)}, f32[8,128]{1,0:T(8,128)}, f32[16,128]{1,0:T(8,128)}) custom-call(s32[32,128]{1,0:T(8,128)} %bitcast.14, s32[32,128]{1,0:T(8,128)} %bitcast.15, s32[8,128]{1,0:T(8,128)} %bitcast.16, s32[8,128]{1,0:T(8,128)} %bitcast.17, s32[8,128]{1,0:T(8,128)} %copy-done.4, ...), custom_call_target="tpu_custom_call" | custom-call | tf_op jit(solution)/shard_map/pallas_call | solution.py:130
  34.8 3.5 %collective-permute-done.12.refs_12_ = bf16[48,2048]{1,0:T(8,128)(2,1)S(1)} collective-permute-done((bf16[48,2048]{1,0:T(8,128)(2,1)S(1)}, bf16[48,2048]{1,0:T(8,128)(2,1)S(1)}, u32[]{:S(2)}, u32[]{:S(2)}) %collective-permute-start.12) | collective-permute-done | bytes 196640 | tf_op jit(solution)/shard_map/ppermute | solution.py:124
  38.3 3.4 %copy-done = bf16[4096,1024]{1,0:T(8,128)(2,1)S(1)} copy-done((bf16[4096,1024]{1,0:T(8,128)(2,1)S(1)}, bf16[4096,1024]{1,0:T(8,128)(2,1)}, u32[]{:S(2)}) %copy-start) | copy-done | bytes 8388632
  41.7 1.0 %copy-done.1 = bf16[48,4096]{1,0:T(8,128)(2,1)S(1)} copy-done((bf16[48,4096]{1,0:T(8,128)(2,1)S(1)}, bf16[48,4096]{1,0:T(8,128)(2,1)}, u32[]{:S(2)}) %copy-start.1) | copy-done | bytes 393240
  44.1 7.8 %shard_map.110 = (f32[16,96,128]{2,1,0:T(8,128)S(1)}, f32[16,96,128]{2,1,0:T(8,128)S(1)}) custom-call(s32[2]{0:T(128)S(1)} %pad_add_fusion.where, f32[32,128]{1,0:T(8,128)S(1)} %copy-done.2, f32[8,128]{1,0:T(8,128)S(1)} %copy-done.3, bf16[4096,1024]{1,0:T(8,128)(2,1)S(1)} %copy-done, bf16[48,4096]{1,0:T(8,128)(2,1)S(1)} %copy-done.1, ...), custom_call_target="tpu_custom_call" | custom-call | tf_op jit(solution)/shard_map/pallas_call | solution.py:147
  51.9 4.0 %collective-permute-start.14 = (f32[16,96,128]{2,1,0:T(8,128)S(1)}, f32[16,96,128]{2,1,0:T(8,128)S(1)}, u32[]{:S(2)}, u32[]{:S(2)}) collective-permute-start(f32[16,96,128]{2,1,0:T(8,128)S(1)} %get-tuple-element.38), channel_id=1, source_target_pairs={{0,1},{1,0},{2,3},{3,2},{4,5},{5,4},{6,7},{7,6},{8,9},{9,8},{10,11... | collective-permute-start | bytes 2359304 | tf_op jit(solution)/shard_map/ppermute | solution.py:164
  55.9 1.9 %collective-permute-done.14 = f32[16,96,128]{2,1,0:T(8,128)S(1)} collective-permute-done((f32[16,96,128]{2,1,0:T(8,128)S(1)}, f32[16,96,128]{2,1,0:T(8,128)S(1)}, u32[]{:S(2)}, u32[]{:S(2)}) %collective-permute-start.14) | collective-permute-done | bytes 786464 | tf_op jit(solution)/shard_map/ppermute | solution.py:164
  57.9 20.5 %all_to_all.5.parts = f32[16,96,128]{2,1,0:T(8,128)} all-to-all(f32[16,96,128]{2,1,0:T(8,128)S(1)} %add.15), channel_id=1, replica_groups=mesh['z'=8,'y'=4,'x'=4,'core'=2] {'y','x'}, dimensions={0} | all-to-all | bytes 1572864 | tf_op jit(solution)/shard_map/all_to_all | solution.py:165
  78.4 1.8 %shard_map.111 = f32[12,1024]{1,0:T(8,128)} custom-call(f32[16,96,128]{2,1,0:T(8,128)} %all_to_all.5.parts, f32[8,128]{1,0:T(8,128)} %get-tuple-element.39.virt, f32[16,128]{1,0:T(8,128)} %get-tuple-element.40.occ), custom_call_target="tpu_custom_call" | custom-call | tf_op jit(solution)/shard_map/pallas_call | solution.py:166
  (28 shorter events, 4.2 us)
Async XLA Ops:
  1.1 10.1 %collective-permute-start.3 = (bf16[48,2048]{1,0:T(8,128)(2,1)S(1)}, bf16[48,2048]{1,0:T(8,128)(2,1)S(1)}, u32[]{:S(2)}, u32[]{:S(2)}) collective-permute-start(bf16[48,2048]{1,0:T(8,128)(2,1)S(1)} %get-tuple-element.41), channel_id=1, source_target_pairs={{0,224},{32,0},{64,32},{96,64},{128,96},{160,128},{192,160},{224,1... | collective-permute-start | bytes 589832 | tf_op jit(solution)/shard_map/ppermute | solution.py:122
  7.5 7.0 %collective-permute-start = (bf16[48,2048]{1,0:T(8,128)(2,1)S(1)}, bf16[48,2048]{1,0:T(8,128)(2,1)S(1)}, u32[]{:S(2)}, u32[]{:S(2)}) collective-permute-start(bf16[48,2048]{1,0:T(8,128)(2,1)S(1)} %get-tuple-element.42), channel_id=1, source_target_pairs={{0,32},{32,64},{64,96},{96,128},{128,160},{160,192},{192,224},{224... | collective-permute-start | bytes 589832 | tf_op jit(solution)/shard_map/ppermute | solution.py:119
  7.5 10.9 %collective-permute-start.1 = (bf16[48,2048]{1,0:T(8,128)(2,1)S(1)}, bf16[48,2048]{1,0:T(8,128)(2,1)S(1)}, u32[]{:S(2)}, u32[]{:S(2)}) collective-permute-start(bf16[48,2048]{1,0:T(8,128)(2,1)S(1)} %get-tuple-element.41), channel_id=1, source_target_pairs={{0,32},{32,64},{64,96},{96,128},{128,160},{160,192},{192,224},{224... | collective-permute-start | bytes 589832 | tf_op jit(solution)/shard_map/ppermute | solution.py:120
  7.5 10.9 %collective-permute-start.2 = (bf16[48,2048]{1,0:T(8,128)(2,1)S(1)}, bf16[48,2048]{1,0:T(8,128)(2,1)S(1)}, u32[]{:S(2)}, u32[]{:S(2)}) collective-permute-start(bf16[48,2048]{1,0:T(8,128)(2,1)S(1)} %get-tuple-element.42), channel_id=1, source_target_pairs={{0,224},{32,0},{64,32},{96,64},{128,96},{160,128},{192,160},{224,1... | collective-permute-start | bytes 589832 | tf_op jit(solution)/shard_map/ppermute | solution.py:121
  11.1 10.0 %collective-permute-start.7 = (bf16[48,2048]{1,0:T(8,128)(2,1)S(1)}, bf16[48,2048]{1,0:T(8,128)(2,1)S(1)}, u32[]{:S(2)}, u32[]{:S(2)}) collective-permute-start(bf16[48,2048]{1,0:T(8,128)(2,1)S(1)} %collective-permute-done.3.refs_3_), channel_id=1, source_target_pairs={{0,224},{32,0},{64,32},{96,64},{128,96},{160,128},{192,160},{224,1... | collective-permute-start | bytes 589832 | tf_op jit(solution)/shard_map/ppermute | solution.py:122
  14.5 7.8 %collective-permute-start.4 = (bf16[48,2048]{1,0:T(8,128)(2,1)S(1)}, bf16[48,2048]{1,0:T(8,128)(2,1)S(1)}, u32[]{:S(2)}, u32[]{:S(2)}) collective-permute-start(bf16[48,2048]{1,0:T(8,128)(2,1)S(1)} %collective-permute-done.refs_0_), channel_id=1, source_target_pairs={{0,32},{32,64},{64,96},{96,128},{128,160},{160,192},{192,224},{224... | collective-permute-start | bytes 589832 | tf_op jit(solution)/shard_map/ppermute | solution.py:119
  15.9 15.8 %copy-start.4 = (s32[8,128]{1,0:T(8,128)}, s32[8,128]{1,0:T(8,128)S(1)}, u32[]{:S(2)}) copy-start(s32[8,128]{1,0:T(8,128)S(1)} %scatter.9.occ) | copy-start | bytes 12292
  18.4 7.9 %collective-permute-start.5 = (bf16[48,2048]{1,0:T(8,128)(2,1)S(1)}, bf16[48,2048]{1,0:T(8,128)(2,1)S(1)}, u32[]{:S(2)}, u32[]{:S(2)}) collective-permute-start(bf16[48,2048]{1,0:T(8,128)(2,1)S(1)} %collective-permute-done.1.refs_1_), channel_id=1, source_target_pairs={{0,32},{32,64},{64,96},{96,128},{128,160},{160,192},{192,224},{224... | collective-permute-start | bytes 589832 | tf_op jit(solution)/shard_map/ppermute | solution.py:120
  18.4 7.9 %collective-permute-start.6 = (bf16[48,2048]{1,0:T(8,128)(2,1)S(1)}, bf16[48,2048]{1,0:T(8,128)(2,1)S(1)}, u32[]{:S(2)}, u32[]{:S(2)}) collective-permute-start(bf16[48,2048]{1,0:T(8,128)(2,1)S(1)} %collective-permute-done.2.refs_2_), channel_id=1, source_target_pairs={{0,224},{32,0},{64,32},{96,64},{128,96},{160,128},{192,160},{224,1... | collective-permute-start | bytes 589832 | tf_op jit(solution)/shard_map/ppermute | solution.py:121
  21.1 7.9 %collective-permute-start.11 = (bf16[48,2048]{1,0:T(8,128)(2,1)S(1)}, bf16[48,2048]{1,0:T(8,128)(2,1)S(1)}, u32[]{:S(2)}, u32[]{:S(2)}) collective-permute-start(bf16[48,2048]{1,0:T(8,128)(2,1)S(1)} %collective-permute-done.7.refs_7_), channel_id=1, source_target_pairs={{0,224},{32,0},{64,32},{96,64},{128,96},{160,128},{192,160},{224,1... | collective-permute-start | bytes 589832 | tf_op jit(solution)/shard_map/ppermute | solution.py:122
  22.3 8.0 %collective-permute-start.8 = (bf16[48,2048]{1,0:T(8,128)(2,1)S(1)}, bf16[48,2048]{1,0:T(8,128)(2,1)S(1)}, u32[]{:S(2)}, u32[]{:S(2)}) collective-permute-start(bf16[48,2048]{1,0:T(8,128)(2,1)S(1)} %collective-permute-done.4.refs_4_), channel_id=1, source_target_pairs={{0,32},{32,64},{64,96},{96,128},{128,160},{160,192},{192,224},{224... | collective-permute-start | bytes 589832 | tf_op jit(solution)/shard_map/ppermute | solution.py:119
  26.3 8.0 %collective-permute-start.9 = (bf16[48,2048]{1,0:T(8,128)(2,1)S(1)}, bf16[48,2048]{1,0:T(8,128)(2,1)S(1)}, u32[]{:S(2)}, u32[]{:S(2)}) collective-permute-start(bf16[48,2048]{1,0:T(8,128)(2,1)S(1)} %collective-permute-done.5.refs_5_), channel_id=1, source_target_pairs={{0,32},{32,64},{64,96},{96,128},{128,160},{160,192},{192,224},{224... | collective-permute-start | bytes 589832 | tf_op jit(solution)/shard_map/ppermute | solution.py:120
  26.3 8.0 %collective-permute-start.10 = (bf16[48,2048]{1,0:T(8,128)(2,1)S(1)}, bf16[48,2048]{1,0:T(8,128)(2,1)S(1)}, u32[]{:S(2)}, u32[]{:S(2)}) collective-permute-start(bf16[48,2048]{1,0:T(8,128)(2,1)S(1)} %collective-permute-done.6.refs_6_), channel_id=1, source_target_pairs={{0,224},{32,0},{64,32},{96,64},{128,96},{160,128},{192,160},{224,1... | collective-permute-start | bytes 589832 | tf_op jit(solution)/shard_map/ppermute | solution.py:121
  29.0 5.8 %collective-permute-start.13 = (bf16[48,2048]{1,0:T(8,128)(2,1)S(1)}, bf16[48,2048]{1,0:T(8,128)(2,1)S(1)}, u32[]{:S(2)}, u32[]{:S(2)}) collective-permute-start(bf16[48,2048]{1,0:T(8,128)(2,1)S(1)} %collective-permute-done.11.refs_11_), channel_id=1, source_target_pairs={{0,224},{32,0},{64,32},{96,64},{128,96},{160,128},{192,160},{224,1... | collective-permute-start | bytes 589832 | tf_op jit(solution)/shard_map/ppermute | solution.py:124
  30.3 8.0 %collective-permute-start.12 = (bf16[48,2048]{1,0:T(8,128)(2,1)S(1)}, bf16[48,2048]{1,0:T(8,128)(2,1)S(1)}, u32[]{:S(2)}, u32[]{:S(2)}) collective-permute-start(bf16[48,2048]{1,0:T(8,128)(2,1)S(1)} %collective-permute-done.8.refs_8_), channel_id=1, source_target_pairs={{0,32},{32,64},{64,96},{96,128},{128,160},{160,192},{192,224},{224... | collective-permute-start | bytes 589832 | tf_op jit(solution)/shard_map/ppermute | solution.py:124
  38.3 3.4 %copy-start = (bf16[4096,1024]{1,0:T(8,128)(2,1)S(1)}, bf16[4096,1024]{1,0:T(8,128)(2,1)}, u32[]{:S(2)}) copy-start(bf16[4096,1024]{1,0:T(8,128)(2,1)} %values.1) | copy-start | bytes 25165828
  41.7 1.0 %copy-start.1 = (bf16[48,4096]{1,0:T(8,128)(2,1)S(1)}, bf16[48,4096]{1,0:T(8,128)(2,1)}, u32[]{:S(2)}) copy-start(bf16[48,4096]{1,0:T(8,128)(2,1)} %own.1) | copy-start | bytes 1179652
  42.7 0.7 copy-start.2
  43.4 0.7 copy-start.3
  51.9 5.9 %collective-permute-start.14 = (f32[16,96,128]{2,1,0:T(8,128)S(1)}, f32[16,96,128]{2,1,0:T(8,128)S(1)}, u32[]{:S(2)}, u32[]{:S(2)}) collective-permute-start(f32[16,96,128]{2,1,0:T(8,128)S(1)} %get-tuple-element.38), channel_id=1, source_target_pairs={{0,1},{1,0},{2,3},{3,2},{4,5},{5,4},{6,7},{7,6},{8,9},{9,8},{10,11... | collective-permute-start | bytes 2359304 | tf_op jit(solution)/shard_map/ppermute | solution.py:164

commit v2 on v1

v2 whole, which is shorter than its diff:
```python
import jax
import jax.numpy as jnp
from jax import lax
from jax.experimental import pallas as pl
from jax.experimental.pallas import tpu as pltpu
from jax.sharding import Mesh, PartitionSpec as P

LANES = 128
K_BLOCK = 1024
FIRST = (0, -1, -1, 1, 1, -2, -2, 2, 2, -3, -3, 3, 3)
SHARDS = (0, -1, 1, -2, 2, -3, 3)
MIB = 1024 * 1024


def lookup(table_ref, index):
    size = table_ref.shape[0]
    high = index // LANES
    low = index % LANES
    picked = jnp.zeros(index.shape, table_ref.dtype)
    for row in range(-(-size // LANES)):
        line = table_ref[pl.ds(row * LANES, min(LANES, size - row * LANES))].reshape(1, -1)
        if line.shape[1] < LANES:
            line = jnp.pad(line, ((0, 0), (0, LANES - line.shape[1])))
        line = jnp.broadcast_to(line, index.shape)
        value = jnp.take_along_axis(line, low, axis=1, mode="promise_in_bounds")
        picked = jnp.where(high == row, value, picked)
    return picked


def tables_kernel(cd1, cd2, ab1, ab2, occ1, occ2, irrep, virt, energy, cd_out, ab_out, virt_out, occ_out):
    for tile in range(cd1.shape[0] // 8):
        part = slice(8 * tile, 8 * tile + 8)
        label = lookup(irrep, cd1[part, :]) ^ lookup(irrep, cd2[part, :])
        cd_out[part, :] = label.astype(jnp.float32)
    label = lookup(irrep, ab1[...]) ^ lookup(irrep, ab2[...])
    ab_out[...] = label.astype(jnp.float32)
    virt_out[...] = lookup(virt, ab1[...]) + lookup(virt, ab2[...])
    for row in range(occ1.shape[0]):
        both = energy[occ1[row]] + energy[occ2[row]]
        occ_out[row : row + 1, :] = jnp.full((1, LANES), both, jnp.float32)


def spread(where, total, place, shard, rows, keep, send):
    first_core = where[1] == 0
    for high in range(2):
        at = place * 4 * rows + 2 * high * rows
        even = total[at : at + rows, :]
        odd = total[at + rows : at + 2 * rows, :]
        kept = jnp.where(first_core, even, odd)
        sent = jnp.where(first_core, odd, even)
        for lane in range(kept.shape[1] // LANES):
            across = slice(lane * LANES, lane * LANES + LANES)
            down = slice(lane * rows, lane * rows + rows)
            keep[2 * shard + high, down, :] = kept[:, across]
            send[2 * shard + high, down, :] = sent[:, across]


def first_kernel(where, cd, ab, values, *refs):
    pieces = refs[:14]
    keep, send, masked, total = refs[14:]
    step = pl.program_id(0)
    steps = pl.num_programs(0)

    @pl.when(step == 0)
    def _():
        total[...] = jnp.zeros_like(total)

    base = pl.multiple_of(step * K_BLOCK, K_BLOCK)
    other = ab[...].astype(jnp.bfloat16)
    for part in range(K_BLOCK // LANES):
        line = cd[pl.ds(step * (K_BLOCK // LANES) + part, 1), :]
        label = jnp.broadcast_to(line, (LANES, LANES)).T.astype(jnp.bfloat16)
        down = slice(part * LANES, part * LANES + LANES)
        for lane in range(values.shape[1] // LANES):
            across = slice(lane * LANES, lane * LANES + LANES)
            block = values[down, across]
            same = label == jnp.broadcast_to(other[lane : lane + 1, :], (LANES, LANES))
            masked[pl.ds(base + part * LANES, LANES), across] = jnp.where(
                same, block, jnp.zeros_like(block)
            )

    def accumulate(half):
        offset = pl.multiple_of((step - half * (steps // 2)) * K_BLOCK, K_BLOCK)
        left = [pieces[2 * i + half][:, pl.ds(offset, K_BLOCK)] for i in range(7)]
        total[...] += jnp.dot(
            jnp.concatenate(left, axis=0),
            masked[pl.ds(base, K_BLOCK), :],
            preferred_element_type=jnp.float32,
        )

    @pl.when(step < steps // 2)
    def _():
        accumulate(0)

    @pl.when(step >= steps // 2)
    def _():
        accumulate(1)

    @pl.when(step == steps - 1)
    def _():
        for place, shift in enumerate(SHARDS):
            shard = lax.rem(where[0] + (shift + 8), 8)
            spread(where, total, place, shard, pieces[0].shape[0] // 4, keep, send)


def last_kernel(where, masked, left, right, keep_in, send_in, keep, send, total):
    half = left.shape[1]
    total[...] = jnp.dot(left[...], masked[:half, :], preferred_element_type=jnp.float32)
    total[...] += jnp.dot(right[...], masked[half:, :], preferred_element_type=jnp.float32)
    keep[...] = keep_in[...]
    send[...] = send_in[...]
    spread(where, total, 0, lax.rem(where[0] + 4, 8), left.shape[0] // 4, keep, send)


def pack_kernel(keep, got, out):
    rows = keep.shape[1]
    for block in range(keep.shape[0]):
        both = keep[block] + got[block]
        top = jnp.maximum(jnp.max(jnp.abs(both), axis=0, keepdims=True), 1e-30)
        power = jnp.floor(14.99 - jnp.log2(top))
        scaled = jnp.clip(jnp.round(both * jnp.exp2(power)), -32767.0, 32767.0)
        out[block, :rows, :] = scaled.astype(jnp.int32).astype(jnp.int16)
        power = jnp.broadcast_to(power, (out.shape[1] - rows, LANES))
        out[block, rows:, :] = power.astype(jnp.int32).astype(jnp.int16)


def finish_kernel(parts, virt, occ, out):
    rows = out.shape[0]
    size = rows * out.shape[1] // LANES
    summed = jnp.zeros((size, LANES), jnp.float32)
    for block in range(parts.shape[0]):
        power = parts[block, size:, :].astype(jnp.int32).astype(jnp.float32)
        value = parts[block, :size, :].astype(jnp.int32).astype(jnp.float32)
        summed += value * jnp.exp2(-power[0:1, :])
    for lane in range(out.shape[1] // LANES):
        ladder = summed[lane * rows : lane * rows + rows, :]
        denom = virt[lane : lane + 1, :] - occ[:rows, :]
        out[:, lane * LANES : lane * LANES + LANES] = ladder / denom


def on_device(amps, integrals, cd1, cd2, ab1, ab2, occ1, occ2, irrep, occ_energy, virt_energy):
    depth = amps.shape[1]
    width = integrals.shape[1]
    rows = occ1.shape[0]
    forward = [(i, (i + 1) % 8) for i in range(8)]
    backward = [(i, (i - 1) % 8) for i in range(8)]
    up = [amps[:, : depth // 2], amps[:, depth // 2 :]]
    down = list(up)
    pieces = list(up)
    for _ in range(3):
        up[0] = lax.ppermute(up[0], "z", forward)
        up[1] = lax.ppermute(up[1], "z", forward)
        down[0] = lax.ppermute(down[0], "z", backward)
        down[1] = lax.ppermute(down[1], "z", backward)
        pieces += up + down
    last = [lax.ppermute(up[0], "z", forward), lax.ppermute(down[1], "z", backward)]

    vmem = pl.BlockSpec(memory_space=pltpu.VMEM)
    smem = pl.BlockSpec(memory_space=pltpu.SMEM)
    square = lambda x: x.reshape(x.shape[0] // LANES, LANES)
    cd, ab, virt, occ = pl.pallas_call(
        tables_kernel,
        out_shape=(
            pltpu.VMEM((depth // LANES, LANES), jnp.float32),
            pltpu.VMEM((width // LANES, LANES), jnp.float32),
            pltpu.VMEM((width // LANES, LANES), jnp.float32),
            pltpu.VMEM((16, LANES), jnp.float32),
        ),
        in_specs=[vmem] * 4 + [smem] * 2 + [vmem] * 2 + [smem],
        out_specs=(vmem,) * 4,
        compiler_params=pltpu.CompilerParams(vmem_limit_bytes=4 * MIB),
    )(
        *[pltpu.with_memory_space_constraint(x, pltpu.HBM) for x in (
            square(cd1), square(cd2), square(ab1), square(ab2), occ1, occ2,
            irrep, virt_energy, occ_energy,
        )]
    )

    where = jnp.stack([lax.axis_index("z"), lax.axis_index("core")]).astype(jnp.int32)
    block = pltpu.VMEM((16, rows * width // LANES, LANES), jnp.float32)
    keep, send, masked = pl.pallas_call(
        first_kernel,
        out_shape=(block, block, pltpu.VMEM((depth, width), jnp.bfloat16)),
        grid_spec=pltpu.PrefetchScalarGridSpec(
            num_scalar_prefetch=1,
            grid=(depth // K_BLOCK,),
            in_specs=[vmem, vmem, pl.BlockSpec((K_BLOCK, width), lambda k, where: (k, 0))]
            + [vmem] * 14,
            out_specs=(vmem, vmem, vmem),
            scratch_shapes=[pltpu.VMEM((7 * amps.shape[0], width), jnp.float32)],
        ),
        compiler_params=pltpu.CompilerParams(vmem_limit_bytes=20 * MIB),
    )(where, cd, ab, pltpu.with_memory_space_constraint(integrals, pltpu.HBM), *pieces)
    keep, send = pl.pallas_call(
        last_kernel,
        out_shape=(block, block),
        grid_spec=pltpu.PrefetchScalarGridSpec(
            num_scalar_prefetch=1,
            grid=(),
            in_specs=[vmem] * 5,
            out_specs=(vmem, vmem),
            scratch_shapes=[pltpu.VMEM((amps.shape[0], width), jnp.float32)],
        ),
        input_output_aliases={4: 0, 5: 1},
        compiler_params=pltpu.CompilerParams(vmem_limit_bytes=20 * MIB),
    )(where, masked, *last, keep, send)

    got = lax.ppermute(send, "core", [(0, 1), (1, 0)])
    packed = pl.pallas_call(
        pack_kernel,
        out_shape=pltpu.VMEM((16, block.shape[1] + 16, LANES), jnp.int16),
        in_specs=[vmem] * 2,
        out_specs=vmem,
        compiler_params=pltpu.CompilerParams(vmem_limit_bytes=4 * MIB),
    )(keep, got)
    parts = lax.all_to_all(packed, ("y", "x"), 0, 0, tiled=True)
    return pl.pallas_call(
        finish_kernel,
        out_shape=jax.ShapeDtypeStruct((rows, width), jnp.float32),
        in_specs=[vmem] * 3,
        out_specs=vmem,
        compiler_params=pltpu.CompilerParams(vmem_limit_bytes=4 * MIB),
    )(parts, virt, occ)


def solution(mesh):
    fine = Mesh(mesh.devices.reshape(8, 4, 4, 2), ("z", "y", "x", "core"))
    col = ("y", "x", "core")
    in_specs = (
        P("z", col), P(col, "z"), P(col), P(col), P("z"), P("z"), P(col), P(col), P(), P(), P(),
    )
    return jax.shard_map(
        on_device, mesh=fine, in_specs=in_specs, out_specs=P(col, "z"), check_vma=False
    )
```

time: 80.7 us -> 68.8 us (0.85)
  local copies, waits for them, and re-layouts: 12.1 us -> 1.05 us
  starting transfers between devices: 23.9 us -> 28.1 us
  blocking collectives: 20.5 us -> 16.5 us
  waiting for transfers between devices: 11.9 us -> 9.47 us
  Pallas kernels: 11.5 us -> 13.4 us
    unnamed x10 -> x0, local copies, waits for them, and re-layouts: 5.77 us -> none
    ppermute x3, waiting for transfers between devices: 0.91 us -> 5.6 us  [on_device(): up[0] = lax.ppermute(up[0], 'z', forward)]
    all_to_all x1, blocking collectives: 20.5 us -> 16.5 us  [on_device(): parts = lax.all_to_all(packed, ('y', 'x'), 0, 0, tiled=True)]
    reshape x3 -> x0, local copies, waits for them, and re-layouts: 3.89 us -> none  [as_table(): jnp.pad(values, (0, size - values.shape[0])).reshape(size // LANES, LANES)]
    ppermute x1, waiting for transfers between devices: 3.5 us -> 0.01 us  [on_device(): lax.ppermute(up[0], 'z', forward)]
    ppermute x3, waiting for transfers between devices: 4.25 us -> 1.17 us  [on_device(): up[1] = lax.ppermute(up[1], 'z', forward)]
    pallas_call x2 -> x4, Pallas kernels: 9.72 us -> 12.6 us  [the longest x1 8.87 us: on_device(): pl.pallas_call(first_kernel, out_shape=(block, block, pltpu.VMEM((depth,...]
    ppermute x1, starting transfers between devices: 0.4 us -> 2.87 us  [on_device(): lax.ppermute(down[1], 'z', backward)]
  transfers between devices with their start and end apart: 15 -> 15, of which waited for: 8 -> 7; matrix products, arithmetic and copies ran while one was open for 7% -> 0% of each run, Pallas kernels for 2% -> 15%
where the time goes in v2:
time: 68.8 us; the launch traced here: 68.6 us
  starting transfers between devices  28.1 us (41%)
  blocking collectives  16.5 us (24%)
  Pallas kernels  13.4 us (19%)
  waiting for transfers between devices  9.47 us (14%)
  local copies, waits for them, and re-layouts  1.05 us (2%)
    all_to_all x1, blocking collectives, on_device(): parts = lax.all_to_all(packed, ('y', 'x'), 0, 0, tiled=True)  16.5 us
    ppermute x3, starting transfers between devices, on_device(): down[1] = lax.ppermute(down[1], 'z', backward)  9.38 us
    pallas_call x1, Pallas kernels, on_device(): pl.pallas_call(first_kernel, out_shape=(block, block, pltpu.VMEM((depth,...  8.87 us
    ppermute x3, starting transfers between devices, on_device(): down[0] = lax.ppermute(down[0], 'z', backward)  8.2 us
    ppermute x3, waiting for transfers between devices, on_device(): up[0] = lax.ppermute(up[0], 'z', forward)  5.6 us
    ppermute x1, starting transfers between devices, on_device(): got = lax.ppermute(send, 'core', [(0, 1), (1, 0)])  4.99 us
    ppermute x1, starting transfers between devices, on_device(): lax.ppermute(down[1], 'z', backward)  2.87 us
    ppermute x3, starting transfers between devices, on_device(): up[0] = lax.ppermute(up[0], 'z', forward)  2.55 us
  transfers between devices with their start and end apart: 15, of which 7 were waited for; matrix products, arithmetic and copies ran while one was open for 0% of the time, Pallas kernels for 15%

profile of v2, /device:TPU:1, one launch (start us, length us, event | category | flops | bytes accessed | tf_op | source)
XLA Modules:
  0.0 68.6 jit_solution(13176661826677007822)
XLA Ops:
  0.0 1.0 %fusion = (bf16[48,2048]{1,0:T(8,128)(2,1)S(1)}, bf16[48,2048]{1,0:T(8,128)(2,1)S(1)}) fusion(bf16[48,4096]{1,0:T(8,128)(2,1)} %param.11), kind=kLoop, calls=%fused_computation.1 | loop fusion | bytes 786432 | tf_op jit(solution)/shard_map/slice | solution.py:147
  1.1 2.5 %collective-permute-start = (bf16[48,2048]{1,0:T(8,128)(2,1)S(1)}, bf16[48,2048]{1,0:T(8,128)(2,1)S(1)}, u32[]{:S(2)}, u32[]{:S(2)}) collective-permute-start(bf16[48,2048]{1,0:T(8,128)(2,1)S(1)} %get-tuple-element.24.refs_0_), channel_id=1, source_target_pairs={{0,32},{32,64},{64,96},{96,128},{128,160},{160,192},{192,224},{224... | collective-permute-start | bytes 589832 | tf_op jit(solution)/shard_map/ppermute | solution.py:151
  3.6 4.0 %collective-permute-start.3 = (bf16[48,2048]{1,0:T(8,128)(2,1)S(1)}, bf16[48,2048]{1,0:T(8,128)(2,1)S(1)}, u32[]{:S(2)}, u32[]{:S(2)}) collective-permute-start(bf16[48,2048]{1,0:T(8,128)(2,1)S(1)} %get-tuple-element.23.refs_1_), channel_id=1, source_target_pairs={{0,224},{32,0},{64,32},{96,64},{128,96},{160,128},{192,160},{224,1... | collective-permute-start | bytes 589832 | tf_op jit(solution)/shard_map/ppermute | solution.py:154
  7.6 1.4 %collective-permute-start.2 = (bf16[48,2048]{1,0:T(8,128)(2,1)S(1)}, bf16[48,2048]{1,0:T(8,128)(2,1)S(1)}, u32[]{:S(2)}, u32[]{:S(2)}) collective-permute-start(bf16[48,2048]{1,0:T(8,128)(2,1)S(1)} %get-tuple-element.24.refs_0_), channel_id=1, source_target_pairs={{0,224},{32,0},{64,32},{96,64},{128,96},{160,128},{192,160},{224,1... | collective-permute-start | bytes 589832 | tf_op jit(solution)/shard_map/ppermute | solution.py:153
  9.0 0.1 collective-permute-start.1
  9.1 3.1 %collective-permute-done.refs_2_ = bf16[48,2048]{1,0:T(8,128)(2,1)S(1)} collective-permute-done((bf16[48,2048]{1,0:T(8,128)(2,1)S(1)}, bf16[48,2048]{1,0:T(8,128)(2,1)S(1)}, u32[]{:S(2)}, u32[]{:S(2)}) %collective-permute-start) | collective-permute-done | bytes 196640 | tf_op jit(solution)/shard_map/ppermute | solution.py:151
  12.2 2.7 %collective-permute-start.7 = (bf16[48,2048]{1,0:T(8,128)(2,1)S(1)}, bf16[48,2048]{1,0:T(8,128)(2,1)S(1)}, u32[]{:S(2)}, u32[]{:S(2)}) collective-permute-start(bf16[48,2048]{1,0:T(8,128)(2,1)S(1)} %collective-permute-done.3.refs_5_), channel_id=1, source_target_pairs={{0,224},{32,0},{64,32},{96,64},{128,96},{160,128},{192,160},{224,1... | collective-permute-start | bytes 589832 | tf_op jit(solution)/shard_map/ppermute | solution.py:154
  14.8 0.6 collective-permute-done.2.refs_4_
  15.4 3.4 %collective-permute-start.6 = (bf16[48,2048]{1,0:T(8,128)(2,1)S(1)}, bf16[48,2048]{1,0:T(8,128)(2,1)S(1)}, u32[]{:S(2)}, u32[]{:S(2)}) collective-permute-start(bf16[48,2048]{1,0:T(8,128)(2,1)S(1)} %collective-permute-done.2.refs_4_), channel_id=1, source_target_pairs={{0,224},{32,0},{64,32},{96,64},{128,96},{160,128},{192,160},{224,1... | collective-permute-start | bytes 589832 | tf_op jit(solution)/shard_map/ppermute | solution.py:153
  18.8 1.5 %collective-permute-done.4.refs_6_ = bf16[48,2048]{1,0:T(8,128)(2,1)S(1)} collective-permute-done((bf16[48,2048]{1,0:T(8,128)(2,1)S(1)}, bf16[48,2048]{1,0:T(8,128)(2,1)S(1)}, u32[]{:S(2)}, u32[]{:S(2)}) %collective-permute-start.4) | collective-permute-done | bytes 196640 | tf_op jit(solution)/shard_map/ppermute | solution.py:151
  20.3 2.7 %collective-permute-start.11 = (bf16[48,2048]{1,0:T(8,128)(2,1)S(1)}, bf16[48,2048]{1,0:T(8,128)(2,1)S(1)}, u32[]{:S(2)}, u32[]{:S(2)}) collective-permute-start(bf16[48,2048]{1,0:T(8,128)(2,1)S(1)} %collective-permute-done.7.refs_9_), channel_id=1, source_target_pairs={{0,224},{32,0},{64,32},{96,64},{128,96},{160,128},{192,160},{224,1... | collective-permute-start | bytes 589832 | tf_op jit(solution)/shard_map/ppermute | solution.py:154
  23.0 0.2 collective-permute-done.6.refs_8_
  23.2 3.4 %collective-permute-start.10 = (bf16[48,2048]{1,0:T(8,128)(2,1)S(1)}, bf16[48,2048]{1,0:T(8,128)(2,1)S(1)}, u32[]{:S(2)}, u32[]{:S(2)}) collective-permute-start(bf16[48,2048]{1,0:T(8,128)(2,1)S(1)} %collective-permute-done.6.refs_8_), channel_id=1, source_target_pairs={{0,224},{32,0},{64,32},{96,64},{128,96},{160,128},{192,160},{224,1... | collective-permute-start | bytes 589832 | tf_op jit(solution)/shard_map/ppermute | solution.py:153
  26.6 1.0 %collective-permute-done.8.refs_10_ = bf16[48,2048]{1,0:T(8,128)(2,1)S(1)} collective-permute-done((bf16[48,2048]{1,0:T(8,128)(2,1)S(1)}, bf16[48,2048]{1,0:T(8,128)(2,1)S(1)}, u32[]{:S(2)}, u32[]{:S(2)}) %collective-permute-start.8) | collective-permute-done | bytes 196640 | tf_op jit(solution)/shard_map/ppermute | solution.py:151
  27.7 2.9 %collective-permute-start.13 = (bf16[48,2048]{1,0:T(8,128)(2,1)S(1)}, bf16[48,2048]{1,0:T(8,128)(2,1)S(1)}, u32[]{:S(2)}, u32[]{:S(2)}) collective-permute-start(bf16[48,2048]{1,0:T(8,128)(2,1)S(1)} %collective-permute-done.11.refs_13_), channel_id=1, source_target_pairs={{0,224},{32,0},{64,32},{96,64},{128,96},{160,128},{192,160},{224,1... | collective-permute-start | bytes 589832 | tf_op jit(solution)/shard_map/ppermute | solution.py:156
  30.5 1.2 %shard_map.109 = (f32[32,128]{1,0:T(8,128)S(1)}, f32[8,128]{1,0:T(8,128)S(1)}, f32[8,128]{1,0:T(8,128)S(1)}, f32[16,128]{1,0:T(8,128)S(1)}) custom-call(s32[32,128]{1,0:T(8,128)} %bitcast.6, s32[32,128]{1,0:T(8,128)} %bitcast.7, s32[8,128]{1,0:T(8,128)} %bitcast.8, s32[8,128]{1,0:T(8,128)} %bitcast.9, s32[12]{0:T(128)} %occ1.1, s32[12]{0:T(128)} %occ2.1, ...), custom_call_target="tpu_custom_call" | custom-call | tf_op jit(solution)/shard_map/pallas_call | solution.py:161
  31.8 1.2 %collective-permute-done.9.refs_11_ = bf16[48,2048]{1,0:T(8,128)(2,1)S(1)} collective-permute-done((bf16[48,2048]{1,0:T(8,128)(2,1)S(1)}, bf16[48,2048]{1,0:T(8,128)(2,1)S(1)}, u32[]{:S(2)}, u32[]{:S(2)}) %collective-permute-start.9) | collective-permute-done | bytes 196640 | tf_op jit(solution)/shard_map/ppermute | solution.py:152
  33.0 8.9 %shard_map.110 = (f32[16,96,128]{2,1,0:T(8,128)S(1)}, f32[16,96,128]{2,1,0:T(8,128)S(1)}, bf16[4096,1024]{1,0:T(8,128)(2,1)S(1)}) custom-call(s32[2]{0:T(128)S(1)} %pad_add_fusion.where, f32[32,128]{1,0:T(8,128)S(1)} %get-tuple-element.14.cd, f32[8,128]{1,0:T(8,128)S(1)} %get-tuple-element.15.ab, bf16[4096,1024]{1,0:T(8,128)(2,1)} %values.1, ...), custom_call_target="tpu_custom_call" | custom-call | tf_op jit(solution)/shard_map/pallas_call | solution.py:181
  41.9 2.4 %shard_map.111 = (f32[16,96,128]{2,1,0:T(8,128)S(1)}, f32[16,96,128]{2,1,0:T(8,128)S(1)}) custom-call(s32[2]{0:T(128)S(1)} %pad_add_fusion.where, bf16[4096,1024]{1,0:T(8,128)(2,1)S(1)} %get-tuple-element.16.masked, bf16[48,2048]{1,0:T(8,128)(2,1)S(1)} %collective-permute-done.12.left, ...), custom_call_target="tpu_custom_call", output_to_operand_aliasing={{0}: (4, {}), {1}: (5, {})} | custom-call | tf_op jit(solution)/shard_map/pallas_call | solution.py:194
  44.2 5.0 %collective-permute-start.14 = (f32[16,96,128]{2,1,0:T(8,128)S(1)}, f32[16,96,128]{2,1,0:T(8,128)S(1)}, u32[]{:S(2)}, u32[]{:S(2)}) collective-permute-start(f32[16,96,128]{2,1,0:T(8,128)S(1)} %get-tuple-element.20), channel_id=1, source_target_pairs={{0,1},{1,0},{2,3},{3,2},{4,5},{5,4},{6,7},{7,6},{8,9},{9,8},{10,11... | collective-permute-start | bytes 2359304 | tf_op jit(solution)/shard_map/ppermute | solution.py:208
  49.2 1.9 %collective-permute-done.14.got = f32[16,96,128]{2,1,0:T(8,128)S(1)} collective-permute-done((f32[16,96,128]{2,1,0:T(8,128)S(1)}, f32[16,96,128]{2,1,0:T(8,128)S(1)}, u32[]{:S(2)}, u32[]{:S(2)}) %collective-permute-start.14) | collective-permute-done | bytes 786464 | tf_op jit(solution)/shard_map/ppermute | solution.py:208
  51.1 0.2 shard_map.112
  51.4 16.5 %all_to_all.5.parts = s16[16,112,128]{2,1,0:T(8,128)(2,1)S(1)} all-to-all(s16[16,112,128]{2,1,0:T(8,128)(2,1)S(1)} %shard_map.112), channel_id=1, replica_groups=mesh['z'=8,'y'=4,'x'=4,'core'=2] {'y','x'}, dimensions={0} | all-to-all | bytes 917504 | tf_op jit(solution)/shard_map/all_to_all | solution.py:216
  67.8 0.8 %shard_map.113 = f32[12,1024]{1,0:T(8,128)} custom-call(s16[16,112,128]{2,1,0:T(8,128)(2,1)S(1)} %all_to_all.5.parts, f32[8,128]{1,0:T(8,128)S(1)} %get-tuple-element.21.virt, f32[16,128]{1,0:T(8,128)S(1)} %get-tuple-element.22.occ), custom_call_target="tpu_custom_call" | custom-call | tf_op jit(solution)/shard_map/pallas_call | solution.py:217
  (14 shorter events, 0.1 us)
Async XLA Ops:
  1.1 11.1 %collective-permute-start = (bf16[48,2048]{1,0:T(8,128)(2,1)S(1)}, bf16[48,2048]{1,0:T(8,128)(2,1)S(1)}, u32[]{:S(2)}, u32[]{:S(2)}) collective-permute-start(bf16[48,2048]{1,0:T(8,128)(2,1)S(1)} %get-tuple-element.24.refs_0_), channel_id=1, source_target_pairs={{0,32},{32,64},{64,96},{96,128},{128,160},{160,192},{192,224},{224... | collective-permute-start | bytes 589832 | tf_op jit(solution)/shard_map/ppermute | solution.py:151
  3.6 8.6 %collective-permute-start.3 = (bf16[48,2048]{1,0:T(8,128)(2,1)S(1)}, bf16[48,2048]{1,0:T(8,128)(2,1)S(1)}, u32[]{:S(2)}, u32[]{:S(2)}) collective-permute-start(bf16[48,2048]{1,0:T(8,128)(2,1)S(1)} %get-tuple-element.23.refs_1_), channel_id=1, source_target_pairs={{0,224},{32,0},{64,32},{96,64},{128,96},{160,128},{192,160},{224,1... | collective-permute-start | bytes 589832 | tf_op jit(solution)/shard_map/ppermute | solution.py:154
  7.6 7.8 %collective-permute-start.2 = (bf16[48,2048]{1,0:T(8,128)(2,1)S(1)}, bf16[48,2048]{1,0:T(8,128)(2,1)S(1)}, u32[]{:S(2)}, u32[]{:S(2)}) collective-permute-start(bf16[48,2048]{1,0:T(8,128)(2,1)S(1)} %get-tuple-element.24.refs_0_), channel_id=1, source_target_pairs={{0,224},{32,0},{64,32},{96,64},{128,96},{160,128},{192,160},{224,1... | collective-permute-start | bytes 589832 | tf_op jit(solution)/shard_map/ppermute | solution.py:153
  9.0 9.8 %collective-permute-start.1 = (bf16[48,2048]{1,0:T(8,128)(2,1)S(1)}, bf16[48,2048]{1,0:T(8,128)(2,1)S(1)}, u32[]{:S(2)}, u32[]{:S(2)}) collective-permute-start(bf16[48,2048]{1,0:T(8,128)(2,1)S(1)} %get-tuple-element.23.refs_1_), channel_id=1, source_target_pairs={{0,32},{32,64},{64,96},{96,128},{128,160},{160,192},{192,224},{224... | collective-permute-start | bytes 589832 | tf_op jit(solution)/shard_map/ppermute | solution.py:152
  12.2 8.2 %collective-permute-start.4 = (bf16[48,2048]{1,0:T(8,128)(2,1)S(1)}, bf16[48,2048]{1,0:T(8,128)(2,1)S(1)}, u32[]{:S(2)}, u32[]{:S(2)}) collective-permute-start(bf16[48,2048]{1,0:T(8,128)(2,1)S(1)} %collective-permute-done.refs_2_), channel_id=1, source_target_pairs={{0,32},{32,64},{64,96},{96,128},{128,160},{160,192},{192,224},{224... | collective-permute-start | bytes 589832 | tf_op jit(solution)/shard_map/ppermute | solution.py:151
  12.2 8.2 %collective-permute-start.7 = (bf16[48,2048]{1,0:T(8,128)(2,1)S(1)}, bf16[48,2048]{1,0:T(8,128)(2,1)S(1)}, u32[]{:S(2)}, u32[]{:S(2)}) collective-permute-start(bf16[48,2048]{1,0:T(8,128)(2,1)S(1)} %collective-permute-done.3.refs_5_), channel_id=1, source_target_pairs={{0,224},{32,0},{64,32},{96,64},{128,96},{160,128},{192,160},{224,1... | collective-permute-start | bytes 589832 | tf_op jit(solution)/shard_map/ppermute | solution.py:154
  15.4 7.8 %collective-permute-start.6 = (bf16[48,2048]{1,0:T(8,128)(2,1)S(1)}, bf16[48,2048]{1,0:T(8,128)(2,1)S(1)}, u32[]{:S(2)}, u32[]{:S(2)}) collective-permute-start(bf16[48,2048]{1,0:T(8,128)(2,1)S(1)} %collective-permute-done.2.refs_4_), channel_id=1, source_target_pairs={{0,224},{32,0},{64,32},{96,64},{128,96},{160,128},{192,160},{224,1... | collective-permute-start | bytes 589832 | tf_op jit(solution)/shard_map/ppermute | solution.py:153
  18.8 7.8 %collective-permute-start.5 = (bf16[48,2048]{1,0:T(8,128)(2,1)S(1)}, bf16[48,2048]{1,0:T(8,128)(2,1)S(1)}, u32[]{:S(2)}, u32[]{:S(2)}) collective-permute-start(bf16[48,2048]{1,0:T(8,128)(2,1)S(1)} %collective-permute-done.1.refs_3_), channel_id=1, source_target_pairs={{0,32},{32,64},{64,96},{96,128},{128,160},{160,192},{192,224},{224... | collective-permute-start | bytes 589832 | tf_op jit(solution)/shard_map/ppermute | solution.py:152
  20.3 7.4 %collective-permute-start.8 = (bf16[48,2048]{1,0:T(8,128)(2,1)S(1)}, bf16[48,2048]{1,0:T(8,128)(2,1)S(1)}, u32[]{:S(2)}, u32[]{:S(2)}) collective-permute-start(bf16[48,2048]{1,0:T(8,128)(2,1)S(1)} %collective-permute-done.4.refs_6_), channel_id=1, source_target_pairs={{0,32},{32,64},{64,96},{96,128},{128,160},{160,192},{192,224},{224... | collective-permute-start | bytes 589832 | tf_op jit(solution)/shard_map/ppermute | solution.py:151
  20.3 7.4 %collective-permute-start.11 = (bf16[48,2048]{1,0:T(8,128)(2,1)S(1)}, bf16[48,2048]{1,0:T(8,128)(2,1)S(1)}, u32[]{:S(2)}, u32[]{:S(2)}) collective-permute-start(bf16[48,2048]{1,0:T(8,128)(2,1)S(1)} %collective-permute-done.7.refs_9_), channel_id=1, source_target_pairs={{0,224},{32,0},{64,32},{96,64},{128,96},{160,128},{192,160},{224,1... | collective-permute-start | bytes 589832 | tf_op jit(solution)/shard_map/ppermute | solution.py:154
  23.2 8.6 %collective-permute-start.10 = (bf16[48,2048]{1,0:T(8,128)(2,1)S(1)}, bf16[48,2048]{1,0:T(8,128)(2,1)S(1)}, u32[]{:S(2)}, u32[]{:S(2)}) collective-permute-start(bf16[48,2048]{1,0:T(8,128)(2,1)S(1)} %collective-permute-done.6.refs_8_), channel_id=1, source_target_pairs={{0,224},{32,0},{64,32},{96,64},{128,96},{160,128},{192,160},{224,1... | collective-permute-start | bytes 589832 | tf_op jit(solution)/shard_map/ppermute | solution.py:153
  26.6 6.4 %collective-permute-start.9 = (bf16[48,2048]{1,0:T(8,128)(2,1)S(1)}, bf16[48,2048]{1,0:T(8,128)(2,1)S(1)}, u32[]{:S(2)}, u32[]{:S(2)}) collective-permute-start(bf16[48,2048]{1,0:T(8,128)(2,1)S(1)} %collective-permute-done.5.refs_7_), channel_id=1, source_target_pairs={{0,32},{32,64},{64,96},{96,128},{128,160},{160,192},{192,224},{224... | collective-permute-start | bytes 589832 | tf_op jit(solution)/shard_map/ppermute | solution.py:152
  27.7 14.2 %collective-permute-start.12 = (bf16[48,2048]{1,0:T(8,128)(2,1)S(1)}, bf16[48,2048]{1,0:T(8,128)(2,1)S(1)}, u32[]{:S(2)}, u32[]{:S(2)}) collective-permute-start(bf16[48,2048]{1,0:T(8,128)(2,1)S(1)} %collective-permute-done.8.refs_10_), channel_id=1, source_target_pairs={{0,32},{32,64},{64,96},{96,128},{128,160},{160,192},{192,224},{224... | collective-permute-start | bytes 589832 | tf_op jit(solution)/shard_map/ppermute | solution.py:156
  27.7 14.2 %collective-permute-start.13 = (bf16[48,2048]{1,0:T(8,128)(2,1)S(1)}, bf16[48,2048]{1,0:T(8,128)(2,1)S(1)}, u32[]{:S(2)}, u32[]{:S(2)}) collective-permute-start(bf16[48,2048]{1,0:T(8,128)(2,1)S(1)} %collective-permute-done.11.refs_13_), channel_id=1, source_target_pairs={{0,224},{32,0},{64,32},{96,64},{128,96},{160,128},{192,160},{224,1... | collective-permute-start | bytes 589832 | tf_op jit(solution)/shard_map/ppermute | solution.py:156
  44.2 6.9 %collective-permute-start.14 = (f32[16,96,128]{2,1,0:T(8,128)S(1)}, f32[16,96,128]{2,1,0:T(8,128)S(1)}, u32[]{:S(2)}, u32[]{:S(2)}) collective-permute-start(f32[16,96,128]{2,1,0:T(8,128)S(1)} %get-tuple-element.20), channel_id=1, source_target_pairs={{0,1},{1,0},{2,3},{3,2},{4,5},{5,4},{6,7},{7,6},{8,9},{9,8},{10,11... | collective-permute-start | bytes 2359304 | tf_op jit(solution)/shard_map/ppermute | solution.py:208

commit v3 on v2

--- a/solution.py
+++ b/solution.py
@@ -7,8 +7,6 @@
 
 LANES = 128
 K_BLOCK = 1024
-FIRST = (0, -1, -1, 1, 1, -2, -2, 2, 2, -3, -3, 3, 3)
-SHARDS = (0, -1, 1, -2, 2, -3, 3)
 MIB = 1024 * 1024
 
 
@@ -40,8 +38,9 @@
         occ_out[row : row + 1, :] = jnp.full((1, LANES), both, jnp.float32)
 
 
-def spread(where, total, place, shard, rows, keep, send):
-    first_core = where[1] == 0
+def spread(where, total, place, offset, rows, keep, send):
+    first_core = where[2] == 0
+    shard = lax.rem(where[0] + where[1] * offset + 8, 8)
     for high in range(2):
         at = place * 4 * rows + 2 * high * rows
         even = total[at : at + rows, :]
@@ -55,16 +54,9 @@
             send[2 * shard + high, down, :] = sent[:, across]
 
 
-def first_kernel(where, cd, ab, values, *refs):
-    pieces = refs[:14]
-    keep, send, masked, total = refs[14:]
+def mask_kernel(cd, ab, values, masked, ready):
     step = pl.program_id(0)
-    steps = pl.num_programs(0)
-
-    @pl.when(step == 0)
-    def _():
-        total[...] = jnp.zeros_like(total)
-
+    ready[...] = jnp.zeros_like(ready)
     base = pl.multiple_of(step * K_BLOCK, K_BLOCK)
     other = ab[...].astype(jnp.bfloat16)
     for part in range(K_BLOCK // LANES):
@@ -79,37 +71,35 @@
                 same, block, jnp.zeros_like(block)
             )
 
-    def accumulate(half):
-        offset = pl.multiple_of((step - half * (steps // 2)) * K_BLOCK, K_BLOCK)
-        left = [pieces[2 * i + half][:, pl.ds(offset, K_BLOCK)] for i in range(7)]
-        total[...] += jnp.dot(
-            jnp.concatenate(left, axis=0),
-            masked[pl.ds(base, K_BLOCK), :],
-            preferred_element_type=jnp.float32,
-        )
-
-    @pl.when(step < steps // 2)
-    def _():
-        accumulate(0)
-
-    @pl.when(step >= steps // 2)
-    def _():
-        accumulate(1)
-
-    @pl.when(step == steps - 1)
-    def _():
-        for place, shift in enumerate(SHARDS):
-            shard = lax.rem(where[0] + (shift + 8), 8)
-            spread(where, total, place, shard, pieces[0].shape[0] // 4, keep, send)
-
-
-def last_kernel(where, masked, left, right, keep_in, send_in, keep, send, total):
-    half = left.shape[1]
-    total[...] = jnp.dot(left[...], masked[:half, :], preferred_element_type=jnp.float32)
-    total[...] += jnp.dot(right[...], masked[half:, :], preferred_element_type=jnp.float32)
+
+def dot_into(total, masked, left, right):
+    half = masked.shape[0] // 2
+    total[...] = jnp.dot(
+        jnp.concatenate(left, axis=0), masked[:half, :], preferred_element_type=jnp.float32
+    )
+    total[...] += jnp.dot(
+        jnp.concatenate(right, axis=0), masked[half:, :], preferred_element_type=jnp.float32
+    )
+
+
+def first_kernel(where, ready, masked, a1, b1, a2, b2, a3, b3, keep, send, total):
+    size = a2.shape[0] // 2
+    left = [a1[...], a2[...], a3[:size, :]]
+    right = [b1[:size, :], b2[:size, :], b1[size:, :], b3[:size, :], b2[size:, :]]
+    dot_into(total, masked, left, right)
+    for place, offset in enumerate((0, 1, -1, -2, 2)):
+        spread(where, total, place, offset, size // 4, keep, send)
+
+
+def last_kernel(where, masked, a3, b3, a4, b4, keep_in, send_in, keep, send, total):
+    size = a4.shape[0] // 2
+    left = [a3[size:, :], a4[...]]
+    right = [b4[:size, :], b3[size:, :], b4[size:, :]]
+    dot_into(total, masked, left, right)
     keep[...] = keep_in[...]
     send[...] = send_in[...]
-    spread(where, total, 0, lax.rem(where[0] + 4, 8), left.shape[0] // 4, keep, send)
+    for place, offset in enumerate((3, -3, 4)):
+        spread(where, total, place, offset, size // 4, keep, send)
 
 
 def pack_kernel(keep, got, out):
@@ -142,19 +132,6 @@
     depth = amps.shape[1]
     width = integrals.shape[1]
     rows = occ1.shape[0]
-    forward = [(i, (i + 1) % 8) for i in range(8)]
-    backward = [(i, (i - 1) % 8) for i in range(8)]
-    up = [amps[:, : depth // 2], amps[:, depth // 2 :]]
-    down = list(up)
-    pieces = list(up)
-    for _ in range(3):
-        up[0] = lax.ppermute(up[0], "z", forward)
-        up[1] = lax.ppermute(up[1], "z", forward)
-        down[0] = lax.ppermute(down[0], "z", backward)
-        down[1] = lax.ppermute(down[1], "z", backward)
-        pieces += up + down
-    last = [lax.ppermute(up[0], "z", forward), lax.ppermute(down[1], "z", backward)]
-
     vmem = pl.BlockSpec(memory_space=pltpu.VMEM)
     smem = pl.BlockSpec(memory_space=pltpu.SMEM)
     square = lambda x: x.reshape(x.shape[0] // LANES, LANES)
@@ -176,34 +153,53 @@
         )]
     )
 
-    where = jnp.stack([lax.axis_index("z"), lax.axis_index("core")]).astype(jnp.int32)
+    layer = lax.axis_index("z")
+    where = jnp.stack([layer, 1 - 2 * (layer % 2), lax.axis_index("core")]).astype(jnp.int32)
+    masked, ready = pl.pallas_call(
+        mask_kernel,
+        out_shape=(pltpu.VMEM((depth, width), jnp.bfloat16), pltpu.VMEM((8, LANES), jnp.float32)),
+        grid=(depth // K_BLOCK,),
+        in_specs=[vmem, vmem, pl.BlockSpec((K_BLOCK, width), lambda k: (k, 0))],
+        out_specs=(vmem, vmem),
+        compiler_params=pltpu.CompilerParams(vmem_limit_bytes=8 * MIB),
+    )(cd, ab, pltpu.with_memory_space_constraint(integrals, pltpu.HBM))
+    inner = [(i, i ^ 1) for i in range(8)]
+    outer = [(i, (i - 1 if i % 2 == 0 else i + 1) % 8) for i in range(8)]
+    a0, b0 = amps[:, : depth // 2], amps[:, depth // 2 :]
+    a1 = jnp.concatenate([a0, lax.ppermute(a0, "z", inner)], axis=0)
+    b1 = jnp.concatenate([b0, lax.ppermute(b0, "z", outer)], axis=0)
+    b1, where = lax.optimization_barrier((b1, where))
+    a2, b2 = lax.ppermute(a1, "z", outer), lax.ppermute(b1, "z", inner)
+    a2, ready = lax.optimization_barrier((a2, ready))
+    a3, b3 = lax.ppermute(a2, "z", inner), lax.ppermute(b2, "z", outer)
+    a4, b4 = lax.ppermute(a3, "z", outer), lax.ppermute(b3, "z", inner)
+
     block = pltpu.VMEM((16, rows * width // LANES, LANES), jnp.float32)
-    keep, send, masked = pl.pallas_call(
+    keep, send = pl.pallas_call(
         first_kernel,
-        out_shape=(block, block, pltpu.VMEM((depth, width), jnp.bfloat16)),
+        out_shape=(block, block),
         grid_spec=pltpu.PrefetchScalarGridSpec(
             num_scalar_prefetch=1,
-            grid=(depth // K_BLOCK,),
-            in_specs=[vmem, vmem, pl.BlockSpec((K_BLOCK, width), lambda k, where: (k, 0))]
-            + [vmem] * 14,
-            out_specs=(vmem, vmem, vmem),
-            scratch_shapes=[pltpu.VMEM((7 * amps.shape[0], width), jnp.float32)],
+            grid=(),
+            in_specs=[vmem] * 8,
+            out_specs=(vmem, vmem),
+            scratch_shapes=[pltpu.VMEM((5 * amps.shape[0], width), jnp.float32)],
         ),
-        compiler_params=pltpu.CompilerParams(vmem_limit_bytes=20 * MIB),
-    )(where, cd, ab, pltpu.with_memory_space_constraint(integrals, pltpu.HBM), *pieces)
+        compiler_params=pltpu.CompilerParams(vmem_limit_bytes=16 * MIB),
+    )(where, ready, masked, a1, b1, a2, b2, a3, b3)
     keep, send = pl.pallas_call(
         last_kernel,
         out_shape=(block, block),
         grid_spec=pltpu.PrefetchScalarGridSpec(
             num_scalar_prefetch=1,
             grid=(),
-            in_specs=[vmem] * 5,
+            in_specs=[vmem] * 7,
             out_specs=(vmem, vmem),
-            scratch_shapes=[pltpu.VMEM((amps.shape[0], width), jnp.float32)],
+            scratch_shapes=[pltpu.VMEM((3 * amps.shape[0], width), jnp.float32)],
         ),
-        input_output_aliases={4: 0, 5: 1},
-        compiler_params=pltpu.CompilerParams(vmem_limit_bytes=20 * MIB),
-    )(where, masked, *last, keep, send)
+        input_output_aliases={6: 0, 7: 1},
+        compiler_params=pltpu.CompilerParams(vmem_limit_bytes=16 * MIB),
+    )(where, masked, a3, b3, a4, b4, keep, send)
 
     got = lax.ppermute(send, "core", [(0, 1), (1, 0)])
     packed = pl.pallas_call(

time: 68.8 us -> 67.1 us (0.975)
  starting transfers between devices: 28.1 us -> 20.4 us
  waiting for transfers between devices: 9.47 us -> 16 us
    ppermute x14 -> x8, starting transfers between devices: 23.1 us -> 15.2 us  [the longest x2 5.14 us: on_device(): a2, b2 = (lax.ppermute(a1, 'z', outer), lax.ppermute(b1, 'z', inner))]
    ppermute x14 -> x8, waiting for transfers between devices: 7.56 us -> 14 us  [the longest x2 7.61 us: on_device(): a3, b3 = (lax.ppermute(a2, 'z', inner), lax.ppermute(b2, 'z', outer))]
    pallas_call x1 -> x2, Pallas kernels: 8.87 us -> 8.26 us  [the longest x1 5.43 us: on_device(): pl.pallas_call(mask_kernel, out_shape=(pltpu.VMEM((depth, width), jnp.bfl...]
  transfers between devices with their start and end apart: 15 -> 9, of which waited for: 7 -> 5; matrix products, arithmetic and copies ran while one was open for 0% -> 0% of each run, Pallas kernels for 15% -> 14%
where the time goes in v3:
time: 67.1 us; the launch traced here: 66.8 us
  starting transfers between devices  20.4 us (30%)
  blocking collectives  16.5 us (25%)
  waiting for transfers between devices  16 us (24%)
  Pallas kernels  12.8 us (19%)
  local copies, waits for them, and re-layouts  1.05 us (2%)
    all_to_all x1, blocking collectives, on_device(): parts = lax.all_to_all(packed, ('y', 'x'), 0, 0, tiled=True)  16.5 us
    ppermute x2, waiting for transfers between devices, on_device(): a3, b3 = (lax.ppermute(a2, 'z', inner), lax.ppermute(b2, 'z', outer))  7.61 us
    pallas_call x1, Pallas kernels, on_device(): pl.pallas_call(mask_kernel, out_shape=(pltpu.VMEM((depth, width), jnp.bfl...  5.43 us
    ppermute x1, starting transfers between devices, on_device(): got = lax.ppermute(send, 'core', [(0, 1), (1, 0)])  5.17 us
    ppermute x2, starting transfers between devices, on_device(): a2, b2 = (lax.ppermute(a1, 'z', outer), lax.ppermute(b1, 'z', inner))  5.14 us
    ppermute x1, starting transfers between devices, on_device(): b1 = jnp.concatenate([b0, lax.ppermute(b0, 'z', outer)], axis=0)  4.67 us
    ppermute x2, waiting for transfers between devices, on_device(): a4, b4 = (lax.ppermute(a3, 'z', outer), lax.ppermute(b3, 'z', inner))  4.3 us
    pallas_call x1, Pallas kernels, on_device(): pl.pallas_call(first_kernel, out_shape=(block, block), grid_spec=pltpu.Pr...  2.83 us
  transfers between devices with their start and end apart: 9, of which 5 were waited for; matrix products, arithmetic and copies ran while one was open for 0% of the time, Pallas kernels for 14%

profile of v3, /device:TPU:1, one launch (start us, length us, event | category | flops | bytes accessed | tf_op | source)
XLA Modules:
  0.0 66.8 jit_solution(18057958532738381345)
XLA Ops:
  0.0 1.0 %fusion = (bf16[48,2048]{1,0:T(8,128)(2,1)S(1)}, bf16[48,2048]{1,0:T(8,128)(2,1)S(1)}) fusion(bf16[48,4096]{1,0:T(8,128)(2,1)} %param.11), kind=kLoop, calls=%fused_computation.3 | loop fusion | bytes 786432 | tf_op jit(solution)/shard_map/slice | solution.py:168
  1.1 2.6 %collective-permute-start.1 = (bf16[48,2048]{1,0:T(8,128)(2,1)S(1)}, bf16[48,2048]{1,0:T(8,128)(2,1)S(1)}, u32[]{:S(2)}, u32[]{:S(2)}) collective-permute-start(bf16[48,2048]{1,0:T(8,128)(2,1)S(1)} %get-tuple-element.33), channel_id=1, source_target_pairs={{0,32},{32,0},{64,96},{96,64},{128,160},{160,128},{192,224},{224,1... | collective-permute-start | bytes 589832 | tf_op jit(solution)/shard_map/ppermute | solution.py:169
  3.6 4.7 %collective-permute-start = (bf16[48,2048]{1,0:T(8,128)(2,1)S(1)}, bf16[48,2048]{1,0:T(8,128)(2,1)S(1)}, u32[]{:S(2)}, u32[]{:S(2)}) collective-permute-start(bf16[48,2048]{1,0:T(8,128)(2,1)S(1)} %get-tuple-element.34), channel_id=1, source_target_pairs={{0,224},{32,64},{64,32},{96,128},{128,96},{160,192},{192,160},{224... | collective-permute-start | bytes 589832 | tf_op jit(solution)/shard_map/ppermute | solution.py:170
  8.3 0.1 pad_add_fusion.where
  8.3 0.0 collective-permute-done.1
  8.4 5.0 %collective-permute-start.2 = (bf16[96,2048]{1,0:T(8,128)(2,1)S(1)}, bf16[96,2048]{1,0:T(8,128)(2,1)S(1)}, u32[]{:S(2)}, u32[]{:S(2)}) collective-permute-start(bf16[96,2048]{1,0:T(8,128)(2,1)S(1)} %pad_maximum_fusion.1.a1), channel_id=1, source_target_pairs={{0,224},{32,64},{64,32},{96,128},{128,96},{160,192},{192,160},{224... | collective-permute-start | bytes 1179656 | tf_op jit(solution)/shard_map/ppermute | solution.py:172
  13.4 0.0 collective-permute-done
  13.5 0.1 collective-permute-start.4
  13.6 1.2 %shard_map.109 = (f32[32,128]{1,0:T(8,128)S(1)}, f32[8,128]{1,0:T(8,128)S(1)}, f32[8,128]{1,0:T(8,128)S(1)}, f32[16,128]{1,0:T(8,128)S(1)}) custom-call(s32[32,128]{1,0:T(8,128)} %bitcast.7, s32[32,128]{1,0:T(8,128)} %bitcast.8, s32[8,128]{1,0:T(8,128)} %bitcast.9, s32[8,128]{1,0:T(8,128)} %bitcast.10, s32[12]{0:T(128)} %occ1.1, s32[12]{0:T(128)} %occ2.1, ...), custom_call_target="tpu_custom_call" | custom-call | tf_op jit(solution)/shard_map/pallas_call | solution.py:138
  14.8 5.4 %shard_map.110 = (bf16[4096,1024]{1,0:T(8,128)(2,1)S(1)}, f32[8,128]{1,0:T(8,128)S(1)}) custom-call(f32[32,128]{1,0:T(8,128)S(1)} %get-tuple-element.20.cd, f32[8,128]{1,0:T(8,128)S(1)} %get-tuple-element.21.ab, bf16[4096,1024]{1,0:T(8,128)(2,1)} %values.1), custom_call_target="tpu_custom_call" | custom-call | tf_op jit(solution)/shard_map/pallas_call | solution.py:158
  20.2 1.1 %collective-permute-done.2.a2 = bf16[96,2048]{1,0:T(8,128)(2,1)S(1)} collective-permute-done((bf16[96,2048]{1,0:T(8,128)(2,1)S(1)}, bf16[96,2048]{1,0:T(8,128)(2,1)S(1)}, u32[]{:S(2)}, u32[]{:S(2)}) %collective-permute-start.2) | collective-permute-done | bytes 393248 | tf_op jit(solution)/shard_map/ppermute | solution.py:172
  21.3 1.0 %collective-permute-done.4.b2 = bf16[96,2048]{1,0:T(8,128)(2,1)S(1)} collective-permute-done((bf16[96,2048]{1,0:T(8,128)(2,1)S(1)}, bf16[96,2048]{1,0:T(8,128)(2,1)S(1)}, u32[]{:S(2)}, u32[]{:S(2)}) %collective-permute-start.4) | collective-permute-done | bytes 393248 | tf_op jit(solution)/shard_map/ppermute | solution.py:172
  22.3 1.5 %collective-permute-start.5 = (bf16[96,2048]{1,0:T(8,128)(2,1)S(1)}, bf16[96,2048]{1,0:T(8,128)(2,1)S(1)}, u32[]{:S(2)}, u32[]{:S(2)}) collective-permute-start(bf16[96,2048]{1,0:T(8,128)(2,1)S(1)} %collective-permute-done.4.b2), channel_id=1, source_target_pairs={{0,224},{32,64},{64,32},{96,128},{128,96},{160,192},{192,160},{224... | collective-permute-start | bytes 1179656 | tf_op jit(solution)/shard_map/ppermute | solution.py:174
  23.8 7.6 %collective-permute-done.5.b3 = bf16[96,2048]{1,0:T(8,128)(2,1)S(1)} collective-permute-done((bf16[96,2048]{1,0:T(8,128)(2,1)S(1)}, bf16[96,2048]{1,0:T(8,128)(2,1)S(1)}, u32[]{:S(2)}, u32[]{:S(2)}) %collective-permute-start.5) | collective-permute-done | bytes 393248 | tf_op jit(solution)/shard_map/ppermute | solution.py:174
  31.4 0.0 collective-permute-start.7
  31.4 1.4 %collective-permute-start.6 = (bf16[96,2048]{1,0:T(8,128)(2,1)S(1)}, bf16[96,2048]{1,0:T(8,128)(2,1)S(1)}, u32[]{:S(2)}, u32[]{:S(2)}) collective-permute-start(bf16[96,2048]{1,0:T(8,128)(2,1)S(1)} %collective-permute-done.3.a3), channel_id=1, source_target_pairs={{0,224},{32,64},{64,32},{96,128},{128,96},{160,192},{192,160},{224... | collective-permute-start | bytes 1179656 | tf_op jit(solution)/shard_map/ppermute | solution.py:175
  32.8 2.8 %shard_map.111 = (f32[16,96,128]{2,1,0:T(8,128)S(1)}, f32[16,96,128]{2,1,0:T(8,128)S(1)}) custom-call(s32[3]{0:T(128)S(1)} %pad_add_fusion.where, f32[8,128]{1,0:T(8,128)S(1)} %get-tuple-element.26.ready, bf16[4096,1024]{1,0:T(8,128)(2,1)S(1)} %get-tuple-element.22.masked, bf16[96,2048]{1,0:T(8,128)(2,1)S(1)} %pad_maximum_fusion.1.a1, ...), custom_call_target="tpu_custom_call" | custom-call | tf_op jit(solution)/shard_map/pallas_call | solution.py:178
  35.7 4.3 %collective-permute-done.7.b4 = bf16[96,2048]{1,0:T(8,128)(2,1)S(1)} collective-permute-done((bf16[96,2048]{1,0:T(8,128)(2,1)S(1)}, bf16[96,2048]{1,0:T(8,128)(2,1)S(1)}, u32[]{:S(2)}, u32[]{:S(2)}) %collective-permute-start.7) | collective-permute-done | bytes 393248 | tf_op jit(solution)/shard_map/ppermute | solution.py:175
  40.0 2.3 %shard_map.112 = (f32[16,96,128]{2,1,0:T(8,128)S(1)}, f32[16,96,128]{2,1,0:T(8,128)S(1)}) custom-call(s32[3]{0:T(128)S(1)} %pad_add_fusion.where, bf16[4096,1024]{1,0:T(8,128)(2,1)S(1)} %get-tuple-element.22.masked, bf16[96,2048]{1,0:T(8,128)(2,1)S(1)} %collective-permute-done.3.a3, ...), custom_call_target="tpu_custom_call", output_to_operand_aliasing={{0}: (6, {}), {1}: (7, {})} | custom-call | tf_op jit(solution)/shard_map/pallas_call | solution.py:190
  42.3 5.2 %collective-permute-start.8 = (f32[16,96,128]{2,1,0:T(8,128)S(1)}, f32[16,96,128]{2,1,0:T(8,128)S(1)}, u32[]{:S(2)}, u32[]{:S(2)}) collective-permute-start(f32[16,96,128]{2,1,0:T(8,128)S(1)} %get-tuple-element.30), channel_id=1, source_target_pairs={{0,1},{1,0},{2,3},{3,2},{4,5},{5,4},{6,7},{7,6},{8,9},{9,8},{10,11... | collective-permute-start | bytes 2359304 | tf_op jit(solution)/shard_map/ppermute | solution.py:204
  47.5 1.9 %collective-permute-done.8.got = f32[16,96,128]{2,1,0:T(8,128)S(1)} collective-permute-done((f32[16,96,128]{2,1,0:T(8,128)S(1)}, f32[16,96,128]{2,1,0:T(8,128)S(1)}, u32[]{:S(2)}, u32[]{:S(2)}) %collective-permute-start.8) | collective-permute-done | bytes 786464 | tf_op jit(solution)/shard_map/ppermute | solution.py:204
  49.4 0.2 shard_map.113
  49.6 16.5 %all_to_all.5.parts = s16[16,112,128]{2,1,0:T(8,128)(2,1)S(1)} all-to-all(s16[16,112,128]{2,1,0:T(8,128)(2,1)S(1)} %shard_map.113), channel_id=1, replica_groups=mesh['z'=8,'y'=4,'x'=4,'core'=2] {'y','x'}, dimensions={0} | all-to-all | bytes 917504 | tf_op jit(solution)/shard_map/all_to_all | solution.py:212
  66.1 0.8 %shard_map.114 = f32[12,1024]{1,0:T(8,128)} custom-call(s16[16,112,128]{2,1,0:T(8,128)(2,1)S(1)} %all_to_all.5.parts, f32[8,128]{1,0:T(8,128)S(1)} %get-tuple-element.31.virt, f32[16,128]{1,0:T(8,128)S(1)} %get-tuple-element.32.occ), custom_call_target="tpu_custom_call" | custom-call | tf_op jit(solution)/shard_map/pallas_call | solution.py:213
  (5 shorter events, 0.1 us)
Async XLA Ops:
  1.1 7.3 %collective-permute-start.1 = (bf16[48,2048]{1,0:T(8,128)(2,1)S(1)}, bf16[48,2048]{1,0:T(8,128)(2,1)S(1)}, u32[]{:S(2)}, u32[]{:S(2)}) collective-permute-start(bf16[48,2048]{1,0:T(8,128)(2,1)S(1)} %get-tuple-element.33), channel_id=1, source_target_pairs={{0,32},{32,0},{64,96},{96,64},{128,160},{160,128},{192,224},{224,1... | collective-permute-start | bytes 589832 | tf_op jit(solution)/shard_map/ppermute | solution.py:169
  3.6 9.8 %collective-permute-start = (bf16[48,2048]{1,0:T(8,128)(2,1)S(1)}, bf16[48,2048]{1,0:T(8,128)(2,1)S(1)}, u32[]{:S(2)}, u32[]{:S(2)}) collective-permute-start(bf16[48,2048]{1,0:T(8,128)(2,1)S(1)} %get-tuple-element.34), channel_id=1, source_target_pairs={{0,224},{32,64},{64,32},{96,128},{128,96},{160,192},{192,160},{224... | collective-permute-start | bytes 589832 | tf_op jit(solution)/shard_map/ppermute | solution.py:170
  8.4 12.9 %collective-permute-start.2 = (bf16[96,2048]{1,0:T(8,128)(2,1)S(1)}, bf16[96,2048]{1,0:T(8,128)(2,1)S(1)}, u32[]{:S(2)}, u32[]{:S(2)}) collective-permute-start(bf16[96,2048]{1,0:T(8,128)(2,1)S(1)} %pad_maximum_fusion.1.a1), channel_id=1, source_target_pairs={{0,224},{32,64},{64,32},{96,128},{128,96},{160,192},{192,160},{224... | collective-permute-start | bytes 1179656 | tf_op jit(solution)/shard_map/ppermute | solution.py:172
  13.5 8.9 %collective-permute-start.4 = (bf16[96,2048]{1,0:T(8,128)(2,1)S(1)}, bf16[96,2048]{1,0:T(8,128)(2,1)S(1)}, u32[]{:S(2)}, u32[]{:S(2)}) collective-permute-start(bf16[96,2048]{1,0:T(8,128)(2,1)S(1)} %pad_maximum_fusion.b1), channel_id=1, source_target_pairs={{0,32},{32,0},{64,96},{96,64},{128,160},{160,128},{192,224},{224,1... | collective-permute-start | bytes 1179656 | tf_op jit(solution)/shard_map/ppermute | solution.py:172
  22.3 9.1 %collective-permute-start.5 = (bf16[96,2048]{1,0:T(8,128)(2,1)S(1)}, bf16[96,2048]{1,0:T(8,128)(2,1)S(1)}, u32[]{:S(2)}, u32[]{:S(2)}) collective-permute-start(bf16[96,2048]{1,0:T(8,128)(2,1)S(1)} %collective-permute-done.4.b2), channel_id=1, source_target_pairs={{0,224},{32,64},{64,32},{96,128},{128,96},{160,192},{192,160},{224... | collective-permute-start | bytes 1179656 | tf_op jit(solution)/shard_map/ppermute | solution.py:174
  23.8 7.6 %collective-permute-start.3 = (bf16[96,2048]{1,0:T(8,128)(2,1)S(1)}, bf16[96,2048]{1,0:T(8,128)(2,1)S(1)}, u32[]{:S(2)}, u32[]{:S(2)}) collective-permute-start(bf16[96,2048]{1,0:T(8,128)(2,1)S(1)} %collective-permute-done.2.a2), channel_id=1, source_target_pairs={{0,32},{32,0},{64,96},{96,64},{128,160},{160,128},{192,224},{224,1... | collective-permute-start | bytes 1179656 | tf_op jit(solution)/shard_map/ppermute | solution.py:174
  31.4 8.6 %collective-permute-start.7 = (bf16[96,2048]{1,0:T(8,128)(2,1)S(1)}, bf16[96,2048]{1,0:T(8,128)(2,1)S(1)}, u32[]{:S(2)}, u32[]{:S(2)}) collective-permute-start(bf16[96,2048]{1,0:T(8,128)(2,1)S(1)} %collective-permute-done.5.b3), channel_id=1, source_target_pairs={{0,32},{32,0},{64,96},{96,64},{128,160},{160,128},{192,224},{224,1... | collective-permute-start | bytes 1179656 | tf_op jit(solution)/shard_map/ppermute | solution.py:175
  31.4 8.6 %collective-permute-start.6 = (bf16[96,2048]{1,0:T(8,128)(2,1)S(1)}, bf16[96,2048]{1,0:T(8,128)(2,1)S(1)}, u32[]{:S(2)}, u32[]{:S(2)}) collective-permute-start(bf16[96,2048]{1,0:T(8,128)(2,1)S(1)} %collective-permute-done.3.a3), channel_id=1, source_target_pairs={{0,224},{32,64},{64,32},{96,128},{128,96},{160,192},{192,160},{224... | collective-permute-start | bytes 1179656 | tf_op jit(solution)/shard_map/ppermute | solution.py:175
  42.3 7.1 %collective-permute-start.8 = (f32[16,96,128]{2,1,0:T(8,128)S(1)}, f32[16,96,128]{2,1,0:T(8,128)S(1)}, u32[]{:S(2)}, u32[]{:S(2)}) collective-permute-start(f32[16,96,128]{2,1,0:T(8,128)S(1)} %get-tuple-element.30), channel_id=1, source_target_pairs={{0,1},{1,0},{2,3},{3,2},{4,5},{5,4},{6,7},{7,6},{8,9},{9,8},{10,11... | collective-permute-start | bytes 2359304 | tf_op jit(solution)/shard_map/ppermute | solution.py:204

commit v4 on v3

--- a/solution.py
+++ b/solution.py
@@ -6,7 +6,6 @@
 from jax.sharding import Mesh, PartitionSpec as P
 
 LANES = 128
-K_BLOCK = 1024
 MIB = 1024 * 1024
 
 
@@ -25,17 +24,42 @@
     return picked
 
 
-def tables_kernel(cd1, cd2, ab1, ab2, occ1, occ2, irrep, virt, energy, cd_out, ab_out, virt_out, occ_out):
-    for tile in range(cd1.shape[0] // 8):
-        part = slice(8 * tile, 8 * tile + 8)
-        label = lookup(irrep, cd1[part, :]) ^ lookup(irrep, cd2[part, :])
-        cd_out[part, :] = label.astype(jnp.float32)
-    label = lookup(irrep, ab1[...]) ^ lookup(irrep, ab2[...])
-    ab_out[...] = label.astype(jnp.float32)
+def mask_kernel(cd1, cd2, ab1, ab2, occ1, occ2, irrep, virt, energy, values, masked, virt_out, occ_out, arrived):
+    blocks = arrived.shape[0]
+    size = values.shape[0] // blocks
+    copies = []
+    for block in range(blocks):
+        down = pl.ds(block * size, size)
+        copies.append(
+            pltpu.make_async_copy(values.at[down, :], masked.at[down, :], arrived.at[block])
+        )
+        copies[-1].start()
+
     virt_out[...] = lookup(virt, ab1[...]) + lookup(virt, ab2[...])
     for row in range(occ1.shape[0]):
         both = energy[occ1[row]] + energy[occ2[row]]
         occ_out[row : row + 1, :] = jnp.full((1, LANES), both, jnp.float32)
+    label = lookup(irrep, ab1[...]) ^ lookup(irrep, ab2[...])
+    other = label.astype(jnp.float32).astype(jnp.bfloat16)
+    other = [jnp.broadcast_to(other[i : i + 1, :], (LANES, LANES)) for i in range(ab1.shape[0])]
+    labels = []
+    for tile in range(cd1.shape[0] // 8):
+        part = slice(8 * tile, 8 * tile + 8)
+        label = lookup(irrep, cd1[part, :]) ^ lookup(irrep, cd2[part, :])
+        labels.append(label.astype(jnp.float32))
+
+    for block in range(blocks):
+        copies[block].wait()
+        for part in range(block * size // LANES, (block + 1) * size // LANES):
+            line = labels[part // 8][part % 8 : part % 8 + 1, :]
+            label = jnp.broadcast_to(line, (LANES, LANES)).T.astype(jnp.bfloat16)
+            down = slice(part * LANES, part * LANES + LANES)
+            for lane in range(masked.shape[1] // LANES):
+                across = slice(lane * LANES, lane * LANES + LANES)
+                piece = masked[down, across]
+                masked[down, across] = jnp.where(
+                    label == other[lane], piece, jnp.zeros_like(piece)
+                )
 
 
 def spread(where, total, place, offset, rows, keep, send):
@@ -54,24 +78,6 @@
             send[2 * shard + high, down, :] = sent[:, across]
 
 
-def mask_kernel(cd, ab, values, masked, ready):
-    step = pl.program_id(0)
-    ready[...] = jnp.zeros_like(ready)
-    base = pl.multiple_of(step * K_BLOCK, K_BLOCK)
-    other = ab[...].astype(jnp.bfloat16)
-    for part in range(K_BLOCK // LANES):
-        line = cd[pl.ds(step * (K_BLOCK // LANES) + part, 1), :]
-        label = jnp.broadcast_to(line, (LANES, LANES)).T.astype(jnp.bfloat16)
-        down = slice(part * LANES, part * LANES + LANES)
-        for lane in range(values.shape[1] // LANES):
-            across = slice(lane * LANES, lane * LANES + LANES)
-            block = values[down, across]
-            same = label == jnp.broadcast_to(other[lane : lane + 1, :], (LANES, LANES))
-            masked[pl.ds(base + part * LANES, LANES), across] = jnp.where(
-                same, block, jnp.zeros_like(block)
-            )
-
-
 def dot_into(total, masked, left, right):
     half = masked.shape[0] // 2
     total[...] = jnp.dot(
@@ -83,23 +89,17 @@
 
 
 def first_kernel(where, ready, masked, a1, b1, a2, b2, a3, b3, keep, send, total):
-    size = a2.shape[0] // 2
-    left = [a1[...], a2[...], a3[:size, :]]
-    right = [b1[:size, :], b2[:size, :], b1[size:, :], b3[:size, :], b2[size:, :]]
-    dot_into(total, masked, left, right)
-    for place, offset in enumerate((0, 1, -1, -2, 2)):
-        spread(where, total, place, offset, size // 4, keep, send)
-
-
-def last_kernel(where, masked, a3, b3, a4, b4, keep_in, send_in, keep, send, total):
-    size = a4.shape[0] // 2
-    left = [a3[size:, :], a4[...]]
-    right = [b4[:size, :], b3[size:, :], b4[size:, :]]
-    dot_into(total, masked, left, right)
+    dot_into(total, masked, [a1[...], a2[...], a3[...]], [b1[...], b2[...], b3[...]])
+    for place, offset in enumerate((0, 1, -1, -2, 2, 3)):
+        spread(where, total, place, offset, a1.shape[0] // 8, keep, send)
+
+
+def last_kernel(where, masked, a4, b4, keep_in, send_in, keep, send, total):
+    dot_into(total, masked, [a4[...]], [b4[...]])
     keep[...] = keep_in[...]
     send[...] = send_in[...]
-    for place, offset in enumerate((3, -3, 4)):
-        spread(where, total, place, offset, size // 4, keep, send)
+    for place, offset in enumerate((-3, -4)):
+        spread(where, total, place, offset, a4.shape[0] // 8, keep, send)
 
 
 def pack_kernel(keep, got, out):
@@ -135,44 +135,42 @@
     vmem = pl.BlockSpec(memory_space=pltpu.VMEM)
     smem = pl.BlockSpec(memory_space=pltpu.SMEM)
     square = lambda x: x.reshape(x.shape[0] // LANES, LANES)
-    cd, ab, virt, occ = pl.pallas_call(
-        tables_kernel,
+    masked, virt, occ = pl.pallas_call(
+        mask_kernel,
         out_shape=(
-            pltpu.VMEM((depth // LANES, LANES), jnp.float32),
-            pltpu.VMEM((width // LANES, LANES), jnp.float32),
+            pltpu.VMEM((depth, width), jnp.bfloat16),
             pltpu.VMEM((width // LANES, LANES), jnp.float32),
             pltpu.VMEM((16, LANES), jnp.float32),
         ),
-        in_specs=[vmem] * 4 + [smem] * 2 + [vmem] * 2 + [smem],
-        out_specs=(vmem,) * 4,
+        in_specs=[vmem] * 4 + [smem] * 2 + [vmem] * 2 + [smem, pl.BlockSpec(memory_space=pl.ANY)],
+        out_specs=(vmem,) * 3,
+        scratch_shapes=[pltpu.SemaphoreType.DMA((8,))],
         compiler_params=pltpu.CompilerParams(vmem_limit_bytes=4 * MIB),
     )(
         *[pltpu.with_memory_space_constraint(x, pltpu.HBM) for x in (
             square(cd1), square(cd2), square(ab1), square(ab2), occ1, occ2,
-            irrep, virt_energy, occ_energy,
+            irrep, virt_energy, occ_energy, integrals,
         )]
     )
 
-    layer = lax.axis_index("z")
-    where = jnp.stack([layer, 1 - 2 * (layer % 2), lax.axis_index("core")]).astype(jnp.int32)
-    masked, ready = pl.pallas_call(
-        mask_kernel,
-        out_shape=(pltpu.VMEM((depth, width), jnp.bfloat16), pltpu.VMEM((8, LANES), jnp.float32)),
-        grid=(depth // K_BLOCK,),
-        in_specs=[vmem, vmem, pl.BlockSpec((K_BLOCK, width), lambda k: (k, 0))],
-        out_specs=(vmem, vmem),
-        compiler_params=pltpu.CompilerParams(vmem_limit_bytes=8 * MIB),
-    )(cd, ab, pltpu.with_memory_space_constraint(integrals, pltpu.HBM))
-    inner = [(i, i ^ 1) for i in range(8)]
-    outer = [(i, (i - 1 if i % 2 == 0 else i + 1) % 8) for i in range(8)]
+    layer, core = lax.axis_index("z"), lax.axis_index("core")
+    sign = (1 - 2 * (layer % 2)) * (1 - 2 * core)
+    where = jnp.stack([layer, sign, core]).astype(jnp.int32)
+    inner = lambda i: i ^ 1
+    outer = lambda i: (i - 1 if i % 2 == 0 else i + 1) % 8
+    odd, even = [], []
+    for i in range(8):
+        odd += [(2 * i, 2 * inner(i)), (2 * i + 1, 2 * outer(i) + 1)]
+        even += [(2 * i, 2 * outer(i)), (2 * i + 1, 2 * inner(i) + 1)]
+    axes = ("z", "core")
     a0, b0 = amps[:, : depth // 2], amps[:, depth // 2 :]
-    a1 = jnp.concatenate([a0, lax.ppermute(a0, "z", inner)], axis=0)
-    b1 = jnp.concatenate([b0, lax.ppermute(b0, "z", outer)], axis=0)
+    a1 = jnp.concatenate([a0, lax.ppermute(a0, axes, odd)], axis=0)
+    b1 = jnp.concatenate([b0, lax.ppermute(b0, axes, odd)], axis=0)
     b1, where = lax.optimization_barrier((b1, where))
-    a2, b2 = lax.ppermute(a1, "z", outer), lax.ppermute(b1, "z", inner)
-    a2, ready = lax.optimization_barrier((a2, ready))
-    a3, b3 = lax.ppermute(a2, "z", inner), lax.ppermute(b2, "z", outer)
-    a4, b4 = lax.ppermute(a3, "z", outer), lax.ppermute(b3, "z", inner)
+    a2, b2 = lax.ppermute(a1, axes, even), lax.ppermute(b1, axes, even)
+    a2, ready = lax.optimization_barrier((a2, virt))
+    a3, b3 = lax.ppermute(a2, axes, odd), lax.ppermute(b2, axes, odd)
+    a4, b4 = lax.ppermute(a3, axes, even), lax.ppermute(b3, axes, even)
 
     block = pltpu.VMEM((16, rows * width // LANES, LANES), jnp.float32)
     keep, send = pl.pallas_call(
@@ -183,7 +181,7 @@
             grid=(),
             in_specs=[vmem] * 8,
             out_specs=(vmem, vmem),
-            scratch_shapes=[pltpu.VMEM((5 * amps.shape[0], width), jnp.float32)],
+            scratch_shapes=[pltpu.VMEM((6 * amps.shape[0], width), jnp.float32)],
         ),
         compiler_params=pltpu.CompilerParams(vmem_limit_bytes=16 * MIB),
     )(where, ready, masked, a1, b1, a2, b2, a3, b3)
@@ -193,13 +191,13 @@
         grid_spec=pltpu.PrefetchScalarGridSpec(
             num_scalar_prefetch=1,
             grid=(),
-            in_specs=[vmem] * 7,
+            in_specs=[vmem] * 5,
             out_specs=(vmem, vmem),
-            scratch_shapes=[pltpu.VMEM((3 * amps.shape[0], width), jnp.float32)],
+            scratch_shapes=[pltpu.VMEM((2 * amps.shape[0], width), jnp.float32)],
         ),
-        input_output_aliases={6: 0, 7: 1},
+        input_output_aliases={4: 0, 5: 1},
         compiler_params=pltpu.CompilerParams(vmem_limit_bytes=16 * MIB),
-    )(where, masked, a3, b3, a4, b4, keep, send)
+    )(where, masked, a4, b4, keep, send)
 
     got = lax.ppermute(send, "core", [(0, 1), (1, 0)])
     packed = pl.pallas_call(

time: 67.1 us -> 70.9 us (1.057)
  waiting for transfers between devices: 16 us -> 27.3 us
  starting transfers between devices: 20.4 us -> 14.5 us
  Pallas kernels: 12.8 us -> 11.2 us
    ppermute x8, waiting for transfers between devices: 14 us -> 25.4 us  [the longest x2 9.34 us: on_device(): a3, b3 = (lax.ppermute(a2, axes, odd), lax.ppermute(b2, axes, odd))]
    ppermute x8, starting transfers between devices: 15.2 us -> 9.49 us  [the longest x1 6.49 us: on_device(): a1 = jnp.concatenate([a0, lax.ppermute(a0, axes, odd)], axis=0)]
    pallas_call x1 -> x0, Pallas kernels: 1.2 us -> none  [on_device(): pl.pallas_call(tables_kernel, out_shape=(pltpu.VMEM((depth // LANES, LANE...]
    pallas_call x1, Pallas kernels: 5.43 us -> 4.61 us  [on_device(): pl.pallas_call(mask_kernel, out_shape=(pltpu.VMEM((depth, width), jnp.bfl...]
  transfers between devices with their start and end apart: 9 -> 9, of which waited for: 5 -> 8; matrix products, arithmetic and copies ran while one was open for 0% -> 0% of each run, Pallas kernels for 14% -> 11%
where the time goes in v4:
time: 70.9 us; the launch traced here: 70.7 us
  waiting for transfers between devices  27.3 us (39%)
  blocking collectives  16.5 us (23%)
  starting transfers between devices  14.5 us (20%)
  Pallas kernels  11.2 us (16%)
  local copies, waits for them, and re-layouts  1.05 us (1%)
    all_to_all x1, blocking collectives, on_device(): parts = lax.all_to_all(packed, ('y', 'x'), 0, 0, tiled=True)  16.5 us
    ppermute x2, waiting for transfers between devices, on_device(): a3, b3 = (lax.ppermute(a2, axes, odd), lax.ppermute(b2, axes, odd))  9.34 us
    ppermute x2, waiting for transfers between devices, on_device(): a4, b4 = (lax.ppermute(a3, axes, even), lax.ppermute(b3, axes, even))  6.8 us
    ppermute x1, starting transfers between devices, on_device(): a1 = jnp.concatenate([a0, lax.ppermute(a0, axes, odd)], axis=0)  6.49 us
    ppermute x1, starting transfers between devices, on_device(): got = lax.ppermute(send, 'core', [(0, 1), (1, 0)])  5 us
    pallas_call x1, Pallas kernels, on_device(): pl.pallas_call(mask_kernel, out_shape=(pltpu.VMEM((depth, width), jnp.bfl...  4.61 us
    ppermute x2, waiting for transfers between devices, on_device(): a2, b2 = (lax.ppermute(a1, axes, even), lax.ppermute(b1, axes, even))  3.83 us
    pallas_call x1, Pallas kernels, on_device(): pl.pallas_call(first_kernel, out_shape=(block, block), grid_spec=pltpu.Pr...  3.26 us
  transfers between devices with their start and end apart: 9, of which 8 were waited for; matrix products, arithmetic and copies ran while one was open for 0% of the time, Pallas kernels for 11%

profile of v4, /device:TPU:1, one launch (start us, length us, event | category | flops | bytes accessed | tf_op | source)
XLA Modules:
  0.0 70.7 jit_solution(10871304039533776315)
XLA Ops:
  0.0 1.0 %fusion = (bf16[48,2048]{1,0:T(8,128)(2,1)S(1)}, bf16[48,2048]{1,0:T(8,128)(2,1)S(1)}) fusion(bf16[48,4096]{1,0:T(8,128)(2,1)} %param.11), kind=kLoop, calls=%fused_computation.3 | loop fusion | bytes 786432 | tf_op jit(solution)/shard_map/slice | solution.py:166
  1.1 6.5 %collective-permute-start.1 = (bf16[48,2048]{1,0:T(8,128)(2,1)S(1)}, bf16[48,2048]{1,0:T(8,128)(2,1)S(1)}, u32[]{:S(2)}, u32[]{:S(2)}) collective-permute-start(bf16[48,2048]{1,0:T(8,128)(2,1)S(1)} %get-tuple-element.27), channel_id=1, source_target_pairs={{0,32},{1,225},{32,0},{33,65},{64,96},{65,33},{96,64},{97,129},{12... | collective-permute-start | bytes 589832 | tf_op jit(solution)/shard_map/ppermute | solution.py:167
  7.5 0.1 collective-permute-start
  7.6 0.1 pad_add_fusion.where
  7.7 2.9 %collective-permute-done.1 = bf16[48,2048]{1,0:T(8,128)(2,1)S(1)} collective-permute-done((bf16[48,2048]{1,0:T(8,128)(2,1)S(1)}, bf16[48,2048]{1,0:T(8,128)(2,1)S(1)}, u32[]{:S(2)}, u32[]{:S(2)}) %collective-permute-start.1) | collective-permute-done | bytes 196640 | tf_op jit(solution)/shard_map/ppermute | solution.py:167
  10.6 0.1 collective-permute-start.2
  10.7 2.5 %collective-permute-done = bf16[48,2048]{1,0:T(8,128)(2,1)S(1)} collective-permute-done((bf16[48,2048]{1,0:T(8,128)(2,1)S(1)}, bf16[48,2048]{1,0:T(8,128)(2,1)S(1)}, u32[]{:S(2)}, u32[]{:S(2)}) %collective-permute-start) | collective-permute-done | bytes 196640 | tf_op jit(solution)/shard_map/ppermute | solution.py:168
  13.3 0.1 collective-permute-start.5
  13.4 4.6 %shard_map.109 = (bf16[4096,1024]{1,0:T(8,128)(2,1)S(1)}, f32[8,128]{1,0:T(8,128)S(1)}, f32[16,128]{1,0:T(8,128)S(1)}) custom-call(s32[32,128]{1,0:T(8,128)} %bitcast.7, s32[32,128]{1,0:T(8,128)} %bitcast.8, s32[8,128]{1,0:T(8,128)} %bitcast.9, s32[8,128]{1,0:T(8,128)} %bitcast.10, s32[12]{0:T(128)} %occ1.1, s32[12]{0:T(128)} %occ2.1, s32[2400]{0:T(1024)} %irrep.1, ...), custom_call_target="tpu_custom_call" | custom-call | tf_op jit(solution)/shard_map/pallas_call | solution.py:138
  18.0 3.8 %collective-permute-done.5.b2 = bf16[96,2048]{1,0:T(8,128)(2,1)S(1)} collective-permute-done((bf16[96,2048]{1,0:T(8,128)(2,1)S(1)}, bf16[96,2048]{1,0:T(8,128)(2,1)S(1)}, u32[]{:S(2)}, u32[]{:S(2)}) %collective-permute-start.5) | collective-permute-done | bytes 393248 | tf_op jit(solution)/shard_map/ppermute | solution.py:170
  21.9 2.7 %collective-permute-start.6 = (bf16[96,2048]{1,0:T(8,128)(2,1)S(1)}, bf16[96,2048]{1,0:T(8,128)(2,1)S(1)}, u32[]{:S(2)}, u32[]{:S(2)}) collective-permute-start(bf16[96,2048]{1,0:T(8,128)(2,1)S(1)} %collective-permute-done.5.b2), channel_id=1, source_target_pairs={{0,32},{1,225},{32,0},{33,65},{64,96},{65,33},{96,64},{97,129},{12... | collective-permute-start | bytes 1179656 | tf_op jit(solution)/shard_map/ppermute | solution.py:172
  24.5 0.0 collective-permute-start.3
  24.6 5.1 %collective-permute-done.6.b3 = bf16[96,2048]{1,0:T(8,128)(2,1)S(1)} collective-permute-done((bf16[96,2048]{1,0:T(8,128)(2,1)S(1)}, bf16[96,2048]{1,0:T(8,128)(2,1)S(1)}, u32[]{:S(2)}, u32[]{:S(2)}) %collective-permute-start.6) | collective-permute-done | bytes 393248 | tf_op jit(solution)/shard_map/ppermute | solution.py:172
  29.7 4.2 %collective-permute-done.3.a3 = bf16[96,2048]{1,0:T(8,128)(2,1)S(1)} collective-permute-done((bf16[96,2048]{1,0:T(8,128)(2,1)S(1)}, bf16[96,2048]{1,0:T(8,128)(2,1)S(1)}, u32[]{:S(2)}, u32[]{:S(2)}) %collective-permute-start.3) | collective-permute-done | bytes 393248 | tf_op jit(solution)/shard_map/ppermute | solution.py:172
  33.9 0.0 collective-permute-start.4
  33.9 3.3 %shard_map.110 = (f32[16,96,128]{2,1,0:T(8,128)S(1)}, f32[16,96,128]{2,1,0:T(8,128)S(1)}) custom-call(s32[3]{0:T(128)S(1)} %pad_add_fusion.where, f32[8,128]{1,0:T(8,128)S(1)} %get-tuple-element.21.ready.virt, bf16[4096,1024]{1,0:T(8,128)(2,1)S(1)} %get-tuple-element.17.masked, bf16[96,2048]{1,0:T(8,128)(2,1)S(1)} %pad_maximum_fusion.1.a1, ...), custom_call_target="tpu_custom_call" | custom-call | tf_op jit(solution)/shard_map/pallas_call | solution.py:176
  37.2 2.9 %collective-permute-done.7.b4 = bf16[96,2048]{1,0:T(8,128)(2,1)S(1)} collective-permute-done((bf16[96,2048]{1,0:T(8,128)(2,1)S(1)}, bf16[96,2048]{1,0:T(8,128)(2,1)S(1)}, u32[]{:S(2)}, u32[]{:S(2)}) %collective-permute-start.7) | collective-permute-done | bytes 393248 | tf_op jit(solution)/shard_map/ppermute | solution.py:173
  40.1 3.9 %collective-permute-done.4.a4 = bf16[96,2048]{1,0:T(8,128)(2,1)S(1)} collective-permute-done((bf16[96,2048]{1,0:T(8,128)(2,1)S(1)}, bf16[96,2048]{1,0:T(8,128)(2,1)S(1)}, u32[]{:S(2)}, u32[]{:S(2)}) %collective-permute-start.4) | collective-permute-done | bytes 393248 | tf_op jit(solution)/shard_map/ppermute | solution.py:173
  44.0 2.3 %shard_map.111 = (f32[16,96,128]{2,1,0:T(8,128)S(1)}, f32[16,96,128]{2,1,0:T(8,128)S(1)}) custom-call(s32[3]{0:T(128)S(1)} %pad_add_fusion.where, bf16[4096,1024]{1,0:T(8,128)(2,1)S(1)} %get-tuple-element.17.masked, bf16[96,2048]{1,0:T(8,128)(2,1)S(1)} %collective-permute-done.4.a4, ...), custom_call_target="tpu_custom_call", output_to_operand_aliasing={{0}: (4, {}), {1}: (5, {})} | custom-call | tf_op jit(solution)/shard_map/pallas_call | solution.py:188
  46.3 5.0 %collective-permute-start.8 = (f32[16,96,128]{2,1,0:T(8,128)S(1)}, f32[16,96,128]{2,1,0:T(8,128)S(1)}, u32[]{:S(2)}, u32[]{:S(2)}) collective-permute-start(f32[16,96,128]{2,1,0:T(8,128)S(1)} %get-tuple-element.25), channel_id=1, source_target_pairs={{0,1},{1,0},{2,3},{3,2},{4,5},{5,4},{6,7},{7,6},{8,9},{9,8},{10,11... | collective-permute-start | bytes 2359304 | tf_op jit(solution)/shard_map/ppermute | solution.py:202
  51.3 1.9 %collective-permute-done.8.got = f32[16,96,128]{2,1,0:T(8,128)S(1)} collective-permute-done((f32[16,96,128]{2,1,0:T(8,128)S(1)}, f32[16,96,128]{2,1,0:T(8,128)S(1)}, u32[]{:S(2)}, u32[]{:S(2)}) %collective-permute-start.8) | collective-permute-done | bytes 786464 | tf_op jit(solution)/shard_map/ppermute | solution.py:202
  53.2 0.2 shard_map.112
  53.4 16.5 %all_to_all.5.parts = s16[16,112,128]{2,1,0:T(8,128)(2,1)S(1)} all-to-all(s16[16,112,128]{2,1,0:T(8,128)(2,1)S(1)} %shard_map.112), channel_id=1, replica_groups=mesh['z'=8,'y'=4,'x'=4,'core'=2] {'y','x'}, dimensions={0} | all-to-all | bytes 917504 | tf_op jit(solution)/shard_map/all_to_all | solution.py:210
  69.9 0.8 %shard_map.113 = f32[12,1024]{1,0:T(8,128)} custom-call(s16[16,112,128]{2,1,0:T(8,128)(2,1)S(1)} %all_to_all.5.parts, f32[8,128]{1,0:T(8,128)S(1)} %get-tuple-element.21.ready.virt, f32[16,128]{1,0:T(8,128)S(1)} %get-tuple-element.26.occ), custom_call_target="tpu_custom_call" | custom-call | tf_op jit(solution)/shard_map/pallas_call | solution.py:211
  (4 shorter events, 0.1 us)
Async XLA Ops:
  1.1 9.6 %collective-permute-start.1 = (bf16[48,2048]{1,0:T(8,128)(2,1)S(1)}, bf16[48,2048]{1,0:T(8,128)(2,1)S(1)}, u32[]{:S(2)}, u32[]{:S(2)}) collective-permute-start(bf16[48,2048]{1,0:T(8,128)(2,1)S(1)} %get-tuple-element.27), channel_id=1, source_target_pairs={{0,32},{1,225},{32,0},{33,65},{64,96},{65,33},{96,64},{97,129},{12... | collective-permute-start | bytes 589832 | tf_op jit(solution)/shard_map/ppermute | solution.py:167
  7.5 5.7 %collective-permute-start = (bf16[48,2048]{1,0:T(8,128)(2,1)S(1)}, bf16[48,2048]{1,0:T(8,128)(2,1)S(1)}, u32[]{:S(2)}, u32[]{:S(2)}) collective-permute-start(bf16[48,2048]{1,0:T(8,128)(2,1)S(1)} %get-tuple-element.28), channel_id=1, source_target_pairs={{0,32},{1,225},{32,0},{33,65},{64,96},{65,33},{96,64},{97,129},{12... | collective-permute-start | bytes 589832 | tf_op jit(solution)/shard_map/ppermute | solution.py:168
  10.6 7.4 %collective-permute-start.2 = (bf16[96,2048]{1,0:T(8,128)(2,1)S(1)}, bf16[96,2048]{1,0:T(8,128)(2,1)S(1)}, u32[]{:S(2)}, u32[]{:S(2)}) collective-permute-start(bf16[96,2048]{1,0:T(8,128)(2,1)S(1)} %pad_maximum_fusion.1.a1), channel_id=1, source_target_pairs={{0,224},{1,33},{32,64},{33,1},{64,32},{65,97},{96,128},{97,65},{12... | collective-permute-start | bytes 1179656 | tf_op jit(solution)/shard_map/ppermute | solution.py:170
  13.3 8.6 %collective-permute-start.5 = (bf16[96,2048]{1,0:T(8,128)(2,1)S(1)}, bf16[96,2048]{1,0:T(8,128)(2,1)S(1)}, u32[]{:S(2)}, u32[]{:S(2)}) collective-permute-start(bf16[96,2048]{1,0:T(8,128)(2,1)S(1)} %pad_maximum_fusion.b1), channel_id=1, source_target_pairs={{0,224},{1,33},{32,64},{33,1},{64,32},{65,97},{96,128},{97,65},{12... | collective-permute-start | bytes 1179656 | tf_op jit(solution)/shard_map/ppermute | solution.py:170
  21.9 7.8 %collective-permute-start.6 = (bf16[96,2048]{1,0:T(8,128)(2,1)S(1)}, bf16[96,2048]{1,0:T(8,128)(2,1)S(1)}, u32[]{:S(2)}, u32[]{:S(2)}) collective-permute-start(bf16[96,2048]{1,0:T(8,128)(2,1)S(1)} %collective-permute-done.5.b2), channel_id=1, source_target_pairs={{0,32},{1,225},{32,0},{33,65},{64,96},{65,33},{96,64},{97,129},{12... | collective-permute-start | bytes 1179656 | tf_op jit(solution)/shard_map/ppermute | solution.py:172
  24.5 9.4 %collective-permute-start.3 = (bf16[96,2048]{1,0:T(8,128)(2,1)S(1)}, bf16[96,2048]{1,0:T(8,128)(2,1)S(1)}, u32[]{:S(2)}, u32[]{:S(2)}) collective-permute-start(bf16[96,2048]{1,0:T(8,128)(2,1)S(1)} %collective-permute-done.2.a2), channel_id=1, source_target_pairs={{0,32},{1,225},{32,0},{33,65},{64,96},{65,33},{96,64},{97,129},{12... | collective-permute-start | bytes 1179656 | tf_op jit(solution)/shard_map/ppermute | solution.py:172
  29.7 10.4 %collective-permute-start.7 = (bf16[96,2048]{1,0:T(8,128)(2,1)S(1)}, bf16[96,2048]{1,0:T(8,128)(2,1)S(1)}, u32[]{:S(2)}, u32[]{:S(2)}) collective-permute-start(bf16[96,2048]{1,0:T(8,128)(2,1)S(1)} %collective-permute-done.6.b3), channel_id=1, source_target_pairs={{0,224},{1,33},{32,64},{33,1},{64,32},{65,97},{96,128},{97,65},{12... | collective-permute-start | bytes 1179656 | tf_op jit(solution)/shard_map/ppermute | solution.py:173
  33.9 10.1 %collective-permute-start.4 = (bf16[96,2048]{1,0:T(8,128)(2,1)S(1)}, bf16[96,2048]{1,0:T(8,128)(2,1)S(1)}, u32[]{:S(2)}, u32[]{:S(2)}) collective-permute-start(bf16[96,2048]{1,0:T(8,128)(2,1)S(1)} %collective-permute-done.3.a3), channel_id=1, source_target_pairs={{0,224},{1,33},{32,64},{33,1},{64,32},{65,97},{96,128},{97,65},{12... | collective-permute-start | bytes 1179656 | tf_op jit(solution)/shard_map/ppermute | solution.py:173
  46.3 6.9 %collective-permute-start.8 = (f32[16,96,128]{2,1,0:T(8,128)S(1)}, f32[16,96,128]{2,1,0:T(8,128)S(1)}, u32[]{:S(2)}, u32[]{:S(2)}) collective-permute-start(f32[16,96,128]{2,1,0:T(8,128)S(1)} %get-tuple-element.25), channel_id=1, source_target_pairs={{0,1},{1,0},{2,3},{3,2},{4,5},{5,4},{6,7},{7,6},{8,9},{9,8},{10,11... | collective-permute-start | bytes 2359304 | tf_op jit(solution)/shard_map/ppermute | solution.py:202

commit v5 on v4

--- a/solution.py
+++ b/solution.py
@@ -6,6 +6,7 @@
 from jax.sharding import Mesh, PartitionSpec as P
 
 LANES = 128
+SHARDS = (0, -1, 1, -2, 2, -3, 3)
 MIB = 1024 * 1024
 
 
@@ -62,9 +63,8 @@
                 )
 
 
-def spread(where, total, place, offset, rows, keep, send):
-    first_core = where[2] == 0
-    shard = lax.rem(where[0] + where[1] * offset + 8, 8)
+def spread(where, total, place, rows, keep, send):
+    first_core = where[1] == 0
     for high in range(2):
         at = place * 4 * rows + 2 * high * rows
         even = total[at : at + rows, :]
@@ -74,44 +74,44 @@
         for lane in range(kept.shape[1] // LANES):
             across = slice(lane * LANES, lane * LANES + LANES)
             down = slice(lane * rows, lane * rows + rows)
-            keep[2 * shard + high, down, :] = kept[:, across]
-            send[2 * shard + high, down, :] = sent[:, across]
-
-
-def dot_into(total, masked, left, right):
+            keep[2 * place + high, down, :] = kept[:, across]
+            send[2 * place + high, down, :] = sent[:, across]
+
+
+def first_kernel(where, ready, masked, *refs):
+    pieces = refs[:14]
+    keep, send, total = refs[14:]
     half = masked.shape[0] // 2
-    total[...] = jnp.dot(
-        jnp.concatenate(left, axis=0), masked[:half, :], preferred_element_type=jnp.float32
-    )
-    total[...] += jnp.dot(
-        jnp.concatenate(right, axis=0), masked[half:, :], preferred_element_type=jnp.float32
-    )
-
-
-def first_kernel(where, ready, masked, a1, b1, a2, b2, a3, b3, keep, send, total):
-    dot_into(total, masked, [a1[...], a2[...], a3[...]], [b1[...], b2[...], b3[...]])
-    for place, offset in enumerate((0, 1, -1, -2, 2, 3)):
-        spread(where, total, place, offset, a1.shape[0] // 8, keep, send)
-
-
-def last_kernel(where, masked, a4, b4, keep_in, send_in, keep, send, total):
-    dot_into(total, masked, [a4[...]], [b4[...]])
-    keep[...] = keep_in[...]
-    send[...] = send_in[...]
-    for place, offset in enumerate((-3, -4)):
-        spread(where, total, place, offset, a4.shape[0] // 8, keep, send)
-
-
-def pack_kernel(keep, got, out):
+    left = jnp.concatenate([piece[...] for piece in pieces[0::2]], axis=0)
+    right = jnp.concatenate([piece[...] for piece in pieces[1::2]], axis=0)
+    total[...] = jnp.dot(left, masked[:half, :], preferred_element_type=jnp.float32)
+    total[...] += jnp.dot(right, masked[half:, :], preferred_element_type=jnp.float32)
+    for place in range(7):
+        spread(where, total, place, pieces[0].shape[0] // 4, keep, send)
+
+
+def last_kernel(where, masked, left, right, keep, send, total):
+    half = left.shape[1]
+    total[...] = jnp.dot(left[...], masked[:half, :], preferred_element_type=jnp.float32)
+    total[...] += jnp.dot(right[...], masked[half:, :], preferred_element_type=jnp.float32)
+    spread(where, total, 0, left.shape[0] // 4, keep, send)
+
+
+def pack_kernel(where, keep, got, last_keep, last_got, out):
     rows = keep.shape[1]
-    for block in range(keep.shape[0]):
-        both = keep[block] + got[block]
-        top = jnp.maximum(jnp.max(jnp.abs(both), axis=0, keepdims=True), 1e-30)
-        power = jnp.floor(14.99 - jnp.log2(top))
-        scaled = jnp.clip(jnp.round(both * jnp.exp2(power)), -32767.0, 32767.0)
-        out[block, :rows, :] = scaled.astype(jnp.int32).astype(jnp.int16)
-        power = jnp.broadcast_to(power, (out.shape[1] - rows, LANES))
-        out[block, rows:, :] = power.astype(jnp.int32).astype(jnp.int16)
+    for place, shift in enumerate(SHARDS + (4,)):
+        shard = lax.rem(where[0] + (shift + 8), 8)
+        for high in range(2):
+            if place < len(SHARDS):
+                both = keep[2 * place + high] + got[2 * place + high]
+            else:
+                both = last_keep[high] + last_got[high]
+            top = jnp.maximum(jnp.max(jnp.abs(both), axis=0, keepdims=True), 1e-30)
+            power = jnp.floor(14.99 - jnp.log2(top))
+            scaled = jnp.clip(jnp.round(both * jnp.exp2(power)), -32767.0, 32767.0)
+            out[2 * shard + high, :rows, :] = scaled.astype(jnp.int32).astype(jnp.int16)
+            power = jnp.broadcast_to(power, (out.shape[1] - rows, LANES))
+            out[2 * shard + high, rows:, :] = power.astype(jnp.int32).astype(jnp.int16)
 
 
 def finish_kernel(parts, virt, occ, out):
@@ -153,60 +153,60 @@
         )]
     )
 
-    layer, core = lax.axis_index("z"), lax.axis_index("core")
-    sign = (1 - 2 * (layer % 2)) * (1 - 2 * core)
-    where = jnp.stack([layer, sign, core]).astype(jnp.int32)
-    inner = lambda i: i ^ 1
-    outer = lambda i: (i - 1 if i % 2 == 0 else i + 1) % 8
-    odd, even = [], []
-    for i in range(8):
-        odd += [(2 * i, 2 * inner(i)), (2 * i + 1, 2 * outer(i) + 1)]
-        even += [(2 * i, 2 * outer(i)), (2 * i + 1, 2 * inner(i) + 1)]
-    axes = ("z", "core")
-    a0, b0 = amps[:, : depth // 2], amps[:, depth // 2 :]
-    a1 = jnp.concatenate([a0, lax.ppermute(a0, axes, odd)], axis=0)
-    b1 = jnp.concatenate([b0, lax.ppermute(b0, axes, odd)], axis=0)
-    b1, where = lax.optimization_barrier((b1, where))
-    a2, b2 = lax.ppermute(a1, axes, even), lax.ppermute(b1, axes, even)
-    a2, ready = lax.optimization_barrier((a2, virt))
-    a3, b3 = lax.ppermute(a2, axes, odd), lax.ppermute(b2, axes, odd)
-    a4, b4 = lax.ppermute(a3, axes, even), lax.ppermute(b3, axes, even)
-
-    block = pltpu.VMEM((16, rows * width // LANES, LANES), jnp.float32)
+    where = jnp.stack([lax.axis_index("z"), lax.axis_index("core")]).astype(jnp.int32)
+    forward = [(i, (i + 1) % 8) for i in range(8)]
+    backward = [(i, (i - 1) % 8) for i in range(8)]
+    up = [amps[:, : depth // 2], amps[:, depth // 2 :]]
+    down = list(up)
+    pieces = list(up)
+    for hop in range(3):
+        up[0] = lax.ppermute(up[0], "z", forward)
+        up[1] = lax.ppermute(up[1], "z", forward)
+        down[0] = lax.ppermute(down[0], "z", backward)
+        down[1] = lax.ppermute(down[1], "z", backward)
+        if hop == 0:
+            up[0], ready, where = lax.optimization_barrier((up[0], virt, where))
+        pieces += up + down
+    last = [lax.ppermute(up[0], "z", forward), lax.ppermute(down[1], "z", backward)]
+    size = rows * width // LANES
+    first = pltpu.VMEM((14, size, LANES), jnp.float32)
+    final = pltpu.VMEM((2, size, LANES), jnp.float32)
     keep, send = pl.pallas_call(
         first_kernel,
-        out_shape=(block, block),
+        out_shape=(first, first),
         grid_spec=pltpu.PrefetchScalarGridSpec(
             num_scalar_prefetch=1,
             grid=(),
-            in_specs=[vmem] * 8,
+            in_specs=[vmem] * 16,
             out_specs=(vmem, vmem),
-            scratch_shapes=[pltpu.VMEM((6 * amps.shape[0], width), jnp.float32)],
-        ),
-        compiler_params=pltpu.CompilerParams(vmem_limit_bytes=16 * MIB),
-    )(where, ready, masked, a1, b1, a2, b2, a3, b3)
-    keep, send = pl.pallas_call(
+            scratch_shapes=[pltpu.VMEM((7 * amps.shape[0], width), jnp.float32)],
+        ),
+        compiler_params=pltpu.CompilerParams(vmem_limit_bytes=8 * MIB),
+    )(where, ready, masked, *pieces)
+    swap = [(0, 1), (1, 0)]
+    send, *last = lax.optimization_barrier((send, *last))
+    got = lax.ppermute(send, "core", swap)
+    last_keep, last_send = pl.pallas_call(
         last_kernel,
-        out_shape=(block, block),
+        out_shape=(final, final),
         grid_spec=pltpu.PrefetchScalarGridSpec(
             num_scalar_prefetch=1,
             grid=(),
-            in_specs=[vmem] * 5,
+            in_specs=[vmem] * 3,
             out_specs=(vmem, vmem),
-            scratch_shapes=[pltpu.VMEM((2 * amps.shape[0], width), jnp.float32)],
-        ),
-        input_output_aliases={4: 0, 5: 1},
-        compiler_params=pltpu.CompilerParams(vmem_limit_bytes=16 * MIB),
-    )(where, masked, a4, b4, keep, send)
-
-    got = lax.ppermute(send, "core", [(0, 1), (1, 0)])
+            scratch_shapes=[pltpu.VMEM((amps.shape[0], width), jnp.float32)],
+        ),
+        compiler_params=pltpu.CompilerParams(vmem_limit_bytes=8 * MIB),
+    )(where, masked, *last)
+    last_got = lax.ppermute(last_send, "core", swap)
     packed = pl.pallas_call(
         pack_kernel,
-        out_shape=pltpu.VMEM((16, block.shape[1] + 16, LANES), jnp.int16),
-        in_specs=[vmem] * 2,
-        out_specs=vmem,
+        out_shape=pltpu.VMEM((16, size + 16, LANES), jnp.int16),
+        grid_spec=pltpu.PrefetchScalarGridSpec(
+            num_scalar_prefetch=1, grid=(), in_specs=[vmem] * 4, out_specs=vmem
+        ),
         compiler_params=pltpu.CompilerParams(vmem_limit_bytes=4 * MIB),
-    )(keep, got)
+    )(where, keep, got, last_keep, last_got)
     parts = lax.all_to_all(packed, ("y", "x"), 0, 0, tiled=True)
     return pl.pallas_call(
         finish_kernel,

time: 70.9 us -> 64.4 us (0.908)
  waiting for transfers between devices: 27.3 us -> 6.68 us
  starting transfers between devices: 14.5 us -> 27.7 us
    ppermute x9 -> x16, waiting for transfers between devices: 27.3 us -> 6.68 us  [the longest x3 2.99 us: on_device(): up[0] = lax.ppermute(up[0], 'z', forward)]
    ppermute x9 -> x16, starting transfers between devices: 14.5 us -> 27.7 us  [the longest x3 9.36 us: on_device(): down[1] = lax.ppermute(down[1], 'z', backward)]
    pallas_call x3, Pallas kernels: 5.8 us -> 6.52 us  [the longest x1 3.65 us: on_device(): pl.pallas_call(first_kernel, out_shape=(first, first), grid_spec=pltpu.Pr...]
  transfers between devices with their start and end apart: 9 -> 16, of which waited for: 8 -> 5; matrix products, arithmetic and copies ran while one was open for 0% -> 0% of each run, Pallas kernels for 11% -> 16%
where the time goes in v5:
time: 64.4 us; the launch traced here: 64.2 us
  starting transfers between devices  27.7 us (43%)
  blocking collectives  16.7 us (26%)
  Pallas kernels  11.9 us (18%)
  waiting for transfers between devices  6.68 us (10%)
  local copies, waits for them, and re-layouts  1.05 us (2%)
    all_to_all x1, blocking collectives, on_device(): parts = lax.all_to_all(packed, ('y', 'x'), 0, 0, tiled=True)  16.7 us
    ppermute x3, starting transfers between devices, on_device(): down[1] = lax.ppermute(down[1], 'z', backward)  9.36 us
    ppermute x3, starting transfers between devices, on_device(): down[0] = lax.ppermute(down[0], 'z', backward)  7.05 us
    ppermute x1, starting transfers between devices, on_device(): got = lax.ppermute(send, 'core', swap)  5.8 us
    pallas_call x1, Pallas kernels, on_device(): pl.pallas_call(mask_kernel, out_shape=(pltpu.VMEM((depth, width), jnp.bfl...  4.6 us
    pallas_call x1, Pallas kernels, on_device(): pl.pallas_call(first_kernel, out_shape=(first, first), grid_spec=pltpu.Pr...  3.65 us
    ppermute x3, waiting for transfers between devices, on_device(): up[0] = lax.ppermute(up[0], 'z', forward)  2.99 us
    ppermute x1, starting transfers between devices, on_device(): lax.ppermute(down[1], 'z', backward)  2.67 us
  transfers between devices with their start and end apart: 16, of which 5 were waited for; matrix products, arithmetic and copies ran while one was open for 0% of the time, Pallas kernels for 16%

profile of v5, /device:TPU:1, one launch (start us, length us, event | category | flops | bytes accessed | tf_op | source)
XLA Modules:
  0.0 64.2 jit_solution(11468059221945016641)
XLA Ops:
  0.0 1.0 %fusion = (bf16[48,2048]{1,0:T(8,128)(2,1)S(1)}, bf16[48,2048]{1,0:T(8,128)(2,1)S(1)}) fusion(bf16[48,4096]{1,0:T(8,128)(2,1)} %param.11), kind=kLoop, calls=%fused_computation.1 | loop fusion | bytes 786432 | tf_op jit(solution)/shard_map/slice | solution.py:159
  1.1 2.5 %collective-permute-start = (bf16[48,2048]{1,0:T(8,128)(2,1)S(1)}, bf16[48,2048]{1,0:T(8,128)(2,1)S(1)}, u32[]{:S(2)}, u32[]{:S(2)}) collective-permute-start(bf16[48,2048]{1,0:T(8,128)(2,1)S(1)} %get-tuple-element.32.refs_0_), channel_id=1, source_target_pairs={{0,32},{32,64},{64,96},{96,128},{128,160},{160,192},{192,224},{224... | collective-permute-start | bytes 589832 | tf_op jit(solution)/shard_map/ppermute | solution.py:163
  3.6 4.0 %collective-permute-start.3 = (bf16[48,2048]{1,0:T(8,128)(2,1)S(1)}, bf16[48,2048]{1,0:T(8,128)(2,1)S(1)}, u32[]{:S(2)}, u32[]{:S(2)}) collective-permute-start(bf16[48,2048]{1,0:T(8,128)(2,1)S(1)} %get-tuple-element.31.refs_1_), channel_id=1, source_target_pairs={{0,224},{32,0},{64,32},{96,64},{128,96},{160,128},{192,160},{224,1... | collective-permute-start | bytes 589832 | tf_op jit(solution)/shard_map/ppermute | solution.py:166
  7.6 1.4 %collective-permute-start.2 = (bf16[48,2048]{1,0:T(8,128)(2,1)S(1)}, bf16[48,2048]{1,0:T(8,128)(2,1)S(1)}, u32[]{:S(2)}, u32[]{:S(2)}) collective-permute-start(bf16[48,2048]{1,0:T(8,128)(2,1)S(1)} %get-tuple-element.32.refs_0_), channel_id=1, source_target_pairs={{0,224},{32,0},{64,32},{96,64},{128,96},{160,128},{192,160},{224,1... | collective-permute-start | bytes 589832 | tf_op jit(solution)/shard_map/ppermute | solution.py:165
  9.0 0.1 collective-permute-start.1
  9.2 4.6 %shard_map.109 = (bf16[4096,1024]{1,0:T(8,128)(2,1)S(1)}, f32[8,128]{1,0:T(8,128)S(1)}, f32[16,128]{1,0:T(8,128)S(1)}) custom-call(s32[32,128]{1,0:T(8,128)} %bitcast.6, s32[32,128]{1,0:T(8,128)} %bitcast.7, s32[8,128]{1,0:T(8,128)} %bitcast.8, s32[8,128]{1,0:T(8,128)} %bitcast.9, s32[12]{0:T(128)} %occ1.1, s32[12]{0:T(128)} %occ2.1, s32[2400]{0:T(1024)} %irrep.1, ...), custom_call_target="tpu_custom_call" | custom-call | tf_op jit(solution)/shard_map/pallas_call | solution.py:138
  13.8 0.1 collective-permute-start.4
  13.9 2.7 %collective-permute-start.7 = (bf16[48,2048]{1,0:T(8,128)(2,1)S(1)}, bf16[48,2048]{1,0:T(8,128)(2,1)S(1)}, u32[]{:S(2)}, u32[]{:S(2)}) collective-permute-start(bf16[48,2048]{1,0:T(8,128)(2,1)S(1)} %collective-permute-done.3.refs_5_), channel_id=1, source_target_pairs={{0,224},{32,0},{64,32},{96,64},{128,96},{160,128},{192,160},{224,1... | collective-permute-start | bytes 589832 | tf_op jit(solution)/shard_map/ppermute | solution.py:166
  16.6 2.3 %collective-permute-start.6 = (bf16[48,2048]{1,0:T(8,128)(2,1)S(1)}, bf16[48,2048]{1,0:T(8,128)(2,1)S(1)}, u32[]{:S(2)}, u32[]{:S(2)}) collective-permute-start(bf16[48,2048]{1,0:T(8,128)(2,1)S(1)} %collective-permute-done.2.refs_4_), channel_id=1, source_target_pairs={{0,224},{32,0},{64,32},{96,64},{128,96},{160,128},{192,160},{224,1... | collective-permute-start | bytes 589832 | tf_op jit(solution)/shard_map/ppermute | solution.py:165
  18.8 1.1 %collective-permute-done.4.refs_6_ = bf16[48,2048]{1,0:T(8,128)(2,1)S(1)} collective-permute-done((bf16[48,2048]{1,0:T(8,128)(2,1)S(1)}, bf16[48,2048]{1,0:T(8,128)(2,1)S(1)}, u32[]{:S(2)}, u32[]{:S(2)}) %collective-permute-start.4) | collective-permute-done | bytes 196640 | tf_op jit(solution)/shard_map/ppermute | solution.py:163
  20.0 2.7 %collective-permute-start.11 = (bf16[48,2048]{1,0:T(8,128)(2,1)S(1)}, bf16[48,2048]{1,0:T(8,128)(2,1)S(1)}, u32[]{:S(2)}, u32[]{:S(2)}) collective-permute-start(bf16[48,2048]{1,0:T(8,128)(2,1)S(1)} %collective-permute-done.7.refs_9_), channel_id=1, source_target_pairs={{0,224},{32,0},{64,32},{96,64},{128,96},{160,128},{192,160},{224,1... | collective-permute-start | bytes 589832 | tf_op jit(solution)/shard_map/ppermute | solution.py:166
  22.6 0.9 %collective-permute-done.6.refs_8_ = bf16[48,2048]{1,0:T(8,128)(2,1)S(1)} collective-permute-done((bf16[48,2048]{1,0:T(8,128)(2,1)S(1)}, bf16[48,2048]{1,0:T(8,128)(2,1)S(1)}, u32[]{:S(2)}, u32[]{:S(2)}) %collective-permute-start.6) | collective-permute-done | bytes 196640 | tf_op jit(solution)/shard_map/ppermute | solution.py:165
  23.5 3.4 %collective-permute-start.10 = (bf16[48,2048]{1,0:T(8,128)(2,1)S(1)}, bf16[48,2048]{1,0:T(8,128)(2,1)S(1)}, u32[]{:S(2)}, u32[]{:S(2)}) collective-permute-start(bf16[48,2048]{1,0:T(8,128)(2,1)S(1)} %collective-permute-done.6.refs_8_), channel_id=1, source_target_pairs={{0,224},{32,0},{64,32},{96,64},{128,96},{160,128},{192,160},{224,1... | collective-permute-start | bytes 589832 | tf_op jit(solution)/shard_map/ppermute | solution.py:165
  27.0 1.9 %collective-permute-done.8.refs_10_ = bf16[48,2048]{1,0:T(8,128)(2,1)S(1)} collective-permute-done((bf16[48,2048]{1,0:T(8,128)(2,1)S(1)}, bf16[48,2048]{1,0:T(8,128)(2,1)S(1)}, u32[]{:S(2)}, u32[]{:S(2)}) %collective-permute-start.8) | collective-permute-done | bytes 196640 | tf_op jit(solution)/shard_map/ppermute | solution.py:163
  28.8 2.7 %collective-permute-start.13 = (bf16[48,2048]{1,0:T(8,128)(2,1)S(1)}, bf16[48,2048]{1,0:T(8,128)(2,1)S(1)}, u32[]{:S(2)}, u32[]{:S(2)}) collective-permute-start(bf16[48,2048]{1,0:T(8,128)(2,1)S(1)} %collective-permute-done.11.refs_13_), channel_id=1, source_target_pairs={{0,224},{32,0},{64,32},{96,64},{128,96},{160,128},{192,160},{224,1... | collective-permute-start | bytes 589832 | tf_op jit(solution)/shard_map/ppermute | solution.py:170
  31.5 1.5 %collective-permute-done.9.refs_11_ = bf16[48,2048]{1,0:T(8,128)(2,1)S(1)} collective-permute-done((bf16[48,2048]{1,0:T(8,128)(2,1)S(1)}, bf16[48,2048]{1,0:T(8,128)(2,1)S(1)}, u32[]{:S(2)}, u32[]{:S(2)}) %collective-permute-start.9) | collective-permute-done | bytes 196640 | tf_op jit(solution)/shard_map/ppermute | solution.py:164
  33.0 3.7 %shard_map.110 = (f32[14,96,128]{2,1,0:T(8,128)S(1)}, f32[14,96,128]{2,1,0:T(8,128)S(1)}) custom-call(s32[2]{0:T(128)S(1)} %pad_add_fusion.where, f32[8,128]{1,0:T(8,128)S(1)} %get-tuple-element.20.ready.virt, bf16[4096,1024]{1,0:T(8,128)(2,1)S(1)} %get-tuple-element.21.masked, bf16[48,2048]{1,0:T(8,128)(2,1)S(1)} %get-tuple-element.32.refs_0_, ...), custom_call_target="tpu_custom_call" | custom-call | tf_op jit(solution)/shard_map/pallas_call | solution.py:174
  36.7 5.8 %collective-permute-start.14 = (f32[14,96,128]{2,1,0:T(8,128)S(1)}, f32[14,96,128]{2,1,0:T(8,128)S(1)}, u32[]{:S(2)}, u32[]{:S(2)}) collective-permute-start(f32[14,96,128]{2,1,0:T(8,128)S(1)} %get-tuple-element.25), channel_id=1, source_target_pairs={{0,1},{1,0},{2,3},{3,2},{4,5},{5,4},{6,7},{7,6},{8,9},{9,8},{10,11... | collective-permute-start | bytes 2064392 | tf_op jit(solution)/shard_map/ppermute | solution.py:188
  42.5 2.1 %shard_map.111 = (f32[2,96,128]{2,1,0:T(8,128)S(1)}, f32[2,96,128]{2,1,0:T(8,128)S(1)}) custom-call(s32[2]{0:T(128)S(1)} %pad_add_fusion.where, bf16[4096,1024]{1,0:T(8,128)(2,1)S(1)} %get-tuple-element.21.masked, bf16[48,2048]{1,0:T(8,128)(2,1)S(1)} %collective-permute-done.12.left, bf16[48,2048]{1,0:T(8,128)(2,1)S(1)} %collective-permute-done.13.right), custom_call_target="tpu_custom_call" | custom-call | tf_op jit(solution)/shard_map/pallas_call | solution.py:189
  44.6 0.1 collective-permute-start.15
  44.7 1.3 %collective-permute-done.15.last_got = f32[2,96,128]{2,1,0:T(8,128)S(1)} collective-permute-done((f32[2,96,128]{2,1,0:T(8,128)S(1)}, f32[2,96,128]{2,1,0:T(8,128)S(1)}, u32[]{:S(2)}, u32[]{:S(2)}) %collective-permute-start.15) | collective-permute-done | bytes 98336 | tf_op jit(solution)/shard_map/ppermute | solution.py:201
  46.0 0.8 %shard_map.112 = s16[16,112,128]{2,1,0:T(8,128)(2,1)S(1)} custom-call(s32[2]{0:T(128)S(1)} %pad_add_fusion.where, f32[14,96,128]{2,1,0:T(8,128)S(1)} %get-tuple-element.23.keep, f32[14,96,128]{2,1,0:T(8,128)S(1)} %collective-permute-done.14.got, f32[2,96,128]{2,1,0:T(8,128)S(1)} %get-tuple-element.28.last_keep, ...), custom_call_target="tpu_custom_call" | custom-call | tf_op jit(solution)/shard_map/pallas_call | solution.py:202
  46.7 16.7 %all_to_all.5.parts = s16[16,112,128]{2,1,0:T(8,128)(2,1)S(1)} all-to-all(s16[16,112,128]{2,1,0:T(8,128)(2,1)S(1)} %shard_map.112), channel_id=1, replica_groups=mesh['z'=8,'y'=4,'x'=4,'core'=2] {'y','x'}, dimensions={0} | all-to-all | bytes 917504 | tf_op jit(solution)/shard_map/all_to_all | solution.py:210
  63.5 0.8 %shard_map.113 = f32[12,1024]{1,0:T(8,128)} custom-call(s16[16,112,128]{2,1,0:T(8,128)(2,1)S(1)} %all_to_all.5.parts, f32[8,128]{1,0:T(8,128)S(1)} %get-tuple-element.20.ready.virt, f32[16,128]{1,0:T(8,128)S(1)} %get-tuple-element.30.occ), custom_call_target="tpu_custom_call" | custom-call | tf_op jit(solution)/shard_map/pallas_call | solution.py:211
  (16 shorter events, 0.1 us)
Async XLA Ops:
  1.1 12.7 %collective-permute-start = (bf16[48,2048]{1,0:T(8,128)(2,1)S(1)}, bf16[48,2048]{1,0:T(8,128)(2,1)S(1)}, u32[]{:S(2)}, u32[]{:S(2)}) collective-permute-start(bf16[48,2048]{1,0:T(8,128)(2,1)S(1)} %get-tuple-element.32.refs_0_), channel_id=1, source_target_pairs={{0,32},{32,64},{64,96},{96,128},{128,160},{160,192},{192,224},{224... | collective-permute-start | bytes 589832 | tf_op jit(solution)/shard_map/ppermute | solution.py:163
  3.6 10.3 %collective-permute-start.3 = (bf16[48,2048]{1,0:T(8,128)(2,1)S(1)}, bf16[48,2048]{1,0:T(8,128)(2,1)S(1)}, u32[]{:S(2)}, u32[]{:S(2)}) collective-permute-start(bf16[48,2048]{1,0:T(8,128)(2,1)S(1)} %get-tuple-element.31.refs_1_), channel_id=1, source_target_pairs={{0,224},{32,0},{64,32},{96,64},{128,96},{160,128},{192,160},{224,1... | collective-permute-start | bytes 589832 | tf_op jit(solution)/shard_map/ppermute | solution.py:166
  7.6 8.9 %collective-permute-start.2 = (bf16[48,2048]{1,0:T(8,128)(2,1)S(1)}, bf16[48,2048]{1,0:T(8,128)(2,1)S(1)}, u32[]{:S(2)}, u32[]{:S(2)}) collective-permute-start(bf16[48,2048]{1,0:T(8,128)(2,1)S(1)} %get-tuple-element.32.refs_0_), channel_id=1, source_target_pairs={{0,224},{32,0},{64,32},{96,64},{128,96},{160,128},{192,160},{224,1... | collective-permute-start | bytes 589832 | tf_op jit(solution)/shard_map/ppermute | solution.py:165
  9.0 9.8 %collective-permute-start.1 = (bf16[48,2048]{1,0:T(8,128)(2,1)S(1)}, bf16[48,2048]{1,0:T(8,128)(2,1)S(1)}, u32[]{:S(2)}, u32[]{:S(2)}) collective-permute-start(bf16[48,2048]{1,0:T(8,128)(2,1)S(1)} %get-tuple-element.31.refs_1_), channel_id=1, source_target_pairs={{0,32},{32,64},{64,96},{96,128},{128,160},{160,192},{192,224},{224... | collective-permute-start | bytes 589832 | tf_op jit(solution)/shard_map/ppermute | solution.py:164
  13.8 6.2 %collective-permute-start.4 = (bf16[48,2048]{1,0:T(8,128)(2,1)S(1)}, bf16[48,2048]{1,0:T(8,128)(2,1)S(1)}, u32[]{:S(2)}, u32[]{:S(2)}) collective-permute-start(bf16[48,2048]{1,0:T(8,128)(2,1)S(1)} %collective-permute-done.refs_2_), channel_id=1, source_target_pairs={{0,32},{32,64},{64,96},{96,128},{128,160},{160,192},{192,224},{224... | collective-permute-start | bytes 589832 | tf_op jit(solution)/shard_map/ppermute | solution.py:163
  13.9 6.1 %collective-permute-start.7 = (bf16[48,2048]{1,0:T(8,128)(2,1)S(1)}, bf16[48,2048]{1,0:T(8,128)(2,1)S(1)}, u32[]{:S(2)}, u32[]{:S(2)}) collective-permute-start(bf16[48,2048]{1,0:T(8,128)(2,1)S(1)} %collective-permute-done.3.refs_5_), channel_id=1, source_target_pairs={{0,224},{32,0},{64,32},{96,64},{128,96},{160,128},{192,160},{224,1... | collective-permute-start | bytes 589832 | tf_op jit(solution)/shard_map/ppermute | solution.py:166
  16.6 7.0 %collective-permute-start.6 = (bf16[48,2048]{1,0:T(8,128)(2,1)S(1)}, bf16[48,2048]{1,0:T(8,128)(2,1)S(1)}, u32[]{:S(2)}, u32[]{:S(2)}) collective-permute-start(bf16[48,2048]{1,0:T(8,128)(2,1)S(1)} %collective-permute-done.2.refs_4_), channel_id=1, source_target_pairs={{0,224},{32,0},{64,32},{96,64},{128,96},{160,128},{192,160},{224,1... | collective-permute-start | bytes 589832 | tf_op jit(solution)/shard_map/ppermute | solution.py:165
  18.8 8.1 %collective-permute-start.5 = (bf16[48,2048]{1,0:T(8,128)(2,1)S(1)}, bf16[48,2048]{1,0:T(8,128)(2,1)S(1)}, u32[]{:S(2)}, u32[]{:S(2)}) collective-permute-start(bf16[48,2048]{1,0:T(8,128)(2,1)S(1)} %collective-permute-done.1.refs_3_), channel_id=1, source_target_pairs={{0,32},{32,64},{64,96},{96,128},{128,160},{160,192},{192,224},{224... | collective-permute-start | bytes 589832 | tf_op jit(solution)/shard_map/ppermute | solution.py:164
  19.9 8.9 %collective-permute-start.8 = (bf16[48,2048]{1,0:T(8,128)(2,1)S(1)}, bf16[48,2048]{1,0:T(8,128)(2,1)S(1)}, u32[]{:S(2)}, u32[]{:S(2)}) collective-permute-start(bf16[48,2048]{1,0:T(8,128)(2,1)S(1)} %collective-permute-done.4.refs_6_), channel_id=1, source_target_pairs={{0,32},{32,64},{64,96},{96,128},{128,160},{160,192},{192,224},{224... | collective-permute-start | bytes 589832 | tf_op jit(solution)/shard_map/ppermute | solution.py:163
  20.0 8.9 %collective-permute-start.11 = (bf16[48,2048]{1,0:T(8,128)(2,1)S(1)}, bf16[48,2048]{1,0:T(8,128)(2,1)S(1)}, u32[]{:S(2)}, u32[]{:S(2)}) collective-permute-start(bf16[48,2048]{1,0:T(8,128)(2,1)S(1)} %collective-permute-done.7.refs_9_), channel_id=1, source_target_pairs={{0,224},{32,0},{64,32},{96,64},{128,96},{160,128},{192,160},{224,1... | collective-permute-start | bytes 589832 | tf_op jit(solution)/shard_map/ppermute | solution.py:166
  23.5 8.0 %collective-permute-start.10 = (bf16[48,2048]{1,0:T(8,128)(2,1)S(1)}, bf16[48,2048]{1,0:T(8,128)(2,1)S(1)}, u32[]{:S(2)}, u32[]{:S(2)}) collective-permute-start(bf16[48,2048]{1,0:T(8,128)(2,1)S(1)} %collective-permute-done.6.refs_8_), channel_id=1, source_target_pairs={{0,224},{32,0},{64,32},{96,64},{128,96},{160,128},{192,160},{224,1... | collective-permute-start | bytes 589832 | tf_op jit(solution)/shard_map/ppermute | solution.py:165
  26.9 6.0 %collective-permute-start.9 = (bf16[48,2048]{1,0:T(8,128)(2,1)S(1)}, bf16[48,2048]{1,0:T(8,128)(2,1)S(1)}, u32[]{:S(2)}, u32[]{:S(2)}) collective-permute-start(bf16[48,2048]{1,0:T(8,128)(2,1)S(1)} %collective-permute-done.5.refs_7_), channel_id=1, source_target_pairs={{0,32},{32,64},{64,96},{96,128},{128,160},{160,192},{192,224},{224... | collective-permute-start | bytes 589832 | tf_op jit(solution)/shard_map/ppermute | solution.py:164
  28.8 7.8 %collective-permute-start.12 = (bf16[48,2048]{1,0:T(8,128)(2,1)S(1)}, bf16[48,2048]{1,0:T(8,128)(2,1)S(1)}, u32[]{:S(2)}, u32[]{:S(2)}) collective-permute-start(bf16[48,2048]{1,0:T(8,128)(2,1)S(1)} %collective-permute-done.8.refs_10_), channel_id=1, source_target_pairs={{0,32},{32,64},{64,96},{96,128},{128,160},{160,192},{192,224},{224... | collective-permute-start | bytes 589832 | tf_op jit(solution)/shard_map/ppermute | solution.py:170
  28.8 7.8 %collective-permute-start.13 = (bf16[48,2048]{1,0:T(8,128)(2,1)S(1)}, bf16[48,2048]{1,0:T(8,128)(2,1)S(1)}, u32[]{:S(2)}, u32[]{:S(2)}) collective-permute-start(bf16[48,2048]{1,0:T(8,128)(2,1)S(1)} %collective-permute-done.11.refs_13_), channel_id=1, source_target_pairs={{0,224},{32,0},{64,32},{96,64},{128,96},{160,128},{192,160},{224,1... | collective-permute-start | bytes 589832 | tf_op jit(solution)/shard_map/ppermute | solution.py:170
  36.7 9.3 %collective-permute-start.14 = (f32[14,96,128]{2,1,0:T(8,128)S(1)}, f32[14,96,128]{2,1,0:T(8,128)S(1)}, u32[]{:S(2)}, u32[]{:S(2)}) collective-permute-start(f32[14,96,128]{2,1,0:T(8,128)S(1)} %get-tuple-element.25), channel_id=1, source_target_pairs={{0,1},{1,0},{2,3},{3,2},{4,5},{5,4},{6,7},{7,6},{8,9},{9,8},{10,11... | collective-permute-start | bytes 2064392 | tf_op jit(solution)/shard_map/ppermute | solution.py:188
  44.6 1.4 %collective-permute-start.15 = (f32[2,96,128]{2,1,0:T(8,128)S(1)}, f32[2,96,128]{2,1,0:T(8,128)S(1)}, u32[]{:S(2)}, u32[]{:S(2)}) collective-permute-start(f32[2,96,128]{2,1,0:T(8,128)S(1)} %get-tuple-element.29), channel_id=1, source_target_pairs={{0,1},{1,0},{2,3},{3,2},{4,5},{5,4},{6,7},{7,6},{8,9},{9,8},{10,11... | collective-permute-start | bytes 294920 | tf_op jit(solution)/shard_map/ppermute | solution.py:201

commit v6 on v5

--- a/solution.py
+++ b/solution.py
@@ -6,7 +6,7 @@
 from jax.sharding import Mesh, PartitionSpec as P
 
 LANES = 128
-SHARDS = (0, -1, 1, -2, 2, -3, 3)
+SHARDS = (0, -1, 1, -2, 2, -3, 3, 4)
 MIB = 1024 * 1024
 
 
@@ -78,40 +78,53 @@
             send[2 * place + high, down, :] = sent[:, across]
 
 
-def first_kernel(where, ready, masked, *refs):
-    pieces = refs[:14]
-    keep, send, total = refs[14:]
+def ladder_kernel(where, ready, masked, *refs):
+    pieces = refs[:-3]
+    keep, send, total = refs[-3:]
     half = masked.shape[0] // 2
     left = jnp.concatenate([piece[...] for piece in pieces[0::2]], axis=0)
     right = jnp.concatenate([piece[...] for piece in pieces[1::2]], axis=0)
     total[...] = jnp.dot(left, masked[:half, :], preferred_element_type=jnp.float32)
     total[...] += jnp.dot(right, masked[half:, :], preferred_element_type=jnp.float32)
-    for place in range(7):
+    for place in range(len(pieces) // 2):
         spread(where, total, place, pieces[0].shape[0] // 4, keep, send)
 
 
-def last_kernel(where, masked, left, right, keep, send, total):
-    half = left.shape[1]
-    total[...] = jnp.dot(left[...], masked[:half, :], preferred_element_type=jnp.float32)
-    total[...] += jnp.dot(right[...], masked[half:, :], preferred_element_type=jnp.float32)
-    spread(where, total, 0, left.shape[0] // 4, keep, send)
-
-
-def pack_kernel(where, keep, got, last_keep, last_got, out):
-    rows = keep.shape[1]
-    for place, shift in enumerate(SHARDS + (4,)):
-        shard = lax.rem(where[0] + (shift + 8), 8)
-        for high in range(2):
-            if place < len(SHARDS):
-                both = keep[2 * place + high] + got[2 * place + high]
-            else:
-                both = last_keep[high] + last_got[high]
-            top = jnp.maximum(jnp.max(jnp.abs(both), axis=0, keepdims=True), 1e-30)
-            power = jnp.floor(14.99 - jnp.log2(top))
-            scaled = jnp.clip(jnp.round(both * jnp.exp2(power)), -32767.0, 32767.0)
-            out[2 * shard + high, :rows, :] = scaled.astype(jnp.int32).astype(jnp.int16)
-            power = jnp.broadcast_to(power, (out.shape[1] - rows, LANES))
-            out[2 * shard + high, rows:, :] = power.astype(jnp.int32).astype(jnp.int16)
+def ladder(where, ready, masked, pieces):
+    vmem = pl.BlockSpec(memory_space=pltpu.VMEM)
+    count = len(pieces) // 2
+    height, width = pieces[0].shape[0], masked.shape[1]
+    block = pltpu.VMEM((2 * count, height * width // 4 // LANES, LANES), jnp.float32)
+    return pl.pallas_call(
+        ladder_kernel,
+        out_shape=(block, block),
+        grid_spec=pltpu.PrefetchScalarGridSpec(
+            num_scalar_prefetch=1,
+            grid=(),
+            in_specs=[vmem] * (2 + len(pieces)),
+            out_specs=(vmem, vmem),
+            scratch_shapes=[pltpu.VMEM((count * height, width), jnp.float32)],
+        ),
+        compiler_params=pltpu.CompilerParams(vmem_limit_bytes=8 * MIB),
+    )(where, ready, masked, *pieces)
+
+
+def pack_kernel(where, *refs):
+    out = refs[-1]
+    kept, got = refs[: len(refs) // 2], refs[len(refs) // 2 : -1]
+    rows = kept[0].shape[1]
+    shifts = iter(SHARDS)
+    for mine, other in zip(kept, got):
+        for place in range(mine.shape[0] // 2):
+            shard = lax.rem(where[0] + (next(shifts) + 8), 8)
+            for high in range(2):
+                both = mine[2 * place + high] + other[2 * place + high]
+                top = jnp.maximum(jnp.max(jnp.abs(both), axis=0, keepdims=True), 1e-30)
+                power = jnp.floor(14.99 - jnp.log2(top))
+                scaled = jnp.clip(jnp.round(both * jnp.exp2(power)), -32767.0, 32767.0)
+                out[2 * shard + high, :rows, :] = scaled.astype(jnp.int32).astype(jnp.int16)
+                power = jnp.broadcast_to(power, (out.shape[1] - rows, LANES))
+                out[2 * shard + high, rows:, :] = power.astype(jnp.int32).astype(jnp.int16)
 
 
 def finish_kernel(parts, virt, occ, out):
@@ -167,46 +180,23 @@
         if hop == 0:
             up[0], ready, where = lax.optimization_barrier((up[0], virt, where))
         pieces += up + down
+    ready, up[0], down[1] = lax.optimization_barrier((ready, up[0], down[1]))
     last = [lax.ppermute(up[0], "z", forward), lax.ppermute(down[1], "z", backward)]
-    size = rows * width // LANES
-    first = pltpu.VMEM((14, size, LANES), jnp.float32)
-    final = pltpu.VMEM((2, size, LANES), jnp.float32)
-    keep, send = pl.pallas_call(
-        first_kernel,
-        out_shape=(first, first),
-        grid_spec=pltpu.PrefetchScalarGridSpec(
-            num_scalar_prefetch=1,
-            grid=(),
-            in_specs=[vmem] * 16,
-            out_specs=(vmem, vmem),
-            scratch_shapes=[pltpu.VMEM((7 * amps.shape[0], width), jnp.float32)],
-        ),
-        compiler_params=pltpu.CompilerParams(vmem_limit_bytes=8 * MIB),
-    )(where, ready, masked, *pieces)
     swap = [(0, 1), (1, 0)]
-    send, *last = lax.optimization_barrier((send, *last))
-    got = lax.ppermute(send, "core", swap)
-    last_keep, last_send = pl.pallas_call(
-        last_kernel,
-        out_shape=(final, final),
-        grid_spec=pltpu.PrefetchScalarGridSpec(
-            num_scalar_prefetch=1,
-            grid=(),
-            in_specs=[vmem] * 3,
-            out_specs=(vmem, vmem),
-            scratch_shapes=[pltpu.VMEM((amps.shape[0], width), jnp.float32)],
-        ),
-        compiler_params=pltpu.CompilerParams(vmem_limit_bytes=8 * MIB),
-    )(where, masked, *last)
-    last_got = lax.ppermute(last_send, "core", swap)
+    keep1, send1 = ladder(where, ready, masked, pieces[:10])
+    keep2, send2 = ladder(where, ready, masked, pieces[10:])
+    send1, send2, *last = lax.optimization_barrier((send1, send2, *last))
+    got1, got2 = lax.ppermute(send1, "core", swap), lax.ppermute(send2, "core", swap)
+    keep3, send3 = ladder(where, ready, masked, last)
+    got3 = lax.ppermute(send3, "core", swap)
     packed = pl.pallas_call(
         pack_kernel,
-        out_shape=pltpu.VMEM((16, size + 16, LANES), jnp.int16),
+        out_shape=pltpu.VMEM((16, rows * width // LANES + 16, LANES), jnp.int16),
         grid_spec=pltpu.PrefetchScalarGridSpec(
-            num_scalar_prefetch=1, grid=(), in_specs=[vmem] * 4, out_specs=vmem
+            num_scalar_prefetch=1, grid=(), in_specs=[vmem] * 6, out_specs=vmem
         ),
         compiler_params=pltpu.CompilerParams(vmem_limit_bytes=4 * MIB),
-    )(where, keep, got, last_keep, last_got)
+    )(where, keep1, keep2, keep3, got1, got2, got3)
     parts = lax.all_to_all(packed, ("y", "x"), 0, 0, tiled=True)
     return pl.pallas_call(
         finish_kernel,

time: 64.4 us -> 64.5 us (level)
  waiting for transfers between devices: 6.68 us -> 5.34 us
  Pallas kernels: 11.9 us -> 13.1 us
    ppermute x3, waiting for transfers between devices: 2.99 us -> 1.43 us  [on_device(): up[0] = lax.ppermute(up[0], 'z', forward)]
    pallas_call x3 -> x4, Pallas kernels: 6.52 us -> 7.71 us  [the longest x3 6.96 us: ladder(): pl.pallas_call(ladder_kernel, out_shape=(block, block), grid_spec=pltpu.P...]
    ppermute x3, starting transfers between devices: 7.05 us -> 8.02 us  [on_device(): down[0] = lax.ppermute(down[0], 'z', backward)]
    ppermute x1, waiting for transfers between devices: 0.01 us -> 0.94 us  [on_device(): lax.ppermute(up[0], 'z', forward)]
    ppermute x3, waiting for transfers between devices: 0.91 us -> 0.01 us  [on_device(): down[0] = lax.ppermute(down[0], 'z', backward)]
    ppermute x2 -> x3, starting transfers between devices: 5.9 us -> 5.15 us  [the longest x1 4.55 us: on_device(): lax.ppermute(send1, 'core', swap)]
  transfers between devices with their start and end apart: 16 -> 17, of which waited for: 5 -> 5; matrix products, arithmetic and copies ran while one was open for 0% -> 0% of each run, Pallas kernels for 16% -> 18%
where the time goes in v6:
time: 64.5 us; the launch traced here: 64.1 us
  starting transfers between devices  27.9 us (43%)
  blocking collectives  16.5 us (26%)
  Pallas kernels  13.1 us (20%)
  waiting for transfers between devices  5.34 us (8%)
  local copies, waits for them, and re-layouts  1.05 us (2%)
    all_to_all x1, blocking collectives, on_device(): parts = lax.all_to_all(packed, ('y', 'x'), 0, 0, tiled=True)  16.5 us
    ppermute x3, starting transfers between devices, on_device(): down[1] = lax.ppermute(down[1], 'z', backward)  9.36 us
    ppermute x3, starting transfers between devices, on_device(): down[0] = lax.ppermute(down[0], 'z', backward)  8.02 us
    pallas_call x3, Pallas kernels, ladder(): pl.pallas_call(ladder_kernel, out_shape=(block, block), grid_spec=pltpu.P...  6.96 us
    pallas_call x1, Pallas kernels, on_device(): pl.pallas_call(mask_kernel, out_shape=(pltpu.VMEM((depth, width), jnp.bfl...  4.6 us
    ppermute x1, starting transfers between devices, on_device(): lax.ppermute(send1, 'core', swap)  4.55 us
    ppermute x1, starting transfers between devices, on_device(): lax.ppermute(down[1], 'z', backward)  2.83 us
    ppermute x3, starting transfers between devices, on_device(): up[0] = lax.ppermute(up[0], 'z', forward)  2.58 us
  transfers between devices with their start and end apart: 17, of which 5 were waited for; matrix products, arithmetic and copies ran while one was open for 0% of the time, Pallas kernels for 18%

profile of v6, /device:TPU:1, one launch (start us, length us, event | category | flops | bytes accessed | tf_op | source)
XLA Modules:
  0.0 64.1 jit_solution(11098919130933424638)
XLA Ops:
  0.0 1.0 %fusion = (bf16[48,2048]{1,0:T(8,128)(2,1)S(1)}, bf16[48,2048]{1,0:T(8,128)(2,1)S(1)}) fusion(bf16[48,4096]{1,0:T(8,128)(2,1)} %param.11), kind=kLoop, calls=%fused_computation.1 | loop fusion | bytes 786432 | tf_op jit(solution)/shard_map/slice | solution.py:172
  1.1 2.5 %collective-permute-start = (bf16[48,2048]{1,0:T(8,128)(2,1)S(1)}, bf16[48,2048]{1,0:T(8,128)(2,1)S(1)}, u32[]{:S(2)}, u32[]{:S(2)}) collective-permute-start(bf16[48,2048]{1,0:T(8,128)(2,1)S(1)} %get-tuple-element.44.refs_0_), channel_id=1, source_target_pairs={{0,32},{32,64},{64,96},{96,128},{128,160},{160,192},{192,224},{224... | collective-permute-start | bytes 589832 | tf_op jit(solution)/shard_map/ppermute | solution.py:176
  3.6 4.0 %collective-permute-start.3 = (bf16[48,2048]{1,0:T(8,128)(2,1)S(1)}, bf16[48,2048]{1,0:T(8,128)(2,1)S(1)}, u32[]{:S(2)}, u32[]{:S(2)}) collective-permute-start(bf16[48,2048]{1,0:T(8,128)(2,1)S(1)} %get-tuple-element.43.refs_1_), channel_id=1, source_target_pairs={{0,224},{32,0},{64,32},{96,64},{128,96},{160,128},{192,160},{224,1... | collective-permute-start | bytes 589832 | tf_op jit(solution)/shard_map/ppermute | solution.py:179
  7.6 2.7 %collective-permute-start.7 = (bf16[48,2048]{1,0:T(8,128)(2,1)S(1)}, bf16[48,2048]{1,0:T(8,128)(2,1)S(1)}, u32[]{:S(2)}, u32[]{:S(2)}) collective-permute-start(bf16[48,2048]{1,0:T(8,128)(2,1)S(1)} %get-tuple-element.44.refs_0_), channel_id=1, source_target_pairs={{0,224},{32,0},{64,32},{96,64},{128,96},{160,128},{192,160},{224,1... | collective-permute-start | bytes 589832 | tf_op jit(solution)/shard_map/ppermute | solution.py:178
  10.3 4.6 %shard_map.109 = (bf16[4096,1024]{1,0:T(8,128)(2,1)S(1)}, f32[8,128]{1,0:T(8,128)S(1)}, f32[16,128]{1,0:T(8,128)S(1)}) custom-call(s32[32,128]{1,0:T(8,128)} %bitcast.6, s32[32,128]{1,0:T(8,128)} %bitcast.7, s32[8,128]{1,0:T(8,128)} %bitcast.8, s32[8,128]{1,0:T(8,128)} %bitcast.9, s32[12]{0:T(128)} %occ1.1, s32[12]{0:T(128)} %occ2.1, s32[2400]{0:T(1024)} %irrep.1, ...), custom_call_target="tpu_custom_call" | custom-call | tf_op jit(solution)/shard_map/pallas_call | solution.py:151
  15.0 2.7 %collective-permute-start.4 = (bf16[48,2048]{1,0:T(8,128)(2,1)S(1)}, bf16[48,2048]{1,0:T(8,128)(2,1)S(1)}, u32[]{:S(2)}, u32[]{:S(2)}) collective-permute-start(bf16[48,2048]{1,0:T(8,128)(2,1)S(1)} %collective-permute-done.3.refs_5_), channel_id=1, source_target_pairs={{0,224},{32,0},{64,32},{96,64},{128,96},{160,128},{192,160},{224,1... | collective-permute-start | bytes 589832 | tf_op jit(solution)/shard_map/ppermute | solution.py:179
  17.7 2.7 %collective-permute-start.9 = (bf16[48,2048]{1,0:T(8,128)(2,1)S(1)}, bf16[48,2048]{1,0:T(8,128)(2,1)S(1)}, u32[]{:S(2)}, u32[]{:S(2)}) collective-permute-start(bf16[48,2048]{1,0:T(8,128)(2,1)S(1)} %collective-permute-done.7.refs_4_), channel_id=1, source_target_pairs={{0,224},{32,0},{64,32},{96,64},{128,96},{160,128},{192,160},{224,1... | collective-permute-start | bytes 589832 | tf_op jit(solution)/shard_map/ppermute | solution.py:178
  20.4 0.7 %collective-permute-done.1.refs_6_ = bf16[48,2048]{1,0:T(8,128)(2,1)S(1)} collective-permute-done((bf16[48,2048]{1,0:T(8,128)(2,1)S(1)}, bf16[48,2048]{1,0:T(8,128)(2,1)S(1)}, u32[]{:S(2)}, u32[]{:S(2)}) %collective-permute-start.1) | collective-permute-done | bytes 196640 | tf_op jit(solution)/shard_map/ppermute | solution.py:176
  21.1 2.7 %collective-permute-start.5 = (bf16[48,2048]{1,0:T(8,128)(2,1)S(1)}, bf16[48,2048]{1,0:T(8,128)(2,1)S(1)}, u32[]{:S(2)}, u32[]{:S(2)}) collective-permute-start(bf16[48,2048]{1,0:T(8,128)(2,1)S(1)} %collective-permute-done.4.refs_9_), channel_id=1, source_target_pairs={{0,224},{32,0},{64,32},{96,64},{128,96},{160,128},{192,160},{224,1... | collective-permute-start | bytes 589832 | tf_op jit(solution)/shard_map/ppermute | solution.py:179
  23.8 2.0 %collective-permute-done.8.refs_7_ = bf16[48,2048]{1,0:T(8,128)(2,1)S(1)} collective-permute-done((bf16[48,2048]{1,0:T(8,128)(2,1)S(1)}, bf16[48,2048]{1,0:T(8,128)(2,1)S(1)}, u32[]{:S(2)}, u32[]{:S(2)}) %collective-permute-start.8) | collective-permute-done | bytes 196640 | tf_op jit(solution)/shard_map/ppermute | solution.py:177
  25.8 2.7 %collective-permute-start.11 = (bf16[48,2048]{1,0:T(8,128)(2,1)S(1)}, bf16[48,2048]{1,0:T(8,128)(2,1)S(1)}, u32[]{:S(2)}, u32[]{:S(2)}) collective-permute-start(bf16[48,2048]{1,0:T(8,128)(2,1)S(1)} %collective-permute-done.9.refs_8_), channel_id=1, source_target_pairs={{0,224},{32,0},{64,32},{96,64},{128,96},{160,128},{192,160},{224,1... | collective-permute-start | bytes 589832 | tf_op jit(solution)/shard_map/ppermute | solution.py:178
  28.5 0.7 %collective-permute-done.2.refs_0_ = bf16[48,2048]{1,0:T(8,128)(2,1)S(1)} collective-permute-done((bf16[48,2048]{1,0:T(8,128)(2,1)S(1)}, bf16[48,2048]{1,0:T(8,128)(2,1)S(1)}, u32[]{:S(2)}, u32[]{:S(2)}) %collective-permute-start.2) | collective-permute-done | bytes 196640 | tf_op jit(solution)/shard_map/ppermute | solution.py:176
  29.2 2.8 %collective-permute-start.13 = (bf16[48,2048]{1,0:T(8,128)(2,1)S(1)}, bf16[48,2048]{1,0:T(8,128)(2,1)S(1)}, u32[]{:S(2)}, u32[]{:S(2)}) collective-permute-start(bf16[48,2048]{1,0:T(8,128)(2,1)S(1)} %collective-permute-done.5.refs_3_), channel_id=1, source_target_pairs={{0,224},{32,0},{64,32},{96,64},{128,96},{160,128},{192,160},{224,1... | collective-permute-start | bytes 589832 | tf_op jit(solution)/shard_map/ppermute | solution.py:184
  32.0 2.8 %shard_map.110 = (f32[10,96,128]{2,1,0:T(8,128)S(1)}, f32[10,96,128]{2,1,0:T(8,128)S(1)}) custom-call(s32[2]{0:T(128)S(1)} %pad_add_fusion.where, f32[8,128]{1,0:T(8,128)S(1)} %get-tuple-element.28.ready.virt, bf16[4096,1024]{1,0:T(8,128)(2,1)S(1)} %get-tuple-element.29.masked, bf16[48,2048]{1,0:T(8,128)(2,1)S(1)} %get-tuple-element.44.refs_0_, ...), custom_call_target="tpu_custom_call" | custom-call | tf_op jit(solution)/shard_map/pallas_call | solution.py:98
  34.8 2.0 %shard_map.111 = (f32[4,96,128]{2,1,0:T(8,128)S(1)}, f32[4,96,128]{2,1,0:T(8,128)S(1)}) custom-call(s32[2]{0:T(128)S(1)} %pad_add_fusion.where, f32[8,128]{1,0:T(8,128)S(1)} %get-tuple-element.28.ready.virt, bf16[4096,1024]{1,0:T(8,128)(2,1)S(1)} %get-tuple-element.29.masked, bf16[48,2048]{1,0:T(8,128)(2,1)S(1)} %collective-permute-done.2.refs_0_, ...), custom_call_target="tpu_custom_call" | custom-call | tf_op jit(solution)/shard_map/pallas_call | solution.py:98
  36.9 0.9 %collective-permute-done.12.refs_0_ = bf16[48,2048]{1,0:T(8,128)(2,1)S(1)} collective-permute-done((bf16[48,2048]{1,0:T(8,128)(2,1)S(1)}, bf16[48,2048]{1,0:T(8,128)(2,1)S(1)}, u32[]{:S(2)}, u32[]{:S(2)}) %collective-permute-start.12) | collective-permute-done | bytes 196640 | tf_op jit(solution)/shard_map/ppermute | solution.py:184
  37.8 4.6 %collective-permute-start.14 = (f32[10,96,128]{2,1,0:T(8,128)S(1)}, f32[10,96,128]{2,1,0:T(8,128)S(1)}, u32[]{:S(2)}, u32[]{:S(2)}) collective-permute-start(f32[10,96,128]{2,1,0:T(8,128)S(1)} %get-tuple-element.39), channel_id=1, source_target_pairs={{0,1},{1,0},{2,3},{3,2},{4,5},{5,4},{6,7},{7,6},{8,9},{9,8},{10,11... | collective-permute-start | bytes 1474568 | tf_op jit(solution)/shard_map/ppermute | solution.py:189
  42.4 0.1 collective-permute-start.15
  42.5 2.1 %shard_map.112 = (f32[2,96,128]{2,1,0:T(8,128)S(1)}, f32[2,96,128]{2,1,0:T(8,128)S(1)}) custom-call(s32[2]{0:T(128)S(1)} %pad_add_fusion.where, f32[8,128]{1,0:T(8,128)S(1)} %get-tuple-element.28.ready.virt, bf16[4096,1024]{1,0:T(8,128)(2,1)S(1)} %get-tuple-element.29.masked, bf16[48,2048]{1,0:T(8,128)(2,1)S(1)} %collective-permute-done.12.refs_0_, ...), custom_call_target="tpu_custom_call" | custom-call | tf_op jit(solution)/shard_map/pallas_call | solution.py:98
  44.6 0.5 collective-permute-start.16
  45.1 0.9 %collective-permute-done.16.refs_5_ = f32[2,96,128]{2,1,0:T(8,128)S(1)} collective-permute-done((f32[2,96,128]{2,1,0:T(8,128)S(1)}, f32[2,96,128]{2,1,0:T(8,128)S(1)}, u32[]{:S(2)}, u32[]{:S(2)}) %collective-permute-start.16) | collective-permute-done | bytes 98336 | tf_op jit(solution)/shard_map/ppermute | solution.py:191
  46.1 0.8 %shard_map.113 = s16[16,112,128]{2,1,0:T(8,128)(2,1)S(1)} custom-call(s32[2]{0:T(128)S(1)} %pad_add_fusion.where, f32[10,96,128]{2,1,0:T(8,128)S(1)} %get-tuple-element.30.refs_0_, f32[4,96,128]{2,1,0:T(8,128)S(1)} %get-tuple-element.31.refs_1_, f32[2,96,128]{2,1,0:T(8,128)S(1)} %get-tuple-element.38.refs_2_, ...), custom_call_target="tpu_custom_call" | custom-call | tf_op jit(solution)/shard_map/pallas_call | solution.py:192
  46.8 16.5 %all_to_all.5.parts = s16[16,112,128]{2,1,0:T(8,128)(2,1)S(1)} all-to-all(s16[16,112,128]{2,1,0:T(8,128)(2,1)S(1)} %shard_map.113), channel_id=1, replica_groups=mesh['z'=8,'y'=4,'x'=4,'core'=2] {'y','x'}, dimensions={0} | all-to-all | bytes 917504 | tf_op jit(solution)/shard_map/all_to_all | solution.py:200
  63.3 0.8 %shard_map.114 = f32[12,1024]{1,0:T(8,128)} custom-call(s16[16,112,128]{2,1,0:T(8,128)(2,1)S(1)} %all_to_all.5.parts, f32[8,128]{1,0:T(8,128)S(1)} %get-tuple-element.28.ready.virt, f32[16,128]{1,0:T(8,128)S(1)} %get-tuple-element.42.occ), custom_call_target="tpu_custom_call" | custom-call | tf_op jit(solution)/shard_map/pallas_call | solution.py:201
  (19 shorter events, 0.2 us)
Async XLA Ops:
  1.1 13.9 %collective-permute-start = (bf16[48,2048]{1,0:T(8,128)(2,1)S(1)}, bf16[48,2048]{1,0:T(8,128)(2,1)S(1)}, u32[]{:S(2)}, u32[]{:S(2)}) collective-permute-start(bf16[48,2048]{1,0:T(8,128)(2,1)S(1)} %get-tuple-element.44.refs_0_), channel_id=1, source_target_pairs={{0,32},{32,64},{64,96},{96,128},{128,160},{160,192},{192,224},{224... | collective-permute-start | bytes 589832 | tf_op jit(solution)/shard_map/ppermute | solution.py:176
  3.6 11.4 %collective-permute-start.3 = (bf16[48,2048]{1,0:T(8,128)(2,1)S(1)}, bf16[48,2048]{1,0:T(8,128)(2,1)S(1)}, u32[]{:S(2)}, u32[]{:S(2)}) collective-permute-start(bf16[48,2048]{1,0:T(8,128)(2,1)S(1)} %get-tuple-element.43.refs_1_), channel_id=1, source_target_pairs={{0,224},{32,0},{64,32},{96,64},{128,96},{160,128},{192,160},{224,1... | collective-permute-start | bytes 589832 | tf_op jit(solution)/shard_map/ppermute | solution.py:179
  7.6 10.1 %collective-permute-start.6 = (bf16[48,2048]{1,0:T(8,128)(2,1)S(1)}, bf16[48,2048]{1,0:T(8,128)(2,1)S(1)}, u32[]{:S(2)}, u32[]{:S(2)}) collective-permute-start(bf16[48,2048]{1,0:T(8,128)(2,1)S(1)} %get-tuple-element.43.refs_1_), channel_id=1, source_target_pairs={{0,32},{32,64},{64,96},{96,128},{128,160},{160,192},{192,224},{224... | collective-permute-start | bytes 589832 | tf_op jit(solution)/shard_map/ppermute | solution.py:177
  7.6 10.1 %collective-permute-start.7 = (bf16[48,2048]{1,0:T(8,128)(2,1)S(1)}, bf16[48,2048]{1,0:T(8,128)(2,1)S(1)}, u32[]{:S(2)}, u32[]{:S(2)}) collective-permute-start(bf16[48,2048]{1,0:T(8,128)(2,1)S(1)} %get-tuple-element.44.refs_0_), channel_id=1, source_target_pairs={{0,224},{32,0},{64,32},{96,64},{128,96},{160,128},{192,160},{224,1... | collective-permute-start | bytes 589832 | tf_op jit(solution)/shard_map/ppermute | solution.py:178
  15.0 6.1 %collective-permute-start.1 = (bf16[48,2048]{1,0:T(8,128)(2,1)S(1)}, bf16[48,2048]{1,0:T(8,128)(2,1)S(1)}, u32[]{:S(2)}, u32[]{:S(2)}) collective-permute-start(bf16[48,2048]{1,0:T(8,128)(2,1)S(1)} %collective-permute-done.refs_2_), channel_id=1, source_target_pairs={{0,32},{32,64},{64,96},{96,128},{128,160},{160,192},{192,224},{224... | collective-permute-start | bytes 589832 | tf_op jit(solution)/shard_map/ppermute | solution.py:176
  15.0 6.1 %collective-permute-start.4 = (bf16[48,2048]{1,0:T(8,128)(2,1)S(1)}, bf16[48,2048]{1,0:T(8,128)(2,1)S(1)}, u32[]{:S(2)}, u32[]{:S(2)}) collective-permute-start(bf16[48,2048]{1,0:T(8,128)(2,1)S(1)} %collective-permute-done.3.refs_5_), channel_id=1, source_target_pairs={{0,224},{32,0},{64,32},{96,64},{128,96},{160,128},{192,160},{224,1... | collective-permute-start | bytes 589832 | tf_op jit(solution)/shard_map/ppermute | solution.py:179
  17.7 8.1 %collective-permute-start.8 = (bf16[48,2048]{1,0:T(8,128)(2,1)S(1)}, bf16[48,2048]{1,0:T(8,128)(2,1)S(1)}, u32[]{:S(2)}, u32[]{:S(2)}) collective-permute-start(bf16[48,2048]{1,0:T(8,128)(2,1)S(1)} %collective-permute-done.6.refs_3_), channel_id=1, source_target_pairs={{0,32},{32,64},{64,96},{96,128},{128,160},{160,192},{192,224},{224... | collective-permute-start | bytes 589832 | tf_op jit(solution)/shard_map/ppermute | solution.py:177
  17.7 8.1 %collective-permute-start.9 = (bf16[48,2048]{1,0:T(8,128)(2,1)S(1)}, bf16[48,2048]{1,0:T(8,128)(2,1)S(1)}, u32[]{:S(2)}, u32[]{:S(2)}) collective-permute-start(bf16[48,2048]{1,0:T(8,128)(2,1)S(1)} %collective-permute-done.7.refs_4_), channel_id=1, source_target_pairs={{0,224},{32,0},{64,32},{96,64},{128,96},{160,128},{192,160},{224,1... | collective-permute-start | bytes 589832 | tf_op jit(solution)/shard_map/ppermute | solution.py:178
  21.1 8.1 %collective-permute-start.2 = (bf16[48,2048]{1,0:T(8,128)(2,1)S(1)}, bf16[48,2048]{1,0:T(8,128)(2,1)S(1)}, u32[]{:S(2)}, u32[]{:S(2)}) collective-permute-start(bf16[48,2048]{1,0:T(8,128)(2,1)S(1)} %collective-permute-done.1.refs_6_), channel_id=1, source_target_pairs={{0,32},{32,64},{64,96},{96,128},{128,160},{160,192},{192,224},{224... | collective-permute-start | bytes 589832 | tf_op jit(solution)/shard_map/ppermute | solution.py:176
  21.1 8.1 %collective-permute-start.5 = (bf16[48,2048]{1,0:T(8,128)(2,1)S(1)}, bf16[48,2048]{1,0:T(8,128)(2,1)S(1)}, u32[]{:S(2)}, u32[]{:S(2)}) collective-permute-start(bf16[48,2048]{1,0:T(8,128)(2,1)S(1)} %collective-permute-done.4.refs_9_), channel_id=1, source_target_pairs={{0,224},{32,0},{64,32},{96,64},{128,96},{160,128},{192,160},{224,1... | collective-permute-start | bytes 589832 | tf_op jit(solution)/shard_map/ppermute | solution.py:179
  25.8 9.0 %collective-permute-start.10 = (bf16[48,2048]{1,0:T(8,128)(2,1)S(1)}, bf16[48,2048]{1,0:T(8,128)(2,1)S(1)}, u32[]{:S(2)}, u32[]{:S(2)}) collective-permute-start(bf16[48,2048]{1,0:T(8,128)(2,1)S(1)} %collective-permute-done.8.refs_7_), channel_id=1, source_target_pairs={{0,32},{32,64},{64,96},{96,128},{128,160},{160,192},{192,224},{224... | collective-permute-start | bytes 589832 | tf_op jit(solution)/shard_map/ppermute | solution.py:177
  25.8 9.0 %collective-permute-start.11 = (bf16[48,2048]{1,0:T(8,128)(2,1)S(1)}, bf16[48,2048]{1,0:T(8,128)(2,1)S(1)}, u32[]{:S(2)}, u32[]{:S(2)}) collective-permute-start(bf16[48,2048]{1,0:T(8,128)(2,1)S(1)} %collective-permute-done.9.refs_8_), channel_id=1, source_target_pairs={{0,224},{32,0},{64,32},{96,64},{128,96},{160,128},{192,160},{224,1... | collective-permute-start | bytes 589832 | tf_op jit(solution)/shard_map/ppermute | solution.py:178
  29.2 8.7 %collective-permute-start.12 = (bf16[48,2048]{1,0:T(8,128)(2,1)S(1)}, bf16[48,2048]{1,0:T(8,128)(2,1)S(1)}, u32[]{:S(2)}, u32[]{:S(2)}) collective-permute-start(bf16[48,2048]{1,0:T(8,128)(2,1)S(1)} %collective-permute-done.2.refs_0_), channel_id=1, source_target_pairs={{0,32},{32,64},{64,96},{96,128},{128,160},{160,192},{192,224},{224... | collective-permute-start | bytes 589832 | tf_op jit(solution)/shard_map/ppermute | solution.py:184
  29.2 8.7 %collective-permute-start.13 = (bf16[48,2048]{1,0:T(8,128)(2,1)S(1)}, bf16[48,2048]{1,0:T(8,128)(2,1)S(1)}, u32[]{:S(2)}, u32[]{:S(2)}) collective-permute-start(bf16[48,2048]{1,0:T(8,128)(2,1)S(1)} %collective-permute-done.5.refs_3_), channel_id=1, source_target_pairs={{0,224},{32,0},{64,32},{96,64},{128,96},{160,128},{192,160},{224,1... | collective-permute-start | bytes 589832 | tf_op jit(solution)/shard_map/ppermute | solution.py:184
  37.8 8.2 %collective-permute-start.14 = (f32[10,96,128]{2,1,0:T(8,128)S(1)}, f32[10,96,128]{2,1,0:T(8,128)S(1)}, u32[]{:S(2)}, u32[]{:S(2)}) collective-permute-start(f32[10,96,128]{2,1,0:T(8,128)S(1)} %get-tuple-element.39), channel_id=1, source_target_pairs={{0,1},{1,0},{2,3},{3,2},{4,5},{5,4},{6,7},{7,6},{8,9},{9,8},{10,11... | collective-permute-start | bytes 1474568 | tf_op jit(solution)/shard_map/ppermute | solution.py:189
  42.4 3.7 %collective-permute-start.15 = (f32[4,96,128]{2,1,0:T(8,128)S(1)}, f32[4,96,128]{2,1,0:T(8,128)S(1)}, u32[]{:S(2)}, u32[]{:S(2)}) collective-permute-start(f32[4,96,128]{2,1,0:T(8,128)S(1)} %get-tuple-element.40), channel_id=1, source_target_pairs={{0,1},{1,0},{2,3},{3,2},{4,5},{5,4},{6,7},{7,6},{8,9},{9,8},{10,11... | collective-permute-start | bytes 589832 | tf_op jit(solution)/shard_map/ppermute | solution.py:189
  44.6 1.4 %collective-permute-start.16 = (f32[2,96,128]{2,1,0:T(8,128)S(1)}, f32[2,96,128]{2,1,0:T(8,128)S(1)}, u32[]{:S(2)}, u32[]{:S(2)}) collective-permute-start(f32[2,96,128]{2,1,0:T(8,128)S(1)} %get-tuple-element.41), channel_id=1, source_target_pairs={{0,1},{1,0},{2,3},{3,2},{4,5},{5,4},{6,7},{7,6},{8,9},{9,8},{10,11... | collective-permute-start | bytes 294920 | tf_op jit(solution)/shard_map/ppermute | solution.py:191

commit v7 on v6

--- a/solution.py
+++ b/solution.py
@@ -6,7 +6,7 @@
 from jax.sharding import Mesh, PartitionSpec as P
 
 LANES = 128
-SHARDS = (0, -1, 1, -2, 2, -3, 3, 4)
+SHARDS = (0, -1, 1, -2, 2, -3, 3)
 MIB = 1024 * 1024
 
 
@@ -25,7 +25,14 @@
     return picked
 
 
-def mask_kernel(cd1, cd2, ab1, ab2, occ1, occ2, irrep, virt, energy, values, masked, virt_out, occ_out, arrived):
+def mask_kernel(*refs):
+    values = refs[9]
+    masked, virt_out, occ_out = refs[10:13]
+    cd1, cd2, ab1, ab2, occ1, occ2, irrep, virt, energy = refs[13:22]
+    ready, arrived = refs[22:]
+    small = [
+        pltpu.make_async_copy(refs[i], refs[13 + i], ready.at[i]) for i in range(9)
+    ]
     blocks = arrived.shape[0]
     size = values.shape[0] // blocks
     copies = []
@@ -34,12 +41,11 @@
         copies.append(
             pltpu.make_async_copy(values.at[down, :], masked.at[down, :], arrived.at[block])
         )
-        copies[-1].start()
-
-    virt_out[...] = lookup(virt, ab1[...]) + lookup(virt, ab2[...])
-    for row in range(occ1.shape[0]):
-        both = energy[occ1[row]] + energy[occ2[row]]
-        occ_out[row : row + 1, :] = jnp.full((1, LANES), both, jnp.float32)
+    for copy in small + copies:
+        copy.start()
+    for copy in small:
+        copy.wait()
+
     label = lookup(irrep, ab1[...]) ^ lookup(irrep, ab2[...])
     other = label.astype(jnp.float32).astype(jnp.bfloat16)
     other = [jnp.broadcast_to(other[i : i + 1, :], (LANES, LANES)) for i in range(ab1.shape[0])]
@@ -48,6 +54,14 @@
         part = slice(8 * tile, 8 * tile + 8)
         label = lookup(irrep, cd1[part, :]) ^ lookup(irrep, cd2[part, :])
         labels.append(label.astype(jnp.float32))
+    virt_out[...] = lookup(virt, ab1[...]) + lookup(virt, ab2[...])
+    both = jnp.zeros((8, LANES), jnp.float32)
+    for occ in (occ1, occ2):
+        row = occ[...].reshape(1, -1)
+        row = jnp.pad(row, ((0, 0), (0, LANES - row.shape[1])))
+        both += lookup(energy, jnp.broadcast_to(row, (8, LANES)))
+    column = jnp.broadcast_to(both[0:1, :], (LANES, LANES)).T
+    occ_out[...] = column[: occ_out.shape[0], :]
 
     for block in range(blocks):
         copies[block].wait()
@@ -81,11 +95,11 @@
 def ladder_kernel(where, ready, masked, *refs):
     pieces = refs[:-3]
     keep, send, total = refs[-3:]
-    half = masked.shape[0] // 2
     left = jnp.concatenate([piece[...] for piece in pieces[0::2]], axis=0)
     right = jnp.concatenate([piece[...] for piece in pieces[1::2]], axis=0)
-    total[...] = jnp.dot(left, masked[:half, :], preferred_element_type=jnp.float32)
-    total[...] += jnp.dot(right, masked[half:, :], preferred_element_type=jnp.float32)
+    total[...] = jnp.dot(
+        jnp.concatenate([left, right], axis=1), masked[...], preferred_element_type=jnp.float32
+    )
     for place in range(len(pieces) // 2):
         spread(where, total, place, pieces[0].shape[0] // 4, keep, send)
 
@@ -105,26 +119,33 @@
             out_specs=(vmem, vmem),
             scratch_shapes=[pltpu.VMEM((count * height, width), jnp.float32)],
         ),
-        compiler_params=pltpu.CompilerParams(vmem_limit_bytes=8 * MIB),
+        compiler_params=pltpu.CompilerParams(vmem_limit_bytes=10 * MIB),
     )(where, ready, masked, *pieces)
 
 
-def pack_kernel(where, *refs):
-    out = refs[-1]
-    kept, got = refs[: len(refs) // 2], refs[len(refs) // 2 : -1]
-    rows = kept[0].shape[1]
-    shifts = iter(SHARDS)
-    for mine, other in zip(kept, got):
-        for place in range(mine.shape[0] // 2):
-            shard = lax.rem(where[0] + (next(shifts) + 8), 8)
-            for high in range(2):
-                both = mine[2 * place + high] + other[2 * place + high]
-                top = jnp.maximum(jnp.max(jnp.abs(both), axis=0, keepdims=True), 1e-30)
-                power = jnp.floor(14.99 - jnp.log2(top))
-                scaled = jnp.clip(jnp.round(both * jnp.exp2(power)), -32767.0, 32767.0)
-                out[2 * shard + high, :rows, :] = scaled.astype(jnp.int32).astype(jnp.int16)
-                power = jnp.broadcast_to(power, (out.shape[1] - rows, LANES))
-                out[2 * shard + high, rows:, :] = power.astype(jnp.int32).astype(jnp.int16)
+def pack_into(where, out, kept, got, shifts):
+    rows = kept.shape[1]
+    for place, shift in enumerate(shifts):
+        shard = lax.rem(where[0] + (shift + 8), 8)
+        for high in range(2):
+            both = kept[2 * place + high] + got[2 * place + high]
+            top = jnp.maximum(jnp.max(jnp.abs(both), axis=0, keepdims=True), 1e-30)
+            power = jnp.floor(14.99 - jnp.log2(top))
+            scaled = jnp.clip(jnp.round(both * jnp.exp2(power)), -32767.0, 32767.0)
+            out[2 * shard + high, :rows, :] = scaled.astype(jnp.int32).astype(jnp.int16)
+            power = jnp.broadcast_to(power, (out.shape[1] - rows, LANES))
+            out[2 * shard + high, rows:, :] = power.astype(jnp.int32).astype(jnp.int16)
+
+
+def pack_kernel(where, kept, got, out):
+    for high in range(2):
+        out[2 * lax.rem(where[0] + 4, 8) + high] = jnp.zeros(out.shape[1:], jnp.int16)
+    pack_into(where, out, kept, got, SHARDS)
+
+
+def repack_kernel(where, kept, got, packed, out):
+    out[...] = packed[...]
+    pack_into(where, out, kept, got, (4,))
 
 
 def finish_kernel(parts, virt, occ, out):
@@ -146,8 +167,8 @@
     width = integrals.shape[1]
     rows = occ1.shape[0]
     vmem = pl.BlockSpec(memory_space=pltpu.VMEM)
-    smem = pl.BlockSpec(memory_space=pltpu.SMEM)
     square = lambda x: x.reshape(x.shape[0] // LANES, LANES)
+    small = [square(x) for x in (cd1, cd2, ab1, ab2)] + [occ1, occ2, irrep, virt_energy, occ_energy]
     masked, virt, occ = pl.pallas_call(
         mask_kernel,
         out_shape=(
@@ -155,21 +176,21 @@
             pltpu.VMEM((width // LANES, LANES), jnp.float32),
             pltpu.VMEM((16, LANES), jnp.float32),
         ),
-        in_specs=[vmem] * 4 + [smem] * 2 + [vmem] * 2 + [smem, pl.BlockSpec(memory_space=pl.ANY)],
+        in_specs=[pl.BlockSpec(memory_space=pl.ANY)] * 10,
         out_specs=(vmem,) * 3,
-        scratch_shapes=[pltpu.SemaphoreType.DMA((8,))],
+        scratch_shapes=[
+            pltpu.VMEM(x.shape, x.dtype) for x in small
+        ] + [pltpu.SemaphoreType.DMA((9,)), pltpu.SemaphoreType.DMA((8,))],
         compiler_params=pltpu.CompilerParams(vmem_limit_bytes=4 * MIB),
     )(
-        *[pltpu.with_memory_space_constraint(x, pltpu.HBM) for x in (
-            square(cd1), square(cd2), square(ab1), square(ab2), occ1, occ2,
-            irrep, virt_energy, occ_energy, integrals,
-        )]
+        *[pltpu.with_memory_space_constraint(x, pltpu.HBM) for x in small + [integrals]]
     )
 
     where = jnp.stack([lax.axis_index("z"), lax.axis_index("core")]).astype(jnp.int32)
     forward = [(i, (i + 1) % 8) for i in range(8)]
     backward = [(i, (i - 1) % 8) for i in range(8)]
-    up = [amps[:, : depth // 2], amps[:, depth // 2 :]]
+    again = lax.optimization_barrier(amps)
+    up = [amps[:, : depth // 2], again[:, depth // 2 :]]
     down = list(up)
     pieces = list(up)
     for hop in range(3):
@@ -180,23 +201,25 @@
         if hop == 0:
             up[0], ready, where = lax.optimization_barrier((up[0], virt, where))
         pieces += up + down
-    ready, up[0], down[1] = lax.optimization_barrier((ready, up[0], down[1]))
     last = [lax.ppermute(up[0], "z", forward), lax.ppermute(down[1], "z", backward)]
     swap = [(0, 1), (1, 0)]
-    keep1, send1 = ladder(where, ready, masked, pieces[:10])
-    keep2, send2 = ladder(where, ready, masked, pieces[10:])
-    send1, send2, *last = lax.optimization_barrier((send1, send2, *last))
-    got1, got2 = lax.ppermute(send1, "core", swap), lax.ppermute(send2, "core", swap)
-    keep3, send3 = ladder(where, ready, masked, last)
-    got3 = lax.ppermute(send3, "core", swap)
-    packed = pl.pallas_call(
-        pack_kernel,
-        out_shape=pltpu.VMEM((16, rows * width // LANES + 16, LANES), jnp.int16),
+    keep, send = ladder(where, ready, masked, pieces)
+    send, *last = lax.optimization_barrier((send, *last))
+    got = lax.ppermute(send, "core", swap)
+    last_keep, last_send = ladder(where, ready, masked, last)
+    last_got = lax.ppermute(last_send, "core", swap)
+    whole = pltpu.VMEM((16, rows * width // LANES + 16, LANES), jnp.int16)
+    pack = lambda kernel, aliases, *operands: pl.pallas_call(
+        kernel,
+        out_shape=whole,
         grid_spec=pltpu.PrefetchScalarGridSpec(
-            num_scalar_prefetch=1, grid=(), in_specs=[vmem] * 6, out_specs=vmem
+            num_scalar_prefetch=1, grid=(), in_specs=[vmem] * (len(operands) - 1), out_specs=vmem
         ),
+        input_output_aliases=aliases,
         compiler_params=pltpu.CompilerParams(vmem_limit_bytes=4 * MIB),
-    )(where, keep1, keep2, keep3, got1, got2, got3)
+    )(*operands)
+    packed = pack(pack_kernel, {}, where, keep, got)
+    packed = pack(repack_kernel, {3: 0}, where, last_keep, last_got, packed)
     parts = lax.all_to_all(packed, ("y", "x"), 0, 0, tiled=True)
     return pl.pallas_call(
         finish_kernel,

time: 64.5 us -> 66.5 us (1.031)
  local copies, waits for them, and re-layouts: 1.05 us -> 1.88 us
    ppermute x3, starting transfers between devices: 8.02 us -> 5.96 us  [on_device(): down[0] = lax.ppermute(down[0], 'z', backward)]
    ppermute x3 -> x2, starting transfers between devices: 5.15 us -> 6.66 us  [the longest x1 6.56 us: on_device(): got = lax.ppermute(send, 'core', swap)]
    ppermute x3, waiting for transfers between devices: 0.01 us -> 1.35 us  [on_device(): down[0] = lax.ppermute(down[0], 'z', backward)]
    pallas_call x3 -> x2, Pallas kernels: 6.96 us -> 5.78 us  [ladder(): pl.pallas_call(ladder_kernel, out_shape=(block, block), grid_spec=pltpu.P...]
    pallas_call x1, Pallas kernels: 4.6 us -> 5.72 us  [on_device(): pl.pallas_call(mask_kernel, out_shape=(pltpu.VMEM((depth, width), jnp.bfl...]
    ppermute x3, waiting for transfers between devices: 1.43 us -> 2.54 us  [on_device(): up[0] = lax.ppermute(up[0], 'z', forward)]
    ppermute x3, waiting for transfers between devices: 2.01 us -> 1.05 us  [on_device(): up[1] = lax.ppermute(up[1], 'z', forward)]
    ppermute x1, waiting for transfers between devices: 0.94 us -> 0.01 us  [on_device(): lax.ppermute(up[0], 'z', forward)]
  transfers between devices with their start and end apart: 17 -> 16, of which waited for: 5 -> 7; matrix products, arithmetic and copies ran while one was open for 0% -> 2% of each run, Pallas kernels for 18% -> 18%
where the time goes in v7:
time: 66.5 us; the launch traced here: 66.3 us
  starting transfers between devices  28.2 us (42%)
  blocking collectives  16.7 us (25%)
  Pallas kernels  13.7 us (21%)
  waiting for transfers between devices  5.6 us (8%)
  local copies, waits for them, and re-layouts  1.88 us (3%)
    all_to_all x1, blocking collectives, on_device(): parts = lax.all_to_all(packed, ('y', 'x'), 0, 0, tiled=True)  16.7 us
    ppermute x3, starting transfers between devices, on_device(): down[1] = lax.ppermute(down[1], 'z', backward)  9.44 us
    ppermute x1, starting transfers between devices, on_device(): got = lax.ppermute(send, 'core', swap)  6.56 us
    ppermute x3, starting transfers between devices, on_device(): down[0] = lax.ppermute(down[0], 'z', backward)  5.96 us
    pallas_call x2, Pallas kernels, ladder(): pl.pallas_call(ladder_kernel, out_shape=(block, block), grid_spec=pltpu.P...  5.78 us
    pallas_call x1, Pallas kernels, on_device(): pl.pallas_call(mask_kernel, out_shape=(pltpu.VMEM((depth, width), jnp.bfl...  5.72 us
    ppermute x1, starting transfers between devices, on_device(): lax.ppermute(down[1], 'z', backward)  3.41 us
    ppermute x3, starting transfers between devices, on_device(): up[0] = lax.ppermute(up[0], 'z', forward)  2.63 us
  transfers between devices with their start and end apart: 16, of which 7 were waited for; matrix products, arithmetic and copies ran while one was open for 2% of the time, Pallas kernels for 18%

profile of v7, /device:TPU:1, one launch (start us, length us, event | category | flops | bytes accessed | tf_op | source)
XLA Modules:
  0.0 66.3 jit_solution(9661858358477399201)
XLA Ops:
  0.0 0.9 %slice.6.refs_0_ = bf16[48,2048]{1,0:T(8,128)(2,1)S(1)} slice(bf16[48,4096]{1,0:T(8,128)(2,1)} %param.11), slice={[0:48], [0:2048]} | slice | bytes 393216 | tf_op jit(solution)/shard_map/slice | solution.py:193
  0.9 2.5 %collective-permute-start = (bf16[48,2048]{1,0:T(8,128)(2,1)S(1)}, bf16[48,2048]{1,0:T(8,128)(2,1)S(1)}, u32[]{:S(2)}, u32[]{:S(2)}) collective-permute-start(bf16[48,2048]{1,0:T(8,128)(2,1)S(1)} %slice.6.refs_0_), channel_id=1, source_target_pairs={{0,32},{32,64},{64,96},{96,128},{128,160},{160,192},{192,224},{224... | collective-permute-start | bytes 589832 | tf_op jit(solution)/shard_map/ppermute | solution.py:197
  3.5 0.9 %slice.8.refs_1_ = bf16[48,2048]{1,0:T(8,128)(2,1)S(1)} slice(bf16[48,4096]{1,0:T(8,128)(2,1)} %param.11), slice={[0:48], [2048:4096]} | slice | bytes 393216 | tf_op jit(solution)/shard_map/slice | solution.py:193
  4.4 4.0 %collective-permute-start.3 = (bf16[48,2048]{1,0:T(8,128)(2,1)S(1)}, bf16[48,2048]{1,0:T(8,128)(2,1)S(1)}, u32[]{:S(2)}, u32[]{:S(2)}) collective-permute-start(bf16[48,2048]{1,0:T(8,128)(2,1)S(1)} %slice.8.refs_1_), channel_id=1, source_target_pairs={{0,224},{32,0},{64,32},{96,64},{128,96},{160,128},{192,160},{224,1... | collective-permute-start | bytes 589832 | tf_op jit(solution)/shard_map/ppermute | solution.py:200
  8.5 1.4 %collective-permute-start.2 = (bf16[48,2048]{1,0:T(8,128)(2,1)S(1)}, bf16[48,2048]{1,0:T(8,128)(2,1)S(1)}, u32[]{:S(2)}, u32[]{:S(2)}) collective-permute-start(bf16[48,2048]{1,0:T(8,128)(2,1)S(1)} %slice.6.refs_0_), channel_id=1, source_target_pairs={{0,224},{32,0},{64,32},{96,64},{128,96},{160,128},{192,160},{224,1... | collective-permute-start | bytes 589832 | tf_op jit(solution)/shard_map/ppermute | solution.py:199
  10.0 5.7 %shard_map.109 = (bf16[4096,1024]{1,0:T(8,128)(2,1)S(1)}, f32[8,128]{1,0:T(8,128)S(1)}, f32[16,128]{1,0:T(8,128)S(1)}) custom-call(s32[32,128]{1,0:T(8,128)} %bitcast.6, s32[32,128]{1,0:T(8,128)} %bitcast.7, s32[8,128]{1,0:T(8,128)} %bitcast.8, s32[8,128]{1,0:T(8,128)} %bitcast.9, s32[12]{0:T(128)} %refs_4_.1, s32[12]{0:T(128)} %refs_5_.1, s32[2400]{0:T(1024)} %refs_6_.1, ...), custom_call_target="tpu_custom_call" | custom-call | tf_op jit(solution)/shard_map/pallas_call | solution.py:172
  15.8 2.7 %collective-permute-start.7 = (bf16[48,2048]{1,0:T(8,128)(2,1)S(1)}, bf16[48,2048]{1,0:T(8,128)(2,1)S(1)}, u32[]{:S(2)}, u32[]{:S(2)}) collective-permute-start(bf16[48,2048]{1,0:T(8,128)(2,1)S(1)} %collective-permute-done.3.refs_5_), channel_id=1, source_target_pairs={{0,224},{32,0},{64,32},{96,64},{128,96},{160,128},{192,160},{224,1... | collective-permute-start | bytes 589832 | tf_op jit(solution)/shard_map/ppermute | solution.py:200
  18.6 1.4 %collective-permute-start.6 = (bf16[48,2048]{1,0:T(8,128)(2,1)S(1)}, bf16[48,2048]{1,0:T(8,128)(2,1)S(1)}, u32[]{:S(2)}, u32[]{:S(2)}) collective-permute-start(bf16[48,2048]{1,0:T(8,128)(2,1)S(1)} %collective-permute-done.2.refs_4_), channel_id=1, source_target_pairs={{0,224},{32,0},{64,32},{96,64},{128,96},{160,128},{192,160},{224,1... | collective-permute-start | bytes 589832 | tf_op jit(solution)/shard_map/ppermute | solution.py:199
  20.1 1.9 %collective-permute-done.4.refs_6_ = bf16[48,2048]{1,0:T(8,128)(2,1)S(1)} collective-permute-done((bf16[48,2048]{1,0:T(8,128)(2,1)S(1)}, bf16[48,2048]{1,0:T(8,128)(2,1)S(1)}, u32[]{:S(2)}, u32[]{:S(2)}) %collective-permute-start.4) | collective-permute-done | bytes 196640 | tf_op jit(solution)/shard_map/ppermute | solution.py:197
  21.9 2.7 %collective-permute-start.11 = (bf16[48,2048]{1,0:T(8,128)(2,1)S(1)}, bf16[48,2048]{1,0:T(8,128)(2,1)S(1)}, u32[]{:S(2)}, u32[]{:S(2)}) collective-permute-start(bf16[48,2048]{1,0:T(8,128)(2,1)S(1)} %collective-permute-done.7.refs_9_), channel_id=1, source_target_pairs={{0,224},{32,0},{64,32},{96,64},{128,96},{160,128},{192,160},{224,1... | collective-permute-start | bytes 589832 | tf_op jit(solution)/shard_map/ppermute | solution.py:200
  24.6 0.9 %collective-permute-done.6.refs_8_ = bf16[48,2048]{1,0:T(8,128)(2,1)S(1)} collective-permute-done((bf16[48,2048]{1,0:T(8,128)(2,1)S(1)}, bf16[48,2048]{1,0:T(8,128)(2,1)S(1)}, u32[]{:S(2)}, u32[]{:S(2)}) %collective-permute-start.6) | collective-permute-done | bytes 196640 | tf_op jit(solution)/shard_map/ppermute | solution.py:199
  25.5 3.1 %collective-permute-start.10 = (bf16[48,2048]{1,0:T(8,128)(2,1)S(1)}, bf16[48,2048]{1,0:T(8,128)(2,1)S(1)}, u32[]{:S(2)}, u32[]{:S(2)}) collective-permute-start(bf16[48,2048]{1,0:T(8,128)(2,1)S(1)} %collective-permute-done.6.refs_8_), channel_id=1, source_target_pairs={{0,224},{32,0},{64,32},{96,64},{128,96},{160,128},{192,160},{224,1... | collective-permute-start | bytes 589832 | tf_op jit(solution)/shard_map/ppermute | solution.py:199
  28.6 0.7 %collective-permute-done.8.refs_10_ = bf16[48,2048]{1,0:T(8,128)(2,1)S(1)} collective-permute-done((bf16[48,2048]{1,0:T(8,128)(2,1)S(1)}, bf16[48,2048]{1,0:T(8,128)(2,1)S(1)}, u32[]{:S(2)}, u32[]{:S(2)}) %collective-permute-start.8) | collective-permute-done | bytes 196640 | tf_op jit(solution)/shard_map/ppermute | solution.py:197
  29.4 3.4 %collective-permute-start.13 = (bf16[48,2048]{1,0:T(8,128)(2,1)S(1)}, bf16[48,2048]{1,0:T(8,128)(2,1)S(1)}, u32[]{:S(2)}, u32[]{:S(2)}) collective-permute-start(bf16[48,2048]{1,0:T(8,128)(2,1)S(1)} %collective-permute-done.11.refs_13_), channel_id=1, source_target_pairs={{0,224},{32,0},{64,32},{96,64},{128,96},{160,128},{192,160},{224,1... | collective-permute-start | bytes 589832 | tf_op jit(solution)/shard_map/ppermute | solution.py:204
  32.8 0.5 collective-permute-done.10.refs_12_
  33.3 1.0 %collective-permute-done.9.refs_11_ = bf16[48,2048]{1,0:T(8,128)(2,1)S(1)} collective-permute-done((bf16[48,2048]{1,0:T(8,128)(2,1)S(1)}, bf16[48,2048]{1,0:T(8,128)(2,1)S(1)}, u32[]{:S(2)}, u32[]{:S(2)}) %collective-permute-start.9) | collective-permute-done | bytes 196640 | tf_op jit(solution)/shard_map/ppermute | solution.py:198
  34.3 3.7 %shard_map.110 = (f32[14,96,128]{2,1,0:T(8,128)S(1)}, f32[14,96,128]{2,1,0:T(8,128)S(1)}) custom-call(s32[2]{0:T(128)S(1)} %pad_add_fusion.where, f32[8,128]{1,0:T(8,128)S(1)} %get-tuple-element.20.ready.virt, bf16[4096,1024]{1,0:T(8,128)(2,1)S(1)} %get-tuple-element.21.masked, bf16[48,2048]{1,0:T(8,128)(2,1)S(1)} %slice.6.refs_0_, ...), custom_call_target="tpu_custom_call" | custom-call | tf_op jit(solution)/shard_map/pallas_call | solution.py:112
  38.0 6.6 %collective-permute-start.15 = (f32[14,96,128]{2,1,0:T(8,128)S(1)}, f32[14,96,128]{2,1,0:T(8,128)S(1)}, u32[]{:S(2)}, u32[]{:S(2)}) collective-permute-start(f32[14,96,128]{2,1,0:T(8,128)S(1)} %get-tuple-element.29), channel_id=1, source_target_pairs={{0,1},{1,0},{2,3},{3,2},{4,5},{5,4},{6,7},{7,6},{8,9},{9,8},{10,11... | collective-permute-start | bytes 2064392 | tf_op jit(solution)/shard_map/ppermute | solution.py:208
  44.6 2.1 %shard_map.111 = (f32[2,96,128]{2,1,0:T(8,128)S(1)}, f32[2,96,128]{2,1,0:T(8,128)S(1)}) custom-call(s32[2]{0:T(128)S(1)} %pad_add_fusion.where, f32[8,128]{1,0:T(8,128)S(1)} %get-tuple-element.20.ready.virt, bf16[4096,1024]{1,0:T(8,128)(2,1)S(1)} %get-tuple-element.21.masked, bf16[48,2048]{1,0:T(8,128)(2,1)S(1)} %collective-permute-done.12.refs_0_, ...), custom_call_target="tpu_custom_call" | custom-call | tf_op jit(solution)/shard_map/pallas_call | solution.py:112
  46.8 0.7 %shard_map.112.packed = s16[16,112,128]{2,1,0:T(8,128)(2,1)S(1)} custom-call(s32[2]{0:T(128)S(1)} %pad_add_fusion.where, f32[14,96,128]{2,1,0:T(8,128)S(1)} %get-tuple-element.28.kept, f32[14,96,128]{2,1,0:T(8,128)S(1)} %collective-permute-done.15.got), custom_call_target="tpu_custom_call" | custom-call | tf_op jit(solution)/shard_map/pallas_call | solution.py:212
  47.6 0.5 collective-permute-done.14.got
  48.1 0.7 %shard_map.113 = s16[16,112,128]{2,1,0:T(8,128)(2,1)S(1)} custom-call(s32[2]{0:T(128)S(1)} %pad_add_fusion.where, f32[2,96,128]{2,1,0:T(8,128)S(1)} %get-tuple-element.26.kept, f32[2,96,128]{2,1,0:T(8,128)S(1)} %collective-permute-done.14.got, s16[16,112,128]{2,1,0:T(8,128)(2,1)S(1)} %shard_map.112.packed), custom_call_target="tpu_custom_call", output_to_operand_aliasing={{}: (3, {})} | custom-call | tf_op jit(solution)/shard_map/pallas_call | solution.py:212
  48.8 16.7 %all_to_all.5.parts = s16[16,112,128]{2,1,0:T(8,128)(2,1)S(1)} all-to-all(s16[16,112,128]{2,1,0:T(8,128)(2,1)S(1)} %shard_map.113), channel_id=1, replica_groups=mesh['z'=8,'y'=4,'x'=4,'core'=2] {'y','x'}, dimensions={0} | all-to-all | bytes 917504 | tf_op jit(solution)/shard_map/all_to_all | solution.py:223
  65.5 0.8 %shard_map.114 = f32[12,1024]{1,0:T(8,128)} custom-call(s16[16,112,128]{2,1,0:T(8,128)(2,1)S(1)} %all_to_all.5.parts, f32[8,128]{1,0:T(8,128)S(1)} %get-tuple-element.20.ready.virt, f32[16,128]{1,0:T(8,128)S(1)} %get-tuple-element.30.occ), custom_call_target="tpu_custom_call" | custom-call | tf_op jit(solution)/shard_map/pallas_call | solution.py:224
  (18 shorter events, 0.5 us)
Async XLA Ops:
  0.9 14.8 %collective-permute-start = (bf16[48,2048]{1,0:T(8,128)(2,1)S(1)}, bf16[48,2048]{1,0:T(8,128)(2,1)S(1)}, u32[]{:S(2)}, u32[]{:S(2)}) collective-permute-start(bf16[48,2048]{1,0:T(8,128)(2,1)S(1)} %slice.6.refs_0_), channel_id=1, source_target_pairs={{0,32},{32,64},{64,96},{96,128},{128,160},{160,192},{192,224},{224... | collective-permute-start | bytes 589832 | tf_op jit(solution)/shard_map/ppermute | solution.py:197
  4.4 11.4 %collective-permute-start.3 = (bf16[48,2048]{1,0:T(8,128)(2,1)S(1)}, bf16[48,2048]{1,0:T(8,128)(2,1)S(1)}, u32[]{:S(2)}, u32[]{:S(2)}) collective-permute-start(bf16[48,2048]{1,0:T(8,128)(2,1)S(1)} %slice.8.refs_1_), channel_id=1, source_target_pairs={{0,224},{32,0},{64,32},{96,64},{128,96},{160,128},{192,160},{224,1... | collective-permute-start | bytes 589832 | tf_op jit(solution)/shard_map/ppermute | solution.py:200
  8.5 10.1 %collective-permute-start.2 = (bf16[48,2048]{1,0:T(8,128)(2,1)S(1)}, bf16[48,2048]{1,0:T(8,128)(2,1)S(1)}, u32[]{:S(2)}, u32[]{:S(2)}) collective-permute-start(bf16[48,2048]{1,0:T(8,128)(2,1)S(1)} %slice.6.refs_0_), channel_id=1, source_target_pairs={{0,224},{32,0},{64,32},{96,64},{128,96},{160,128},{192,160},{224,1... | collective-permute-start | bytes 589832 | tf_op jit(solution)/shard_map/ppermute | solution.py:199
  9.9 10.0 %collective-permute-start.1 = (bf16[48,2048]{1,0:T(8,128)(2,1)S(1)}, bf16[48,2048]{1,0:T(8,128)(2,1)S(1)}, u32[]{:S(2)}, u32[]{:S(2)}) collective-permute-start(bf16[48,2048]{1,0:T(8,128)(2,1)S(1)} %slice.8.refs_1_), channel_id=1, source_target_pairs={{0,32},{32,64},{64,96},{96,128},{128,160},{160,192},{192,224},{224... | collective-permute-start | bytes 589832 | tf_op jit(solution)/shard_map/ppermute | solution.py:198
  15.7 6.2 %collective-permute-start.4 = (bf16[48,2048]{1,0:T(8,128)(2,1)S(1)}, bf16[48,2048]{1,0:T(8,128)(2,1)S(1)}, u32[]{:S(2)}, u32[]{:S(2)}) collective-permute-start(bf16[48,2048]{1,0:T(8,128)(2,1)S(1)} %collective-permute-done.refs_2_), channel_id=1, source_target_pairs={{0,32},{32,64},{64,96},{96,128},{128,160},{160,192},{192,224},{224... | collective-permute-start | bytes 589832 | tf_op jit(solution)/shard_map/ppermute | solution.py:197
  15.8 6.1 %collective-permute-start.7 = (bf16[48,2048]{1,0:T(8,128)(2,1)S(1)}, bf16[48,2048]{1,0:T(8,128)(2,1)S(1)}, u32[]{:S(2)}, u32[]{:S(2)}) collective-permute-start(bf16[48,2048]{1,0:T(8,128)(2,1)S(1)} %collective-permute-done.3.refs_5_), channel_id=1, source_target_pairs={{0,224},{32,0},{64,32},{96,64},{128,96},{160,128},{192,160},{224,1... | collective-permute-start | bytes 589832 | tf_op jit(solution)/shard_map/ppermute | solution.py:200
  18.6 6.9 %collective-permute-start.6 = (bf16[48,2048]{1,0:T(8,128)(2,1)S(1)}, bf16[48,2048]{1,0:T(8,128)(2,1)S(1)}, u32[]{:S(2)}, u32[]{:S(2)}) collective-permute-start(bf16[48,2048]{1,0:T(8,128)(2,1)S(1)} %collective-permute-done.2.refs_4_), channel_id=1, source_target_pairs={{0,224},{32,0},{64,32},{96,64},{128,96},{160,128},{192,160},{224,1... | collective-permute-start | bytes 589832 | tf_op jit(solution)/shard_map/ppermute | solution.py:199
  20.0 8.6 %collective-permute-start.5 = (bf16[48,2048]{1,0:T(8,128)(2,1)S(1)}, bf16[48,2048]{1,0:T(8,128)(2,1)S(1)}, u32[]{:S(2)}, u32[]{:S(2)}) collective-permute-start(bf16[48,2048]{1,0:T(8,128)(2,1)S(1)} %collective-permute-done.1.refs_3_), channel_id=1, source_target_pairs={{0,32},{32,64},{64,96},{96,128},{128,160},{160,192},{192,224},{224... | collective-permute-start | bytes 589832 | tf_op jit(solution)/shard_map/ppermute | solution.py:198
  21.9 7.4 %collective-permute-start.8 = (bf16[48,2048]{1,0:T(8,128)(2,1)S(1)}, bf16[48,2048]{1,0:T(8,128)(2,1)S(1)}, u32[]{:S(2)}, u32[]{:S(2)}) collective-permute-start(bf16[48,2048]{1,0:T(8,128)(2,1)S(1)} %collective-permute-done.4.refs_6_), channel_id=1, source_target_pairs={{0,32},{32,64},{64,96},{96,128},{128,160},{160,192},{192,224},{224... | collective-permute-start | bytes 589832 | tf_op jit(solution)/shard_map/ppermute | solution.py:197
  21.9 7.5 %collective-permute-start.11 = (bf16[48,2048]{1,0:T(8,128)(2,1)S(1)}, bf16[48,2048]{1,0:T(8,128)(2,1)S(1)}, u32[]{:S(2)}, u32[]{:S(2)}) collective-permute-start(bf16[48,2048]{1,0:T(8,128)(2,1)S(1)} %collective-permute-done.7.refs_9_), channel_id=1, source_target_pairs={{0,224},{32,0},{64,32},{96,64},{128,96},{160,128},{192,160},{224,1... | collective-permute-start | bytes 589832 | tf_op jit(solution)/shard_map/ppermute | solution.py:200
  25.5 7.8 %collective-permute-start.10 = (bf16[48,2048]{1,0:T(8,128)(2,1)S(1)}, bf16[48,2048]{1,0:T(8,128)(2,1)S(1)}, u32[]{:S(2)}, u32[]{:S(2)}) collective-permute-start(bf16[48,2048]{1,0:T(8,128)(2,1)S(1)} %collective-permute-done.6.refs_8_), channel_id=1, source_target_pairs={{0,224},{32,0},{64,32},{96,64},{128,96},{160,128},{192,160},{224,1... | collective-permute-start | bytes 589832 | tf_op jit(solution)/shard_map/ppermute | solution.py:199
  28.6 5.7 %collective-permute-start.9 = (bf16[48,2048]{1,0:T(8,128)(2,1)S(1)}, bf16[48,2048]{1,0:T(8,128)(2,1)S(1)}, u32[]{:S(2)}, u32[]{:S(2)}) collective-permute-start(bf16[48,2048]{1,0:T(8,128)(2,1)S(1)} %collective-permute-done.5.refs_7_), channel_id=1, source_target_pairs={{0,32},{32,64},{64,96},{96,128},{128,160},{160,192},{192,224},{224... | collective-permute-start | bytes 589832 | tf_op jit(solution)/shard_map/ppermute | solution.py:198
  29.3 8.7 %collective-permute-start.12 = (bf16[48,2048]{1,0:T(8,128)(2,1)S(1)}, bf16[48,2048]{1,0:T(8,128)(2,1)S(1)}, u32[]{:S(2)}, u32[]{:S(2)}) collective-permute-start(bf16[48,2048]{1,0:T(8,128)(2,1)S(1)} %collective-permute-done.8.refs_10_), channel_id=1, source_target_pairs={{0,32},{32,64},{64,96},{96,128},{128,160},{160,192},{192,224},{224... | collective-permute-start | bytes 589832 | tf_op jit(solution)/shard_map/ppermute | solution.py:204
  29.4 8.6 %collective-permute-start.13 = (bf16[48,2048]{1,0:T(8,128)(2,1)S(1)}, bf16[48,2048]{1,0:T(8,128)(2,1)S(1)}, u32[]{:S(2)}, u32[]{:S(2)}) collective-permute-start(bf16[48,2048]{1,0:T(8,128)(2,1)S(1)} %collective-permute-done.11.refs_13_), channel_id=1, source_target_pairs={{0,224},{32,0},{64,32},{96,64},{128,96},{160,128},{192,160},{224,1... | collective-permute-start | bytes 589832 | tf_op jit(solution)/shard_map/ppermute | solution.py:204
  38.0 8.8 %collective-permute-start.15 = (f32[14,96,128]{2,1,0:T(8,128)S(1)}, f32[14,96,128]{2,1,0:T(8,128)S(1)}, u32[]{:S(2)}, u32[]{:S(2)}) collective-permute-start(f32[14,96,128]{2,1,0:T(8,128)S(1)} %get-tuple-element.29), channel_id=1, source_target_pairs={{0,1},{1,0},{2,3},{3,2},{4,5},{5,4},{6,7},{7,6},{8,9},{9,8},{10,11... | collective-permute-start | bytes 2064392 | tf_op jit(solution)/shard_map/ppermute | solution.py:208
  46.7 1.4 %collective-permute-start.14 = (f32[2,96,128]{2,1,0:T(8,128)S(1)}, f32[2,96,128]{2,1,0:T(8,128)S(1)}, u32[]{:S(2)}, u32[]{:S(2)}) collective-permute-start(f32[2,96,128]{2,1,0:T(8,128)S(1)} %get-tuple-element.27), channel_id=1, source_target_pairs={{0,1},{1,0},{2,3},{3,2},{4,5},{5,4},{6,7},{7,6},{8,9},{9,8},{10,11... | collective-permute-start | bytes 294920 | tf_op jit(solution)/shard_map/ppermute | solution.py:210

commit v8 on v5

--- a/solution.py
+++ b/solution.py
@@ -25,35 +25,29 @@
     return picked
 
 
-def mask_kernel(cd1, cd2, ab1, ab2, occ1, occ2, irrep, virt, energy, values, masked, virt_out, occ_out, arrived):
+def fetch(values, masked, arrived, first):
     blocks = arrived.shape[0]
-    size = values.shape[0] // blocks
+    size = masked.shape[0] // blocks
     copies = []
     for block in range(blocks):
-        down = pl.ds(block * size, size)
         copies.append(
-            pltpu.make_async_copy(values.at[down, :], masked.at[down, :], arrived.at[block])
+            pltpu.make_async_copy(
+                values.at[pl.ds(first + block * size, size), :],
+                masked.at[pl.ds(block * size, size), :],
+                arrived.at[block],
+            )
         )
         copies[-1].start()
-
-    virt_out[...] = lookup(virt, ab1[...]) + lookup(virt, ab2[...])
-    for row in range(occ1.shape[0]):
-        both = energy[occ1[row]] + energy[occ2[row]]
-        occ_out[row : row + 1, :] = jnp.full((1, LANES), both, jnp.float32)
-    label = lookup(irrep, ab1[...]) ^ lookup(irrep, ab2[...])
-    other = label.astype(jnp.float32).astype(jnp.bfloat16)
-    other = [jnp.broadcast_to(other[i : i + 1, :], (LANES, LANES)) for i in range(ab1.shape[0])]
-    labels = []
-    for tile in range(cd1.shape[0] // 8):
-        part = slice(8 * tile, 8 * tile + 8)
-        label = lookup(irrep, cd1[part, :]) ^ lookup(irrep, cd2[part, :])
-        labels.append(label.astype(jnp.float32))
-
-    for block in range(blocks):
-        copies[block].wait()
+    return copies
+
+
+def apply_mask(copies, masked, lines, other):
+    size = masked.shape[0] // len(copies)
+    other = [jnp.broadcast_to(other[i : i + 1, :], (LANES, LANES)) for i in range(other.shape[0])]
+    for block, copy in enumerate(copies):
+        copy.wait()
         for part in range(block * size // LANES, (block + 1) * size // LANES):
-            line = labels[part // 8][part % 8 : part % 8 + 1, :]
-            label = jnp.broadcast_to(line, (LANES, LANES)).T.astype(jnp.bfloat16)
+            label = jnp.broadcast_to(lines(part), (LANES, LANES)).T.astype(jnp.bfloat16)
             down = slice(part * LANES, part * LANES + LANES)
             for lane in range(masked.shape[1] // LANES):
                 across = slice(lane * LANES, lane * LANES + LANES)
@@ -61,6 +55,33 @@
                 masked[down, across] = jnp.where(
                     label == other[lane], piece, jnp.zeros_like(piece)
                 )
+
+
+def low_kernel(cd1, cd2, ab1, ab2, occ1, occ2, irrep, virt, energy, values, masked, cd_out, ab_out, virt_out, occ_out, arrived):
+    copies = fetch(values, masked, arrived, 0)
+    label = lookup(irrep, ab1[...]) ^ lookup(irrep, ab2[...])
+    other = label.astype(jnp.float32)
+    ab_out[...] = other
+    labels = []
+    for tile in range(cd1.shape[0] // 8):
+        part = slice(8 * tile, 8 * tile + 8)
+        label = lookup(irrep, cd1[part, :]) ^ lookup(irrep, cd2[part, :])
+        labels.append(label.astype(jnp.float32))
+    for tile in range(len(labels) // 2):
+        cd_out[8 * tile : 8 * tile + 8, :] = labels[len(labels) // 2 + tile]
+    virt_out[...] = lookup(virt, ab1[...]) + lookup(virt, ab2[...])
+    for row in range(occ1.shape[0]):
+        both = energy[occ1[row]] + energy[occ2[row]]
+        occ_out[row : row + 1, :] = jnp.full((1, LANES), both, jnp.float32)
+    lines = lambda part: labels[part // 8][part % 8 : part % 8 + 1, :]
+    apply_mask(copies, masked, lines, other.astype(jnp.bfloat16))
+
+
+def high_kernel(cd, ab, values, after1, after2, masked, ready, arrived):
+    copies = fetch(values, masked, arrived, masked.shape[0])
+    ready[...] = ab[...]
+    lines = lambda part: cd[part : part + 1, :]
+    apply_mask(copies, masked, lines, ab[...].astype(jnp.bfloat16))
 
 
 def spread(where, total, place, rows, keep, send):
@@ -78,22 +99,20 @@
             send[2 * place + high, down, :] = sent[:, across]
 
 
-def first_kernel(where, ready, masked, *refs):
+def first_kernel(where, ready, low, high, *refs):
     pieces = refs[:14]
     keep, send, total = refs[14:]
-    half = masked.shape[0] // 2
     left = jnp.concatenate([piece[...] for piece in pieces[0::2]], axis=0)
     right = jnp.concatenate([piece[...] for piece in pieces[1::2]], axis=0)
-    total[...] = jnp.dot(left, masked[:half, :], preferred_element_type=jnp.float32)
-    total[...] += jnp.dot(right, masked[half:, :], preferred_element_type=jnp.float32)
+    total[...] = jnp.dot(left, low[...], preferred_element_type=jnp.float32)
+    total[...] += jnp.dot(right, high[...], preferred_element_type=jnp.float32)
     for place in range(7):
         spread(where, total, place, pieces[0].shape[0] // 4, keep, send)
 
 
-def last_kernel(where, masked, left, right, keep, send, total):
-    half = left.shape[1]
-    total[...] = jnp.dot(left[...], masked[:half, :], preferred_element_type=jnp.float32)
-    total[...] += jnp.dot(right[...], masked[half:, :], preferred_element_type=jnp.float32)
+def last_kernel(where, low, high, left, right, keep, send, total):
+    total[...] = jnp.dot(left[...], low[...], preferred_element_type=jnp.float32)
+    total[...] += jnp.dot(right[...], high[...], preferred_element_type=jnp.float32)
     spread(where, total, 0, left.shape[0] // 4, keep, send)
 
 
@@ -135,23 +154,27 @@
     vmem = pl.BlockSpec(memory_space=pltpu.VMEM)
     smem = pl.BlockSpec(memory_space=pltpu.SMEM)
     square = lambda x: x.reshape(x.shape[0] // LANES, LANES)
-    masked, virt, occ = pl.pallas_call(
-        mask_kernel,
+    tables = [pltpu.with_memory_space_constraint(x, pltpu.HBM) for x in (
+        square(cd1), square(cd2), square(ab1), square(ab2), occ1, occ2,
+        irrep, virt_energy, occ_energy, integrals,
+    )]
+    half = pltpu.VMEM((depth // 2, width), jnp.bfloat16)
+    lines = pltpu.VMEM((width // LANES, LANES), jnp.float32)
+    hbm = pl.BlockSpec(memory_space=pl.ANY)
+    low, cd, ab, virt, occ = pl.pallas_call(
+        low_kernel,
         out_shape=(
-            pltpu.VMEM((depth, width), jnp.bfloat16),
-            pltpu.VMEM((width // LANES, LANES), jnp.float32),
+            half,
+            pltpu.VMEM((depth // LANES // 2, LANES), jnp.float32),
+            lines,
+            lines,
             pltpu.VMEM((16, LANES), jnp.float32),
         ),
-        in_specs=[vmem] * 4 + [smem] * 2 + [vmem] * 2 + [smem, pl.BlockSpec(memory_space=pl.ANY)],
-        out_specs=(vmem,) * 3,
-        scratch_shapes=[pltpu.SemaphoreType.DMA((8,))],
+        in_specs=[vmem] * 4 + [smem] * 2 + [vmem] * 2 + [smem, hbm],
+        out_specs=(vmem,) * 5,
+        scratch_shapes=[pltpu.SemaphoreType.DMA((4,))],
         compiler_params=pltpu.CompilerParams(vmem_limit_bytes=4 * MIB),
-    )(
-        *[pltpu.with_memory_space_constraint(x, pltpu.HBM) for x in (
-            square(cd1), square(cd2), square(ab1), square(ab2), occ1, occ2,
-            irrep, virt_energy, occ_energy, integrals,
-        )]
-    )
+    )(*tables)
 
     where = jnp.stack([lax.axis_index("z"), lax.axis_index("core")]).astype(jnp.int32)
     forward = [(i, (i + 1) % 8) for i in range(8)]
@@ -165,7 +188,17 @@
         down[0] = lax.ppermute(down[0], "z", backward)
         down[1] = lax.ppermute(down[1], "z", backward)
         if hop == 0:
-            up[0], ready, where = lax.optimization_barrier((up[0], virt, where))
+            up[0], cd, where = lax.optimization_barrier((up[0], cd, where))
+            high, ready = pl.pallas_call(
+                high_kernel,
+                out_shape=(half, lines),
+                in_specs=[vmem, vmem, hbm, hbm, hbm],
+                out_specs=(vmem, vmem),
+                scratch_shapes=[pltpu.SemaphoreType.DMA((4,))],
+                compiler_params=pltpu.CompilerParams(vmem_limit_bytes=4 * MIB),
+            )(cd, ab, tables[-1], up[1], down[0])
+        if hop == 1:
+            up[0], ready = lax.optimization_barrier((up[0], ready))
         pieces += up + down
     last = [lax.ppermute(up[0], "z", forward), lax.ppermute(down[1], "z", backward)]
     size = rows * width // LANES
@@ -177,12 +210,12 @@
         grid_spec=pltpu.PrefetchScalarGridSpec(
             num_scalar_prefetch=1,
             grid=(),
-            in_specs=[vmem] * 16,
+            in_specs=[vmem] * 17,
             out_specs=(vmem, vmem),
             scratch_shapes=[pltpu.VMEM((7 * amps.shape[0], width), jnp.float32)],
         ),
         compiler_params=pltpu.CompilerParams(vmem_limit_bytes=8 * MIB),
-    )(where, ready, masked, *pieces)
+    )(where, ready, low, high, *pieces)
     swap = [(0, 1), (1, 0)]
     send, *last = lax.optimization_barrier((send, *last))
     got = lax.ppermute(send, "core", swap)
@@ -192,12 +225,12 @@
         grid_spec=pltpu.PrefetchScalarGridSpec(
             num_scalar_prefetch=1,
             grid=(),
-            in_specs=[vmem] * 3,
+            in_specs=[vmem] * 4,
             out_specs=(vmem, vmem),
             scratch_shapes=[pltpu.VMEM((amps.shape[0], width), jnp.float32)],
         ),
         compiler_params=pltpu.CompilerParams(vmem_limit_bytes=8 * MIB),
-    )(where, masked, *last)
+    )(where, low, high, *last)
     last_got = lax.ppermute(last_send, "core", swap)
     packed = pl.pallas_call(
         pack_kernel,

time: 64.4 us -> 63.8 us (level)
  waiting for transfers between devices: 6.68 us -> 4.84 us
  Pallas kernels: 11.9 us -> 13.1 us
    pallas_call x1 -> x2, Pallas kernels: 4.6 us -> 5.82 us  [the longest x1 3.33 us: on_device(): pl.pallas_call(low_kernel, out_shape=(half, pltpu.VMEM((depth // LANES //...]
    ppermute x3, waiting for transfers between devices: 0.91 us -> 0.01 us  [on_device(): down[0] = lax.ppermute(down[0], 'z', backward)]
    ppermute x1, starting transfers between devices: 5.8 us -> 5 us  [on_device(): got = lax.ppermute(send, 'core', swap)]
    ppermute x3, starting transfers between devices: 7.05 us -> 7.77 us  [on_device(): down[0] = lax.ppermute(down[0], 'z', backward)]
  transfers between devices with their start and end apart: 16 -> 16, of which waited for: 5 -> 3; matrix products, arithmetic and copies ran while one was open for 0% -> 0% of each run, Pallas kernels for 16% -> 18%
where the time goes in v8:
time: 63.8 us; the launch traced here: 63.6 us
  starting transfers between devices  27.7 us (43%)
  blocking collectives  16.7 us (26%)
  Pallas kernels  13.1 us (21%)
  waiting for transfers between devices  4.84 us (8%)
  local copies, waits for them, and re-layouts  1.05 us (2%)
    all_to_all x1, blocking collectives, on_device(): parts = lax.all_to_all(packed, ('y', 'x'), 0, 0, tiled=True)  16.7 us
    ppermute x3, starting transfers between devices, on_device(): down[1] = lax.ppermute(down[1], 'z', backward)  9.43 us
    ppermute x3, starting transfers between devices, on_device(): down[0] = lax.ppermute(down[0], 'z', backward)  7.77 us
    ppermute x1, starting transfers between devices, on_device(): got = lax.ppermute(send, 'core', swap)  5 us
    pallas_call x1, Pallas kernels, on_device(): pl.pallas_call(first_kernel, out_shape=(first, first), grid_spec=pltpu.Pr...  3.66 us
    pallas_call x1, Pallas kernels, on_device(): pl.pallas_call(low_kernel, out_shape=(half, pltpu.VMEM((depth // LANES //...  3.33 us
    ppermute x3, starting transfers between devices, on_device(): up[0] = lax.ppermute(up[0], 'z', forward)  2.71 us
    ppermute x1, starting transfers between devices, on_device(): lax.ppermute(down[1], 'z', backward)  2.67 us
  transfers between devices with their start and end apart: 16, of which 3 were waited for; matrix products, arithmetic and copies ran while one was open for 0% of the time, Pallas kernels for 18%

profile of v8, /device:TPU:1, one launch (start us, length us, event | category | flops | bytes accessed | tf_op | source)
XLA Modules:
  0.0 63.6 jit_solution(5621942589446793662)
XLA Ops:
  0.0 1.0 %fusion = (bf16[48,2048]{1,0:T(8,128)(2,1)S(1)}, bf16[48,2048]{1,0:T(8,128)(2,1)S(1)}) fusion(bf16[48,4096]{1,0:T(8,128)(2,1)} %param.11), kind=kLoop, calls=%fused_computation.1 | loop fusion | bytes 786432 | tf_op jit(solution)/shard_map/slice | solution.py:182
  1.1 2.5 %collective-permute-start = (bf16[48,2048]{1,0:T(8,128)(2,1)S(1)}, bf16[48,2048]{1,0:T(8,128)(2,1)S(1)}, u32[]{:S(2)}, u32[]{:S(2)}) collective-permute-start(bf16[48,2048]{1,0:T(8,128)(2,1)S(1)} %get-tuple-element.44.refs_0_), channel_id=1, source_target_pairs={{0,32},{32,64},{64,96},{96,128},{128,160},{160,192},{192,224},{224... | collective-permute-start | bytes 589832 | tf_op jit(solution)/shard_map/ppermute | solution.py:186
  3.6 4.0 %collective-permute-start.4 = (bf16[48,2048]{1,0:T(8,128)(2,1)S(1)}, bf16[48,2048]{1,0:T(8,128)(2,1)S(1)}, u32[]{:S(2)}, u32[]{:S(2)}) collective-permute-start(bf16[48,2048]{1,0:T(8,128)(2,1)S(1)} %get-tuple-element.43.refs_1_), channel_id=1, source_target_pairs={{0,224},{32,0},{64,32},{96,64},{128,96},{160,128},{192,160},{224,1... | collective-permute-start | bytes 589832 | tf_op jit(solution)/shard_map/ppermute | solution.py:189
  7.6 2.7 %collective-permute-start.3 = (bf16[48,2048]{1,0:T(8,128)(2,1)S(1)}, bf16[48,2048]{1,0:T(8,128)(2,1)S(1)}, u32[]{:S(2)}, u32[]{:S(2)}) collective-permute-start(bf16[48,2048]{1,0:T(8,128)(2,1)S(1)} %get-tuple-element.44.refs_0_), channel_id=1, source_target_pairs={{0,224},{32,0},{64,32},{96,64},{128,96},{160,128},{192,160},{224,1... | collective-permute-start | bytes 589832 | tf_op jit(solution)/shard_map/ppermute | solution.py:188
  10.3 0.1 pad_add_fusion.where
  10.4 3.3 %shard_map.109 = (bf16[2048,1024]{1,0:T(8,128)(2,1)S(1)}, f32[16,128]{1,0:T(8,128)S(1)}, f32[8,128]{1,0:T(8,128)S(1)}, f32[8,128]{1,0:T(8,128)S(1)}, f32[16,128]{1,0:T(8,128)S(1)}) custom-call(s32[32,128]{1,0:T(8,128)} %bitcast.6, s32[32,128]{1,0:T(8,128)} %bitcast.7, s32[8,128]{1,0:T(8,128)} %bitcast.8, s32[8,128]{1,0:T(8,128)} %bitcast.9, s32[12]{0:T(128)} %occ1.1, ...), custom_call_target="tpu_custom_call" | custom-call | tf_op jit(solution)/shard_map/pallas_call | solution.py:164
  13.7 0.1 collective-permute-start.1
  13.8 2.7 %collective-permute-start.7 = (bf16[48,2048]{1,0:T(8,128)(2,1)S(1)}, bf16[48,2048]{1,0:T(8,128)(2,1)S(1)}, u32[]{:S(2)}, u32[]{:S(2)}) collective-permute-start(bf16[48,2048]{1,0:T(8,128)(2,1)S(1)} %collective-permute-done.4.refs_5_), channel_id=1, source_target_pairs={{0,224},{32,0},{64,32},{96,64},{128,96},{160,128},{192,160},{224,1... | collective-permute-start | bytes 589832 | tf_op jit(solution)/shard_map/ppermute | solution.py:189
  16.5 2.3 %collective-permute-start.6 = (bf16[48,2048]{1,0:T(8,128)(2,1)S(1)}, bf16[48,2048]{1,0:T(8,128)(2,1)S(1)}, u32[]{:S(2)}, u32[]{:S(2)}) collective-permute-start(bf16[48,2048]{1,0:T(8,128)(2,1)S(1)} %collective-permute-done.3.after2.refs_4_), channel_id=1, source_target_pairs={{0,224},{32,0},{64,32},{96,64},{128,96},{160,128},{192,160},{224,1... | collective-permute-start | bytes 589832 | tf_op jit(solution)/shard_map/ppermute | solution.py:188
  18.8 2.5 %shard_map.110 = (bf16[2048,1024]{1,0:T(8,128)(2,1)S(1)}, f32[8,128]{1,0:T(8,128)S(1)}) custom-call(f32[16,128]{1,0:T(8,128)S(1)} %get-tuple-element.27.cd, f32[8,128]{1,0:T(8,128)S(1)} %get-tuple-element.28.ab, bf16[4096,1024]{1,0:T(8,128)(2,1)} %values.3, bf16[48,2048]{1,0:T(8,128)(2,1)S(1)} %collective-permute-done.2.after1.refs_3_, ...), custom_call_target="tpu_custom_call" | custom-call | tf_op jit(solution)/shard_map/pallas_call | solution.py:192
  21.3 0.1 collective-permute-start.8
  21.4 2.7 %collective-permute-start.11 = (bf16[48,2048]{1,0:T(8,128)(2,1)S(1)}, bf16[48,2048]{1,0:T(8,128)(2,1)S(1)}, u32[]{:S(2)}, u32[]{:S(2)}) collective-permute-start(bf16[48,2048]{1,0:T(8,128)(2,1)S(1)} %collective-permute-done.7.refs_9_), channel_id=1, source_target_pairs={{0,224},{32,0},{64,32},{96,64},{128,96},{160,128},{192,160},{224,1... | collective-permute-start | bytes 589832 | tf_op jit(solution)/shard_map/ppermute | solution.py:189
  24.2 2.8 %collective-permute-start.10 = (bf16[48,2048]{1,0:T(8,128)(2,1)S(1)}, bf16[48,2048]{1,0:T(8,128)(2,1)S(1)}, u32[]{:S(2)}, u32[]{:S(2)}) collective-permute-start(bf16[48,2048]{1,0:T(8,128)(2,1)S(1)} %collective-permute-done.6.refs_8_), channel_id=1, source_target_pairs={{0,224},{32,0},{64,32},{96,64},{128,96},{160,128},{192,160},{224,1... | collective-permute-start | bytes 589832 | tf_op jit(solution)/shard_map/ppermute | solution.py:188
  27.0 2.6 %collective-permute-done.8.refs_10_ = bf16[48,2048]{1,0:T(8,128)(2,1)S(1)} collective-permute-done((bf16[48,2048]{1,0:T(8,128)(2,1)S(1)}, bf16[48,2048]{1,0:T(8,128)(2,1)S(1)}, u32[]{:S(2)}, u32[]{:S(2)}) %collective-permute-start.8) | collective-permute-done | bytes 196640 | tf_op jit(solution)/shard_map/ppermute | solution.py:186
  29.5 2.7 %collective-permute-start.13 = (bf16[48,2048]{1,0:T(8,128)(2,1)S(1)}, bf16[48,2048]{1,0:T(8,128)(2,1)S(1)}, u32[]{:S(2)}, u32[]{:S(2)}) collective-permute-start(bf16[48,2048]{1,0:T(8,128)(2,1)S(1)} %collective-permute-done.11.refs_13_), channel_id=1, source_target_pairs={{0,224},{32,0},{64,32},{96,64},{128,96},{160,128},{192,160},{224,1... | collective-permute-start | bytes 589832 | tf_op jit(solution)/shard_map/ppermute | solution.py:203
  32.2 0.9 %collective-permute-done.9.refs_11_ = bf16[48,2048]{1,0:T(8,128)(2,1)S(1)} collective-permute-done((bf16[48,2048]{1,0:T(8,128)(2,1)S(1)}, bf16[48,2048]{1,0:T(8,128)(2,1)S(1)}, u32[]{:S(2)}, u32[]{:S(2)}) %collective-permute-start.9) | collective-permute-done | bytes 196640 | tf_op jit(solution)/shard_map/ppermute | solution.py:187
  33.2 3.7 %shard_map.111 = (f32[14,96,128]{2,1,0:T(8,128)S(1)}, f32[14,96,128]{2,1,0:T(8,128)S(1)}) custom-call(s32[2]{0:T(128)S(1)} %pad_add_fusion.where, f32[8,128]{1,0:T(8,128)S(1)} %get-tuple-element.30.ready, bf16[2048,1024]{1,0:T(8,128)(2,1)S(1)} %get-tuple-element.31.low, bf16[2048,1024]{1,0:T(8,128)(2,1)S(1)} %get-tuple-element.32.high, ...), custom_call_target="tpu_custom_call" | custom-call | tf_op jit(solution)/shard_map/pallas_call | solution.py:207
  36.8 5.0 %collective-permute-start.14 = (f32[14,96,128]{2,1,0:T(8,128)S(1)}, f32[14,96,128]{2,1,0:T(8,128)S(1)}, u32[]{:S(2)}, u32[]{:S(2)}) collective-permute-start(f32[14,96,128]{2,1,0:T(8,128)S(1)} %get-tuple-element.36), channel_id=1, source_target_pairs={{0,1},{1,0},{2,3},{3,2},{4,5},{5,4},{6,7},{7,6},{8,9},{9,8},{10,11... | collective-permute-start | bytes 2064392 | tf_op jit(solution)/shard_map/ppermute | solution.py:221
  41.8 2.1 %shard_map.112 = (f32[2,96,128]{2,1,0:T(8,128)S(1)}, f32[2,96,128]{2,1,0:T(8,128)S(1)}) custom-call(s32[2]{0:T(128)S(1)} %pad_add_fusion.where, bf16[2048,1024]{1,0:T(8,128)(2,1)S(1)} %get-tuple-element.31.low, bf16[2048,1024]{1,0:T(8,128)(2,1)S(1)} %get-tuple-element.32.high, bf16[48,2048]{1,0:T(8,128)(2,1)S(1)} %collective-permute-done.12.left, ...), custom_call_target="tpu_custom_call" | custom-call | tf_op jit(solution)/shard_map/pallas_call | solution.py:222
  44.0 0.1 collective-permute-start.15
  44.1 1.3 %collective-permute-done.15.last_got = f32[2,96,128]{2,1,0:T(8,128)S(1)} collective-permute-done((f32[2,96,128]{2,1,0:T(8,128)S(1)}, f32[2,96,128]{2,1,0:T(8,128)S(1)}, u32[]{:S(2)}, u32[]{:S(2)}) %collective-permute-start.15) | collective-permute-done | bytes 98336 | tf_op jit(solution)/shard_map/ppermute | solution.py:234
  45.4 0.8 %shard_map.113 = s16[16,112,128]{2,1,0:T(8,128)(2,1)S(1)} custom-call(s32[2]{0:T(128)S(1)} %pad_add_fusion.where, f32[14,96,128]{2,1,0:T(8,128)S(1)} %get-tuple-element.34.keep, f32[14,96,128]{2,1,0:T(8,128)S(1)} %collective-permute-done.14.got, f32[2,96,128]{2,1,0:T(8,128)S(1)} %get-tuple-element.39.last_keep, ...), custom_call_target="tpu_custom_call" | custom-call | tf_op jit(solution)/shard_map/pallas_call | solution.py:235
  46.1 16.7 %all_to_all.5.parts = s16[16,112,128]{2,1,0:T(8,128)(2,1)S(1)} all-to-all(s16[16,112,128]{2,1,0:T(8,128)(2,1)S(1)} %shard_map.113), channel_id=1, replica_groups=mesh['z'=8,'y'=4,'x'=4,'core'=2] {'y','x'}, dimensions={0} | all-to-all | bytes 917504 | tf_op jit(solution)/shard_map/all_to_all | solution.py:243
  62.9 0.8 %shard_map.114 = f32[12,1024]{1,0:T(8,128)} custom-call(s16[16,112,128]{2,1,0:T(8,128)(2,1)S(1)} %all_to_all.5.parts, f32[8,128]{1,0:T(8,128)S(1)} %get-tuple-element.41.virt, f32[16,128]{1,0:T(8,128)S(1)} %get-tuple-element.42.occ), custom_call_target="tpu_custom_call" | custom-call | tf_op jit(solution)/shard_map/pallas_call | solution.py:244
  (17 shorter events, 0.0 us)
Async XLA Ops:
  1.1 12.7 %collective-permute-start = (bf16[48,2048]{1,0:T(8,128)(2,1)S(1)}, bf16[48,2048]{1,0:T(8,128)(2,1)S(1)}, u32[]{:S(2)}, u32[]{:S(2)}) collective-permute-start(bf16[48,2048]{1,0:T(8,128)(2,1)S(1)} %get-tuple-element.44.refs_0_), channel_id=1, source_target_pairs={{0,32},{32,64},{64,96},{96,128},{128,160},{160,192},{192,224},{224... | collective-permute-start | bytes 589832 | tf_op jit(solution)/shard_map/ppermute | solution.py:186
  3.6 10.2 %collective-permute-start.4 = (bf16[48,2048]{1,0:T(8,128)(2,1)S(1)}, bf16[48,2048]{1,0:T(8,128)(2,1)S(1)}, u32[]{:S(2)}, u32[]{:S(2)}) collective-permute-start(bf16[48,2048]{1,0:T(8,128)(2,1)S(1)} %get-tuple-element.43.refs_1_), channel_id=1, source_target_pairs={{0,224},{32,0},{64,32},{96,64},{128,96},{160,128},{192,160},{224,1... | collective-permute-start | bytes 589832 | tf_op jit(solution)/shard_map/ppermute | solution.py:189
  7.6 11.2 %collective-permute-start.2 = (bf16[48,2048]{1,0:T(8,128)(2,1)S(1)}, bf16[48,2048]{1,0:T(8,128)(2,1)S(1)}, u32[]{:S(2)}, u32[]{:S(2)}) collective-permute-start(bf16[48,2048]{1,0:T(8,128)(2,1)S(1)} %get-tuple-element.43.refs_1_), channel_id=1, source_target_pairs={{0,32},{32,64},{64,96},{96,128},{128,160},{160,192},{192,224},{224... | collective-permute-start | bytes 589832 | tf_op jit(solution)/shard_map/ppermute | solution.py:187
  7.6 8.9 %collective-permute-start.3 = (bf16[48,2048]{1,0:T(8,128)(2,1)S(1)}, bf16[48,2048]{1,0:T(8,128)(2,1)S(1)}, u32[]{:S(2)}, u32[]{:S(2)}) collective-permute-start(bf16[48,2048]{1,0:T(8,128)(2,1)S(1)} %get-tuple-element.44.refs_0_), channel_id=1, source_target_pairs={{0,224},{32,0},{64,32},{96,64},{128,96},{160,128},{192,160},{224,1... | collective-permute-start | bytes 589832 | tf_op jit(solution)/shard_map/ppermute | solution.py:188
  13.7 7.6 %collective-permute-start.1 = (bf16[48,2048]{1,0:T(8,128)(2,1)S(1)}, bf16[48,2048]{1,0:T(8,128)(2,1)S(1)}, u32[]{:S(2)}, u32[]{:S(2)}) collective-permute-start(bf16[48,2048]{1,0:T(8,128)(2,1)S(1)} %collective-permute-done.refs_2_), channel_id=1, source_target_pairs={{0,32},{32,64},{64,96},{96,128},{128,160},{160,192},{192,224},{224... | collective-permute-start | bytes 589832 | tf_op jit(solution)/shard_map/ppermute | solution.py:186
  13.8 7.6 %collective-permute-start.7 = (bf16[48,2048]{1,0:T(8,128)(2,1)S(1)}, bf16[48,2048]{1,0:T(8,128)(2,1)S(1)}, u32[]{:S(2)}, u32[]{:S(2)}) collective-permute-start(bf16[48,2048]{1,0:T(8,128)(2,1)S(1)} %collective-permute-done.4.refs_5_), channel_id=1, source_target_pairs={{0,224},{32,0},{64,32},{96,64},{128,96},{160,128},{192,160},{224,1... | collective-permute-start | bytes 589832 | tf_op jit(solution)/shard_map/ppermute | solution.py:189
  16.5 7.7 %collective-permute-start.6 = (bf16[48,2048]{1,0:T(8,128)(2,1)S(1)}, bf16[48,2048]{1,0:T(8,128)(2,1)S(1)}, u32[]{:S(2)}, u32[]{:S(2)}) collective-permute-start(bf16[48,2048]{1,0:T(8,128)(2,1)S(1)} %collective-permute-done.3.after2.refs_4_), channel_id=1, source_target_pairs={{0,224},{32,0},{64,32},{96,64},{128,96},{160,128},{192,160},{224,1... | collective-permute-start | bytes 589832 | tf_op jit(solution)/shard_map/ppermute | solution.py:188
  18.8 8.1 %collective-permute-start.5 = (bf16[48,2048]{1,0:T(8,128)(2,1)S(1)}, bf16[48,2048]{1,0:T(8,128)(2,1)S(1)}, u32[]{:S(2)}, u32[]{:S(2)}) collective-permute-start(bf16[48,2048]{1,0:T(8,128)(2,1)S(1)} %collective-permute-done.2.after1.refs_3_), channel_id=1, source_target_pairs={{0,32},{32,64},{64,96},{96,128},{128,160},{160,192},{192,224},{224... | collective-permute-start | bytes 589832 | tf_op jit(solution)/shard_map/ppermute | solution.py:187
  21.3 8.2 %collective-permute-start.8 = (bf16[48,2048]{1,0:T(8,128)(2,1)S(1)}, bf16[48,2048]{1,0:T(8,128)(2,1)S(1)}, u32[]{:S(2)}, u32[]{:S(2)}) collective-permute-start(bf16[48,2048]{1,0:T(8,128)(2,1)S(1)} %collective-permute-done.1.refs_6_), channel_id=1, source_target_pairs={{0,32},{32,64},{64,96},{96,128},{128,160},{160,192},{192,224},{224... | collective-permute-start | bytes 589832 | tf_op jit(solution)/shard_map/ppermute | solution.py:186
  21.4 8.1 %collective-permute-start.11 = (bf16[48,2048]{1,0:T(8,128)(2,1)S(1)}, bf16[48,2048]{1,0:T(8,128)(2,1)S(1)}, u32[]{:S(2)}, u32[]{:S(2)}) collective-permute-start(bf16[48,2048]{1,0:T(8,128)(2,1)S(1)} %collective-permute-done.7.refs_9_), channel_id=1, source_target_pairs={{0,224},{32,0},{64,32},{96,64},{128,96},{160,128},{192,160},{224,1... | collective-permute-start | bytes 589832 | tf_op jit(solution)/shard_map/ppermute | solution.py:189
  24.2 8.0 %collective-permute-start.10 = (bf16[48,2048]{1,0:T(8,128)(2,1)S(1)}, bf16[48,2048]{1,0:T(8,128)(2,1)S(1)}, u32[]{:S(2)}, u32[]{:S(2)}) collective-permute-start(bf16[48,2048]{1,0:T(8,128)(2,1)S(1)} %collective-permute-done.6.refs_8_), channel_id=1, source_target_pairs={{0,224},{32,0},{64,32},{96,64},{128,96},{160,128},{192,160},{224,1... | collective-permute-start | bytes 589832 | tf_op jit(solution)/shard_map/ppermute | solution.py:188
  26.9 6.2 %collective-permute-start.9 = (bf16[48,2048]{1,0:T(8,128)(2,1)S(1)}, bf16[48,2048]{1,0:T(8,128)(2,1)S(1)}, u32[]{:S(2)}, u32[]{:S(2)}) collective-permute-start(bf16[48,2048]{1,0:T(8,128)(2,1)S(1)} %collective-permute-done.5.refs_7_), channel_id=1, source_target_pairs={{0,32},{32,64},{64,96},{96,128},{128,160},{160,192},{192,224},{224... | collective-permute-start | bytes 589832 | tf_op jit(solution)/shard_map/ppermute | solution.py:187
  29.5 7.3 %collective-permute-start.12 = (bf16[48,2048]{1,0:T(8,128)(2,1)S(1)}, bf16[48,2048]{1,0:T(8,128)(2,1)S(1)}, u32[]{:S(2)}, u32[]{:S(2)}) collective-permute-start(bf16[48,2048]{1,0:T(8,128)(2,1)S(1)} %collective-permute-done.8.refs_10_), channel_id=1, source_target_pairs={{0,32},{32,64},{64,96},{96,128},{128,160},{160,192},{192,224},{224... | collective-permute-start | bytes 589832 | tf_op jit(solution)/shard_map/ppermute | solution.py:203
  29.5 7.3 %collective-permute-start.13 = (bf16[48,2048]{1,0:T(8,128)(2,1)S(1)}, bf16[48,2048]{1,0:T(8,128)(2,1)S(1)}, u32[]{:S(2)}, u32[]{:S(2)}) collective-permute-start(bf16[48,2048]{1,0:T(8,128)(2,1)S(1)} %collective-permute-done.11.refs_13_), channel_id=1, source_target_pairs={{0,224},{32,0},{64,32},{96,64},{128,96},{160,128},{192,160},{224,1... | collective-permute-start | bytes 589832 | tf_op jit(solution)/shard_map/ppermute | solution.py:203
  36.8 8.5 %collective-permute-start.14 = (f32[14,96,128]{2,1,0:T(8,128)S(1)}, f32[14,96,128]{2,1,0:T(8,128)S(1)}, u32[]{:S(2)}, u32[]{:S(2)}) collective-permute-start(f32[14,96,128]{2,1,0:T(8,128)S(1)} %get-tuple-element.36), channel_id=1, source_target_pairs={{0,1},{1,0},{2,3},{3,2},{4,5},{5,4},{6,7},{7,6},{8,9},{9,8},{10,11... | collective-permute-start | bytes 2064392 | tf_op jit(solution)/shard_map/ppermute | solution.py:221
  44.0 1.4 %collective-permute-start.15 = (f32[2,96,128]{2,1,0:T(8,128)S(1)}, f32[2,96,128]{2,1,0:T(8,128)S(1)}, u32[]{:S(2)}, u32[]{:S(2)}) collective-permute-start(f32[2,96,128]{2,1,0:T(8,128)S(1)} %get-tuple-element.40), channel_id=1, source_target_pairs={{0,1},{1,0},{2,3},{3,2},{4,5},{5,4},{6,7},{7,6},{8,9},{9,8},{10,11... | collective-permute-start | bytes 294920 | tf_op jit(solution)/shard_map/ppermute | solution.py:234

commit v9 on v8

--- a/solution.py
+++ b/solution.py
@@ -6,7 +6,7 @@
 from jax.sharding import Mesh, PartitionSpec as P
 
 LANES = 128
-SHARDS = (0, -1, 1, -2, 2, -3, 3)
+SHARDS = (0, -1, 1, -2, 2, -3, 3, 4)
 MIB = 1024 * 1024
 
 
@@ -99,38 +99,53 @@
             send[2 * place + high, down, :] = sent[:, across]
 
 
-def first_kernel(where, ready, low, high, *refs):
-    pieces = refs[:14]
-    keep, send, total = refs[14:]
+def ladder_kernel(where, ready, low, high, after1, after2, *refs):
+    pieces = refs[:-3]
+    keep, send, total = refs[-3:]
     left = jnp.concatenate([piece[...] for piece in pieces[0::2]], axis=0)
     right = jnp.concatenate([piece[...] for piece in pieces[1::2]], axis=0)
     total[...] = jnp.dot(left, low[...], preferred_element_type=jnp.float32)
     total[...] += jnp.dot(right, high[...], preferred_element_type=jnp.float32)
-    for place in range(7):
+    for place in range(len(pieces) // 2):
         spread(where, total, place, pieces[0].shape[0] // 4, keep, send)
 
 
-def last_kernel(where, low, high, left, right, keep, send, total):
-    total[...] = jnp.dot(left[...], low[...], preferred_element_type=jnp.float32)
-    total[...] += jnp.dot(right[...], high[...], preferred_element_type=jnp.float32)
-    spread(where, total, 0, left.shape[0] // 4, keep, send)
-
-
-def pack_kernel(where, keep, got, last_keep, last_got, out):
-    rows = keep.shape[1]
-    for place, shift in enumerate(SHARDS + (4,)):
-        shard = lax.rem(where[0] + (shift + 8), 8)
-        for high in range(2):
-            if place < len(SHARDS):
-                both = keep[2 * place + high] + got[2 * place + high]
-            else:
-                both = last_keep[high] + last_got[high]
-            top = jnp.maximum(jnp.max(jnp.abs(both), axis=0, keepdims=True), 1e-30)
-            power = jnp.floor(14.99 - jnp.log2(top))
-            scaled = jnp.clip(jnp.round(both * jnp.exp2(power)), -32767.0, 32767.0)
-            out[2 * shard + high, :rows, :] = scaled.astype(jnp.int32).astype(jnp.int16)
-            power = jnp.broadcast_to(power, (out.shape[1] - rows, LANES))
-            out[2 * shard + high, rows:, :] = power.astype(jnp.int32).astype(jnp.int16)
+def ladder(where, ready, low, high, after, pieces):
+    vmem = pl.BlockSpec(memory_space=pltpu.VMEM)
+    hbm = pl.BlockSpec(memory_space=pl.ANY)
+    count = len(pieces) // 2
+    height, width = pieces[0].shape[0], low.shape[1]
+    block = pltpu.VMEM((2 * count, height * width // 4 // LANES, LANES), jnp.float32)
+    return pl.pallas_call(
+        ladder_kernel,
+        out_shape=(block, block),
+        grid_spec=pltpu.PrefetchScalarGridSpec(
+            num_scalar_prefetch=1,
+            grid=(),
+            in_specs=[vmem] * 3 + [hbm] * 2 + [vmem] * len(pieces),
+            out_specs=(vmem, vmem),
+            scratch_shapes=[pltpu.VMEM((count * height, width), jnp.float32)],
+        ),
+        compiler_params=pltpu.CompilerParams(vmem_limit_bytes=8 * MIB),
+    )(where, ready, low, high, *after, *pieces)
+
+
+def pack_kernel(where, *refs):
+    out = refs[-1]
+    kept, got = refs[: len(refs) // 2], refs[len(refs) // 2 : -1]
+    rows = kept[0].shape[1]
+    shifts = iter(SHARDS)
+    for mine, other in zip(kept, got):
+        for place in range(mine.shape[0] // 2):
+            shard = lax.rem(where[0] + (next(shifts) + 8), 8)
+            for high in range(2):
+                both = mine[2 * place + high] + other[2 * place + high]
+                top = jnp.maximum(jnp.max(jnp.abs(both), axis=0, keepdims=True), 1e-30)
+                power = jnp.floor(14.99 - jnp.log2(top))
+                scaled = jnp.clip(jnp.round(both * jnp.exp2(power)), -32767.0, 32767.0)
+                out[2 * shard + high, :rows, :] = scaled.astype(jnp.int32).astype(jnp.int16)
+                power = jnp.broadcast_to(power, (out.shape[1] - rows, LANES))
+                out[2 * shard + high, rows:, :] = power.astype(jnp.int32).astype(jnp.int16)
 
 
 def finish_kernel(parts, virt, occ, out):
@@ -201,45 +216,22 @@
             up[0], ready = lax.optimization_barrier((up[0], ready))
         pieces += up + down
     last = [lax.ppermute(up[0], "z", forward), lax.ppermute(down[1], "z", backward)]
-    size = rows * width // LANES
-    first = pltpu.VMEM((14, size, LANES), jnp.float32)
-    final = pltpu.VMEM((2, size, LANES), jnp.float32)
-    keep, send = pl.pallas_call(
-        first_kernel,
-        out_shape=(first, first),
-        grid_spec=pltpu.PrefetchScalarGridSpec(
-            num_scalar_prefetch=1,
-            grid=(),
-            in_specs=[vmem] * 17,
-            out_specs=(vmem, vmem),
-            scratch_shapes=[pltpu.VMEM((7 * amps.shape[0], width), jnp.float32)],
-        ),
-        compiler_params=pltpu.CompilerParams(vmem_limit_bytes=8 * MIB),
-    )(where, ready, low, high, *pieces)
     swap = [(0, 1), (1, 0)]
-    send, *last = lax.optimization_barrier((send, *last))
-    got = lax.ppermute(send, "core", swap)
-    last_keep, last_send = pl.pallas_call(
-        last_kernel,
-        out_shape=(final, final),
-        grid_spec=pltpu.PrefetchScalarGridSpec(
-            num_scalar_prefetch=1,
-            grid=(),
-            in_specs=[vmem] * 4,
-            out_specs=(vmem, vmem),
-            scratch_shapes=[pltpu.VMEM((amps.shape[0], width), jnp.float32)],
-        ),
-        compiler_params=pltpu.CompilerParams(vmem_limit_bytes=8 * MIB),
-    )(where, low, high, *last)
-    last_got = lax.ppermute(last_send, "core", swap)
+    after = [up[0], down[1]]
+    keep1, send1 = ladder(where, ready, low, high, after, pieces[:10])
+    keep2, send2 = ladder(where, ready, low, high, after, pieces[10:])
+    send1, send2, *last = lax.optimization_barrier((send1, send2, *last))
+    got1, got2 = lax.ppermute(send1, "core", swap), lax.ppermute(send2, "core", swap)
+    keep3, send3 = ladder(where, ready, low, high, after, last)
+    got3 = lax.ppermute(send3, "core", swap)
     packed = pl.pallas_call(
         pack_kernel,
-        out_shape=pltpu.VMEM((16, size + 16, LANES), jnp.int16),
+        out_shape=pltpu.VMEM((16, rows * width // LANES + 16, LANES), jnp.int16),
         grid_spec=pltpu.PrefetchScalarGridSpec(
-            num_scalar_prefetch=1, grid=(), in_specs=[vmem] * 4, out_specs=vmem
+            num_scalar_prefetch=1, grid=(), in_specs=[vmem] * 6, out_specs=vmem
         ),
         compiler_params=pltpu.CompilerParams(vmem_limit_bytes=4 * MIB),
-    )(where, keep, got, last_keep, last_got)
+    )(where, keep1, keep2, keep3, got1, got2, got3)
     parts = lax.all_to_all(packed, ("y", "x"), 0, 0, tiled=True)
     return pl.pallas_call(
         finish_kernel,

time: 63.8 us -> 63.5 us (level)
  waiting for transfers between devices: 4.84 us -> 2.78 us
  Pallas kernels: 13.1 us -> 14.3 us
  starting transfers between devices: 27.7 us -> 28.5 us
    ppermute x3, waiting for transfers between devices: 2.59 us -> 0.7 us  [on_device(): up[0] = lax.ppermute(up[0], 'z', forward)]
    pallas_call x3 -> x4, Pallas kernels: 6.53 us -> 7.72 us  [the longest x3 6.97 us: ladder(): pl.pallas_call(ladder_kernel, out_shape=(block, block), grid_spec=pltpu.P...]
    ppermute x1, waiting for transfers between devices: 0.01 us -> 0.96 us  [on_device(): lax.ppermute(up[0], 'z', forward)]
    ppermute x3, waiting for transfers between devices: 0.94 us -> 0.15 us  [on_device(): up[1] = lax.ppermute(up[1], 'z', forward)]
    ppermute x2 -> x3, starting transfers between devices: 5.1 us -> 5.56 us  [the longest x1 4.96 us: on_device(): lax.ppermute(send1, 'core', swap)]
    ppermute x2 -> x3, waiting for transfers between devices: 1.29 us -> 0.95 us  [the longest x1 0.94 us: on_device(): got3 = lax.ppermute(send3, 'core', swap)]
  transfers between devices with their start and end apart: 16 -> 17, of which waited for: 3 -> 4; matrix products, arithmetic and copies ran while one was open for 0% -> 0% of each run, Pallas kernels for 18% -> 20%
where the time goes in v9:
time: 63.5 us; the launch traced here: 63.3 us
  starting transfers between devices  28.5 us (45%)
  blocking collectives  16.5 us (26%)
  Pallas kernels  14.3 us (23%)
  waiting for transfers between devices  2.78 us (4%)
  local copies, waits for them, and re-layouts  1.05 us (2%)
    all_to_all x1, blocking collectives, on_device(): parts = lax.all_to_all(packed, ('y', 'x'), 0, 0, tiled=True)  16.5 us
    ppermute x3, starting transfers between devices, on_device(): down[1] = lax.ppermute(down[1], 'z', backward)  9.34 us
    ppermute x3, starting transfers between devices, on_device(): down[0] = lax.ppermute(down[0], 'z', backward)  8.03 us
    pallas_call x3, Pallas kernels, ladder(): pl.pallas_call(ladder_kernel, out_shape=(block, block), grid_spec=pltpu.P...  6.97 us
    ppermute x1, starting transfers between devices, on_device(): lax.ppermute(send1, 'core', swap)  4.96 us
    pallas_call x1, Pallas kernels, on_device(): pl.pallas_call(low_kernel, out_shape=(half, pltpu.VMEM((depth // LANES //...  3.33 us
    ppermute x1, starting transfers between devices, on_device(): lax.ppermute(down[1], 'z', backward)  2.82 us
    ppermute x3, starting transfers between devices, on_device(): up[0] = lax.ppermute(up[0], 'z', forward)  2.71 us
  transfers between devices with their start and end apart: 17, of which 4 were waited for; matrix products, arithmetic and copies ran while one was open for 0% of the time, Pallas kernels for 20%

profile of v9, /device:TPU:1, one launch (start us, length us, event | category | flops | bytes accessed | tf_op | source)
XLA Modules:
  0.0 63.3 jit_solution(10953413510009793565)
XLA Ops:
  0.0 1.0 %fusion = (bf16[48,2048]{1,0:T(8,128)(2,1)S(1)}, bf16[48,2048]{1,0:T(8,128)(2,1)S(1)}) fusion(bf16[48,4096]{1,0:T(8,128)(2,1)} %param.11), kind=kLoop, calls=%fused_computation.1 | loop fusion | bytes 786432 | tf_op jit(solution)/shard_map/slice | solution.py:197
  1.1 2.5 %collective-permute-start = (bf16[48,2048]{1,0:T(8,128)(2,1)S(1)}, bf16[48,2048]{1,0:T(8,128)(2,1)S(1)}, u32[]{:S(2)}, u32[]{:S(2)}) collective-permute-start(bf16[48,2048]{1,0:T(8,128)(2,1)S(1)} %get-tuple-element.50.refs_0_), channel_id=1, source_target_pairs={{0,32},{32,64},{64,96},{96,128},{128,160},{160,192},{192,224},{224... | collective-permute-start | bytes 589832 | tf_op jit(solution)/shard_map/ppermute | solution.py:201
  3.6 4.0 %collective-permute-start.5 = (bf16[48,2048]{1,0:T(8,128)(2,1)S(1)}, bf16[48,2048]{1,0:T(8,128)(2,1)S(1)}, u32[]{:S(2)}, u32[]{:S(2)}) collective-permute-start(bf16[48,2048]{1,0:T(8,128)(2,1)S(1)} %get-tuple-element.49.refs_1_), channel_id=1, source_target_pairs={{0,224},{32,0},{64,32},{96,64},{128,96},{160,128},{192,160},{224,1... | collective-permute-start | bytes 589832 | tf_op jit(solution)/shard_map/ppermute | solution.py:204
  7.6 2.7 %collective-permute-start.3 = (bf16[48,2048]{1,0:T(8,128)(2,1)S(1)}, bf16[48,2048]{1,0:T(8,128)(2,1)S(1)}, u32[]{:S(2)}, u32[]{:S(2)}) collective-permute-start(bf16[48,2048]{1,0:T(8,128)(2,1)S(1)} %get-tuple-element.50.refs_0_), channel_id=1, source_target_pairs={{0,224},{32,0},{64,32},{96,64},{128,96},{160,128},{192,160},{224,1... | collective-permute-start | bytes 589832 | tf_op jit(solution)/shard_map/ppermute | solution.py:203
  10.4 3.3 %shard_map.109 = (bf16[2048,1024]{1,0:T(8,128)(2,1)S(1)}, f32[16,128]{1,0:T(8,128)S(1)}, f32[8,128]{1,0:T(8,128)S(1)}, f32[8,128]{1,0:T(8,128)S(1)}, f32[16,128]{1,0:T(8,128)S(1)}) custom-call(s32[32,128]{1,0:T(8,128)} %bitcast.6, s32[32,128]{1,0:T(8,128)} %bitcast.7, s32[8,128]{1,0:T(8,128)} %bitcast.8, s32[8,128]{1,0:T(8,128)} %bitcast.9, s32[12]{0:T(128)} %occ1.1, ...), custom_call_target="tpu_custom_call" | custom-call | tf_op jit(solution)/shard_map/pallas_call | solution.py:179
  13.8 2.7 %collective-permute-start.6 = (bf16[48,2048]{1,0:T(8,128)(2,1)S(1)}, bf16[48,2048]{1,0:T(8,128)(2,1)S(1)}, u32[]{:S(2)}, u32[]{:S(2)}) collective-permute-start(bf16[48,2048]{1,0:T(8,128)(2,1)S(1)} %collective-permute-done.5.refs_5_), channel_id=1, source_target_pairs={{0,224},{32,0},{64,32},{96,64},{128,96},{160,128},{192,160},{224,1... | collective-permute-start | bytes 589832 | tf_op jit(solution)/shard_map/ppermute | solution.py:204
  16.5 2.7 %collective-permute-start.9 = (bf16[48,2048]{1,0:T(8,128)(2,1)S(1)}, bf16[48,2048]{1,0:T(8,128)(2,1)S(1)}, u32[]{:S(2)}, u32[]{:S(2)}) collective-permute-start(bf16[48,2048]{1,0:T(8,128)(2,1)S(1)} %collective-permute-done.3.after2.refs_4_), channel_id=1, source_target_pairs={{0,224},{32,0},{64,32},{96,64},{128,96},{160,128},{192,160},{224,1... | collective-permute-start | bytes 589832 | tf_op jit(solution)/shard_map/ppermute | solution.py:203
  19.2 2.5 %shard_map.110 = (bf16[2048,1024]{1,0:T(8,128)(2,1)S(1)}, f32[8,128]{1,0:T(8,128)S(1)}) custom-call(f32[16,128]{1,0:T(8,128)S(1)} %get-tuple-element.30.cd, f32[8,128]{1,0:T(8,128)S(1)} %get-tuple-element.31.ab, bf16[4096,1024]{1,0:T(8,128)(2,1)} %values.3, bf16[48,2048]{1,0:T(8,128)(2,1)S(1)} %collective-permute-done.2.after1.refs_3_, ...), custom_call_target="tpu_custom_call" | custom-call | tf_op jit(solution)/shard_map/pallas_call | solution.py:207
  21.8 2.7 %collective-permute-start.7 = (bf16[48,2048]{1,0:T(8,128)(2,1)S(1)}, bf16[48,2048]{1,0:T(8,128)(2,1)S(1)}, u32[]{:S(2)}, u32[]{:S(2)}) collective-permute-start(bf16[48,2048]{1,0:T(8,128)(2,1)S(1)} %collective-permute-done.6.refs_9_), channel_id=1, source_target_pairs={{0,224},{32,0},{64,32},{96,64},{128,96},{160,128},{192,160},{224,1... | collective-permute-start | bytes 589832 | tf_op jit(solution)/shard_map/ppermute | solution.py:204
  24.4 0.1 collective-permute-done.8.refs_7_
  24.6 2.7 %collective-permute-start.11 = (bf16[48,2048]{1,0:T(8,128)(2,1)S(1)}, bf16[48,2048]{1,0:T(8,128)(2,1)S(1)}, u32[]{:S(2)}, u32[]{:S(2)}) collective-permute-start(bf16[48,2048]{1,0:T(8,128)(2,1)S(1)} %collective-permute-done.9.refs_8_), channel_id=1, source_target_pairs={{0,224},{32,0},{64,32},{96,64},{128,96},{160,128},{192,160},{224,1... | collective-permute-start | bytes 589832 | tf_op jit(solution)/shard_map/ppermute | solution.py:203
  27.3 0.7 %collective-permute-done.4.after1.refs_0_ = bf16[48,2048]{1,0:T(8,128)(2,1)S(1)} collective-permute-done((bf16[48,2048]{1,0:T(8,128)(2,1)S(1)}, bf16[48,2048]{1,0:T(8,128)(2,1)S(1)}, u32[]{:S(2)}, u32[]{:S(2)}) %collective-permute-start.4) | collective-permute-done | bytes 196640 | tf_op jit(solution)/shard_map/ppermute | solution.py:201
  28.0 2.8 %collective-permute-start.13 = (bf16[48,2048]{1,0:T(8,128)(2,1)S(1)}, bf16[48,2048]{1,0:T(8,128)(2,1)S(1)}, u32[]{:S(2)}, u32[]{:S(2)}) collective-permute-start(bf16[48,2048]{1,0:T(8,128)(2,1)S(1)} %collective-permute-done.7.after2.refs_3_), channel_id=1, source_target_pairs={{0,224},{32,0},{64,32},{96,64},{128,96},{160,128},{192,160},{224,1... | collective-permute-start | bytes 589832 | tf_op jit(solution)/shard_map/ppermute | solution.py:218
  30.8 2.8 %shard_map.111 = (f32[10,96,128]{2,1,0:T(8,128)S(1)}, f32[10,96,128]{2,1,0:T(8,128)S(1)}) custom-call(s32[2]{0:T(128)S(1)} %pad_add_fusion.where, f32[8,128]{1,0:T(8,128)S(1)} %get-tuple-element.33.ready, bf16[2048,1024]{1,0:T(8,128)(2,1)S(1)} %get-tuple-element.34.low, bf16[2048,1024]{1,0:T(8,128)(2,1)S(1)} %get-tuple-element.35.high, ...), custom_call_target="tpu_custom_call" | custom-call | tf_op jit(solution)/shard_map/pallas_call | solution.py:119
  33.6 2.0 %shard_map.112 = (f32[4,96,128]{2,1,0:T(8,128)S(1)}, f32[4,96,128]{2,1,0:T(8,128)S(1)}) custom-call(s32[2]{0:T(128)S(1)} %pad_add_fusion.where, f32[8,128]{1,0:T(8,128)S(1)} %get-tuple-element.33.ready, bf16[2048,1024]{1,0:T(8,128)(2,1)S(1)} %get-tuple-element.34.low, bf16[2048,1024]{1,0:T(8,128)(2,1)S(1)} %get-tuple-element.35.high, ...), custom_call_target="tpu_custom_call" | custom-call | tf_op jit(solution)/shard_map/pallas_call | solution.py:119
  35.7 1.0 %collective-permute-done.12.refs_0_ = bf16[48,2048]{1,0:T(8,128)(2,1)S(1)} collective-permute-done((bf16[48,2048]{1,0:T(8,128)(2,1)S(1)}, bf16[48,2048]{1,0:T(8,128)(2,1)S(1)}, u32[]{:S(2)}, u32[]{:S(2)}) %collective-permute-start.12) | collective-permute-done | bytes 196640 | tf_op jit(solution)/shard_map/ppermute | solution.py:218
  36.7 5.0 %collective-permute-start.14 = (f32[10,96,128]{2,1,0:T(8,128)S(1)}, f32[10,96,128]{2,1,0:T(8,128)S(1)}, u32[]{:S(2)}, u32[]{:S(2)}) collective-permute-start(f32[10,96,128]{2,1,0:T(8,128)S(1)} %get-tuple-element.44), channel_id=1, source_target_pairs={{0,1},{1,0},{2,3},{3,2},{4,5},{5,4},{6,7},{7,6},{8,9},{9,8},{10,11... | collective-permute-start | bytes 1474568 | tf_op jit(solution)/shard_map/ppermute | solution.py:224
  41.6 0.1 collective-permute-start.15
  41.7 2.1 %shard_map.113 = (f32[2,96,128]{2,1,0:T(8,128)S(1)}, f32[2,96,128]{2,1,0:T(8,128)S(1)}) custom-call(s32[2]{0:T(128)S(1)} %pad_add_fusion.where, f32[8,128]{1,0:T(8,128)S(1)} %get-tuple-element.33.ready, bf16[2048,1024]{1,0:T(8,128)(2,1)S(1)} %get-tuple-element.34.low, bf16[2048,1024]{1,0:T(8,128)(2,1)S(1)} %get-tuple-element.35.high, ...), custom_call_target="tpu_custom_call" | custom-call | tf_op jit(solution)/shard_map/pallas_call | solution.py:119
  43.8 0.5 collective-permute-start.16
  44.3 0.9 %collective-permute-done.16.refs_5_ = f32[2,96,128]{2,1,0:T(8,128)S(1)} collective-permute-done((f32[2,96,128]{2,1,0:T(8,128)S(1)}, f32[2,96,128]{2,1,0:T(8,128)S(1)}, u32[]{:S(2)}, u32[]{:S(2)}) %collective-permute-start.16) | collective-permute-done | bytes 98336 | tf_op jit(solution)/shard_map/ppermute | solution.py:226
  45.3 0.8 %shard_map.114 = s16[16,112,128]{2,1,0:T(8,128)(2,1)S(1)} custom-call(s32[2]{0:T(128)S(1)} %pad_add_fusion.where, f32[10,96,128]{2,1,0:T(8,128)S(1)} %get-tuple-element.37.refs_0_, f32[4,96,128]{2,1,0:T(8,128)S(1)} %get-tuple-element.38.refs_1_, f32[2,96,128]{2,1,0:T(8,128)S(1)} %get-tuple-element.43.refs_2_, ...), custom_call_target="tpu_custom_call" | custom-call | tf_op jit(solution)/shard_map/pallas_call | solution.py:227
  46.0 16.5 %all_to_all.5.parts = s16[16,112,128]{2,1,0:T(8,128)(2,1)S(1)} all-to-all(s16[16,112,128]{2,1,0:T(8,128)(2,1)S(1)} %shard_map.114), channel_id=1, replica_groups=mesh['z'=8,'y'=4,'x'=4,'core'=2] {'y','x'}, dimensions={0} | all-to-all | bytes 917504 | tf_op jit(solution)/shard_map/all_to_all | solution.py:235
  62.5 0.8 %shard_map.115 = f32[12,1024]{1,0:T(8,128)} custom-call(s16[16,112,128]{2,1,0:T(8,128)(2,1)S(1)} %all_to_all.5.parts, f32[8,128]{1,0:T(8,128)S(1)} %get-tuple-element.47.virt, f32[16,128]{1,0:T(8,128)S(1)} %get-tuple-element.48.occ), custom_call_target="tpu_custom_call" | custom-call | tf_op jit(solution)/shard_map/pallas_call | solution.py:236
  (20 shorter events, 0.3 us)
Async XLA Ops:
  1.1 12.7 %collective-permute-start = (bf16[48,2048]{1,0:T(8,128)(2,1)S(1)}, bf16[48,2048]{1,0:T(8,128)(2,1)S(1)}, u32[]{:S(2)}, u32[]{:S(2)}) collective-permute-start(bf16[48,2048]{1,0:T(8,128)(2,1)S(1)} %get-tuple-element.50.refs_0_), channel_id=1, source_target_pairs={{0,32},{32,64},{64,96},{96,128},{128,160},{160,192},{192,224},{224... | collective-permute-start | bytes 589832 | tf_op jit(solution)/shard_map/ppermute | solution.py:201
  3.6 10.2 %collective-permute-start.5 = (bf16[48,2048]{1,0:T(8,128)(2,1)S(1)}, bf16[48,2048]{1,0:T(8,128)(2,1)S(1)}, u32[]{:S(2)}, u32[]{:S(2)}) collective-permute-start(bf16[48,2048]{1,0:T(8,128)(2,1)S(1)} %get-tuple-element.49.refs_1_), channel_id=1, source_target_pairs={{0,224},{32,0},{64,32},{96,64},{128,96},{160,128},{192,160},{224,1... | collective-permute-start | bytes 589832 | tf_op jit(solution)/shard_map/ppermute | solution.py:204
  7.6 8.9 %collective-permute-start.2 = (bf16[48,2048]{1,0:T(8,128)(2,1)S(1)}, bf16[48,2048]{1,0:T(8,128)(2,1)S(1)}, u32[]{:S(2)}, u32[]{:S(2)}) collective-permute-start(bf16[48,2048]{1,0:T(8,128)(2,1)S(1)} %get-tuple-element.49.refs_1_), channel_id=1, source_target_pairs={{0,32},{32,64},{64,96},{96,128},{128,160},{160,192},{192,224},{224... | collective-permute-start | bytes 589832 | tf_op jit(solution)/shard_map/ppermute | solution.py:202
  7.6 8.9 %collective-permute-start.3 = (bf16[48,2048]{1,0:T(8,128)(2,1)S(1)}, bf16[48,2048]{1,0:T(8,128)(2,1)S(1)}, u32[]{:S(2)}, u32[]{:S(2)}) collective-permute-start(bf16[48,2048]{1,0:T(8,128)(2,1)S(1)} %get-tuple-element.50.refs_0_), channel_id=1, source_target_pairs={{0,224},{32,0},{64,32},{96,64},{128,96},{160,128},{192,160},{224,1... | collective-permute-start | bytes 589832 | tf_op jit(solution)/shard_map/ppermute | solution.py:203
  13.7 7.9 %collective-permute-start.1 = (bf16[48,2048]{1,0:T(8,128)(2,1)S(1)}, bf16[48,2048]{1,0:T(8,128)(2,1)S(1)}, u32[]{:S(2)}, u32[]{:S(2)}) collective-permute-start(bf16[48,2048]{1,0:T(8,128)(2,1)S(1)} %collective-permute-done.refs_2_), channel_id=1, source_target_pairs={{0,32},{32,64},{64,96},{96,128},{128,160},{160,192},{192,224},{224... | collective-permute-start | bytes 589832 | tf_op jit(solution)/shard_map/ppermute | solution.py:201
  13.8 7.9 %collective-permute-start.6 = (bf16[48,2048]{1,0:T(8,128)(2,1)S(1)}, bf16[48,2048]{1,0:T(8,128)(2,1)S(1)}, u32[]{:S(2)}, u32[]{:S(2)}) collective-permute-start(bf16[48,2048]{1,0:T(8,128)(2,1)S(1)} %collective-permute-done.5.refs_5_), channel_id=1, source_target_pairs={{0,224},{32,0},{64,32},{96,64},{128,96},{160,128},{192,160},{224,1... | collective-permute-start | bytes 589832 | tf_op jit(solution)/shard_map/ppermute | solution.py:204
  16.5 8.1 %collective-permute-start.8 = (bf16[48,2048]{1,0:T(8,128)(2,1)S(1)}, bf16[48,2048]{1,0:T(8,128)(2,1)S(1)}, u32[]{:S(2)}, u32[]{:S(2)}) collective-permute-start(bf16[48,2048]{1,0:T(8,128)(2,1)S(1)} %collective-permute-done.2.after1.refs_3_), channel_id=1, source_target_pairs={{0,32},{32,64},{64,96},{96,128},{128,160},{160,192},{192,224},{224... | collective-permute-start | bytes 589832 | tf_op jit(solution)/shard_map/ppermute | solution.py:202
  16.5 8.1 %collective-permute-start.9 = (bf16[48,2048]{1,0:T(8,128)(2,1)S(1)}, bf16[48,2048]{1,0:T(8,128)(2,1)S(1)}, u32[]{:S(2)}, u32[]{:S(2)}) collective-permute-start(bf16[48,2048]{1,0:T(8,128)(2,1)S(1)} %collective-permute-done.3.after2.refs_4_), channel_id=1, source_target_pairs={{0,224},{32,0},{64,32},{96,64},{128,96},{160,128},{192,160},{224,1... | collective-permute-start | bytes 589832 | tf_op jit(solution)/shard_map/ppermute | solution.py:203
  21.7 6.3 %collective-permute-start.4 = (bf16[48,2048]{1,0:T(8,128)(2,1)S(1)}, bf16[48,2048]{1,0:T(8,128)(2,1)S(1)}, u32[]{:S(2)}, u32[]{:S(2)}) collective-permute-start(bf16[48,2048]{1,0:T(8,128)(2,1)S(1)} %collective-permute-done.1.refs_6_), channel_id=1, source_target_pairs={{0,32},{32,64},{64,96},{96,128},{128,160},{160,192},{192,224},{224... | collective-permute-start | bytes 589832 | tf_op jit(solution)/shard_map/ppermute | solution.py:201
  21.8 6.2 %collective-permute-start.7 = (bf16[48,2048]{1,0:T(8,128)(2,1)S(1)}, bf16[48,2048]{1,0:T(8,128)(2,1)S(1)}, u32[]{:S(2)}, u32[]{:S(2)}) collective-permute-start(bf16[48,2048]{1,0:T(8,128)(2,1)S(1)} %collective-permute-done.6.refs_9_), channel_id=1, source_target_pairs={{0,224},{32,0},{64,32},{96,64},{128,96},{160,128},{192,160},{224,1... | collective-permute-start | bytes 589832 | tf_op jit(solution)/shard_map/ppermute | solution.py:204
  24.6 9.0 %collective-permute-start.10 = (bf16[48,2048]{1,0:T(8,128)(2,1)S(1)}, bf16[48,2048]{1,0:T(8,128)(2,1)S(1)}, u32[]{:S(2)}, u32[]{:S(2)}) collective-permute-start(bf16[48,2048]{1,0:T(8,128)(2,1)S(1)} %collective-permute-done.8.refs_7_), channel_id=1, source_target_pairs={{0,32},{32,64},{64,96},{96,128},{128,160},{160,192},{192,224},{224... | collective-permute-start | bytes 589832 | tf_op jit(solution)/shard_map/ppermute | solution.py:202
  24.6 9.0 %collective-permute-start.11 = (bf16[48,2048]{1,0:T(8,128)(2,1)S(1)}, bf16[48,2048]{1,0:T(8,128)(2,1)S(1)}, u32[]{:S(2)}, u32[]{:S(2)}) collective-permute-start(bf16[48,2048]{1,0:T(8,128)(2,1)S(1)} %collective-permute-done.9.refs_8_), channel_id=1, source_target_pairs={{0,224},{32,0},{64,32},{96,64},{128,96},{160,128},{192,160},{224,1... | collective-permute-start | bytes 589832 | tf_op jit(solution)/shard_map/ppermute | solution.py:203
  28.0 8.7 %collective-permute-start.12 = (bf16[48,2048]{1,0:T(8,128)(2,1)S(1)}, bf16[48,2048]{1,0:T(8,128)(2,1)S(1)}, u32[]{:S(2)}, u32[]{:S(2)}) collective-permute-start(bf16[48,2048]{1,0:T(8,128)(2,1)S(1)} %collective-permute-done.4.after1.refs_0_), channel_id=1, source_target_pairs={{0,32},{32,64},{64,96},{96,128},{128,160},{160,192},{192,224},{224... | collective-permute-start | bytes 589832 | tf_op jit(solution)/shard_map/ppermute | solution.py:218
  28.0 8.7 %collective-permute-start.13 = (bf16[48,2048]{1,0:T(8,128)(2,1)S(1)}, bf16[48,2048]{1,0:T(8,128)(2,1)S(1)}, u32[]{:S(2)}, u32[]{:S(2)}) collective-permute-start(bf16[48,2048]{1,0:T(8,128)(2,1)S(1)} %collective-permute-done.7.after2.refs_3_), channel_id=1, source_target_pairs={{0,224},{32,0},{64,32},{96,64},{128,96},{160,128},{192,160},{224,1... | collective-permute-start | bytes 589832 | tf_op jit(solution)/shard_map/ppermute | solution.py:218
  36.7 8.6 %collective-permute-start.14 = (f32[10,96,128]{2,1,0:T(8,128)S(1)}, f32[10,96,128]{2,1,0:T(8,128)S(1)}, u32[]{:S(2)}, u32[]{:S(2)}) collective-permute-start(f32[10,96,128]{2,1,0:T(8,128)S(1)} %get-tuple-element.44), channel_id=1, source_target_pairs={{0,1},{1,0},{2,3},{3,2},{4,5},{5,4},{6,7},{7,6},{8,9},{9,8},{10,11... | collective-permute-start | bytes 1474568 | tf_op jit(solution)/shard_map/ppermute | solution.py:224
  41.6 3.7 %collective-permute-start.15 = (f32[4,96,128]{2,1,0:T(8,128)S(1)}, f32[4,96,128]{2,1,0:T(8,128)S(1)}, u32[]{:S(2)}, u32[]{:S(2)}) collective-permute-start(f32[4,96,128]{2,1,0:T(8,128)S(1)} %get-tuple-element.45), channel_id=1, source_target_pairs={{0,1},{1,0},{2,3},{3,2},{4,5},{5,4},{6,7},{7,6},{8,9},{9,8},{10,11... | collective-permute-start | bytes 589832 | tf_op jit(solution)/shard_map/ppermute | solution.py:224
  43.8 1.4 %collective-permute-start.16 = (f32[2,96,128]{2,1,0:T(8,128)S(1)}, f32[2,96,128]{2,1,0:T(8,128)S(1)}, u32[]{:S(2)}, u32[]{:S(2)}) collective-permute-start(f32[2,96,128]{2,1,0:T(8,128)S(1)} %get-tuple-element.46), channel_id=1, source_target_pairs={{0,1},{1,0},{2,3},{3,2},{4,5},{5,4},{6,7},{7,6},{8,9},{9,8},{10,11... | collective-permute-start | bytes 294920 | tf_op jit(solution)/shard_map/ppermute | solution.py:226

commit v10 on v9

--- a/solution.py
+++ b/solution.py
@@ -130,22 +130,27 @@
     )(where, ready, low, high, *after, *pieces)
 
 
-def pack_kernel(where, *refs):
-    out = refs[-1]
-    kept, got = refs[: len(refs) // 2], refs[len(refs) // 2 : -1]
-    rows = kept[0].shape[1]
-    shifts = iter(SHARDS)
-    for mine, other in zip(kept, got):
-        for place in range(mine.shape[0] // 2):
-            shard = lax.rem(where[0] + (next(shifts) + 8), 8)
-            for high in range(2):
-                both = mine[2 * place + high] + other[2 * place + high]
-                top = jnp.maximum(jnp.max(jnp.abs(both), axis=0, keepdims=True), 1e-30)
-                power = jnp.floor(14.99 - jnp.log2(top))
-                scaled = jnp.clip(jnp.round(both * jnp.exp2(power)), -32767.0, 32767.0)
-                out[2 * shard + high, :rows, :] = scaled.astype(jnp.int32).astype(jnp.int16)
-                power = jnp.broadcast_to(power, (out.shape[1] - rows, LANES))
-                out[2 * shard + high, rows:, :] = power.astype(jnp.int32).astype(jnp.int16)
+def touch_kernel(ready, after1, after2, after3, out):
+    out[...] = ready[...]
+
+
+def pack_kernel(where, first_keep, last_keep, first_got, last_got, out):
+    rows = first_keep.shape[1]
+    first = first_keep.shape[0] // 2
+    for place, shift in enumerate(SHARDS):
+        shard = lax.rem(where[0] + (shift + 8), 8)
+        for high in range(2):
+            if place < first:
+                both = first_keep[2 * place + high] + first_got[2 * place + high]
+            else:
+                at = 2 * (place - first) + high
+                both = last_keep[at] + last_got[at]
+            top = jnp.maximum(jnp.max(jnp.abs(both), axis=0, keepdims=True), 1e-30)
+            power = jnp.floor(14.99 - jnp.log2(top))
+            scaled = jnp.clip(jnp.round(both * jnp.exp2(power)), -32767.0, 32767.0)
+            out[2 * shard + high, :rows, :] = scaled.astype(jnp.int32).astype(jnp.int16)
+            power = jnp.broadcast_to(power, (out.shape[1] - rows, LANES))
+            out[2 * shard + high, rows:, :] = power.astype(jnp.int32).astype(jnp.int16)
 
 
 def finish_kernel(parts, virt, occ, out):
@@ -218,20 +223,26 @@
     last = [lax.ppermute(up[0], "z", forward), lax.ppermute(down[1], "z", backward)]
     swap = [(0, 1), (1, 0)]
     after = [up[0], down[1]]
-    keep1, send1 = ladder(where, ready, low, high, after, pieces[:10])
-    keep2, send2 = ladder(where, ready, low, high, after, pieces[10:])
-    send1, send2, *last = lax.optimization_barrier((send1, send2, *last))
-    got1, got2 = lax.ppermute(send1, "core", swap), lax.ppermute(send2, "core", swap)
-    keep3, send3 = ladder(where, ready, low, high, after, last)
-    got3 = lax.ppermute(send3, "core", swap)
+    keep, send = ladder(where, ready, low, high, after, pieces[:10])
+    touched = pl.pallas_call(
+        touch_kernel,
+        out_shape=lines,
+        in_specs=[vmem, hbm, hbm, hbm],
+        out_specs=vmem,
+        compiler_params=pltpu.CompilerParams(vmem_limit_bytes=1 * MIB),
+    )(ready, up[1], down[0], keep)
+    send, ready, *last = lax.optimization_barrier((send, touched, *last))
+    got = lax.ppermute(send, "core", swap)
+    last_keep, last_send = ladder(where, ready, low, high, after, pieces[10:] + last)
+    last_got = lax.ppermute(last_send, "core", swap)
     packed = pl.pallas_call(
         pack_kernel,
         out_shape=pltpu.VMEM((16, rows * width // LANES + 16, LANES), jnp.int16),
         grid_spec=pltpu.PrefetchScalarGridSpec(
-            num_scalar_prefetch=1, grid=(), in_specs=[vmem] * 6, out_specs=vmem
+            num_scalar_prefetch=1, grid=(), in_specs=[vmem] * 4, out_specs=vmem
         ),
         compiler_params=pltpu.CompilerParams(vmem_limit_bytes=4 * MIB),
-    )(where, keep1, keep2, keep3, got1, got2, got3)
+    )(where, keep, last_keep, got, last_got)
     parts = lax.all_to_all(packed, ("y", "x"), 0, 0, tiled=True)
     return pl.pallas_call(
         finish_kernel,

time: 63.5 us -> 62.9 us (level)
  waiting for transfers between devices: 2.78 us -> 5.44 us
  Pallas kernels: 14.3 us -> 12.2 us
  starting transfers between devices: 28.5 us -> 26.6 us
    pallas_call x3 -> x2, Pallas kernels: 6.97 us -> 4.83 us  [ladder(): pl.pallas_call(ladder_kernel, out_shape=(block, block), grid_spec=pltpu.P...]
    ppermute x1, waiting for transfers between devices: 0.96 us -> 3 us  [on_device(): lax.ppermute(up[0], 'z', forward)]
    ppermute x3 -> x2, starting transfers between devices: 5.56 us -> 3.69 us  [the longest x1 3.6 us: on_device(): got = lax.ppermute(send, 'core', swap)]
    ppermute x3 -> x2, waiting for transfers between devices: 0.95 us -> 1.57 us  [the longest x1 1.57 us: on_device(): last_got = lax.ppermute(last_send, 'core', swap)]
  transfers between devices with their start and end apart: 17 -> 16, of which waited for: 4 -> 4; matrix products, arithmetic and copies ran while one was open for 0% -> 0% of each run, Pallas kernels for 20% -> 17%
where the time goes in v10:
time: 62.9 us; the launch traced here: 62.2 us
  starting transfers between devices  26.6 us (42%)
  blocking collectives  16.8 us (27%)
  Pallas kernels  12.2 us (19%)
  waiting for transfers between devices  5.44 us (9%)
  local copies, waits for them, and re-layouts  1.05 us (2%)
    all_to_all x1, blocking collectives, on_device(): parts = lax.all_to_all(packed, ('y', 'x'), 0, 0, tiled=True)  16.8 us
    ppermute x3, starting transfers between devices, on_device(): down[1] = lax.ppermute(down[1], 'z', backward)  9.34 us
    ppermute x3, starting transfers between devices, on_device(): down[0] = lax.ppermute(down[0], 'z', backward)  8.03 us
    pallas_call x2, Pallas kernels, ladder(): pl.pallas_call(ladder_kernel, out_shape=(block, block), grid_spec=pltpu.P...  4.83 us
    ppermute x1, starting transfers between devices, on_device(): got = lax.ppermute(send, 'core', swap)  3.6 us
    pallas_call x1, Pallas kernels, on_device(): pl.pallas_call(low_kernel, out_shape=(half, pltpu.VMEM((depth // LANES //...  3.33 us
    ppermute x1, waiting for transfers between devices, on_device(): lax.ppermute(up[0], 'z', forward)  3 us
    ppermute x1, starting transfers between devices, on_device(): lax.ppermute(down[1], 'z', backward)  2.82 us
  transfers between devices with their start and end apart: 16, of which 4 were waited for; matrix products, arithmetic and copies ran while one was open for 0% of the time, Pallas kernels for 17%

profile of v10, /device:TPU:1, one launch (start us, length us, event | category | flops | bytes accessed | tf_op | source)
XLA Modules:
  0.0 62.2 jit_solution(17889268228215633866)
XLA Ops:
  0.0 1.0 %fusion = (bf16[48,2048]{1,0:T(8,128)(2,1)S(1)}, bf16[48,2048]{1,0:T(8,128)(2,1)S(1)}) fusion(bf16[48,4096]{1,0:T(8,128)(2,1)} %param.11), kind=kLoop, calls=%fused_computation.1 | loop fusion | bytes 786432 | tf_op jit(solution)/shard_map/slice | solution.py:202
  1.1 2.5 %collective-permute-start = (bf16[48,2048]{1,0:T(8,128)(2,1)S(1)}, bf16[48,2048]{1,0:T(8,128)(2,1)S(1)}, u32[]{:S(2)}, u32[]{:S(2)}) collective-permute-start(bf16[48,2048]{1,0:T(8,128)(2,1)S(1)} %get-tuple-element.46.refs_0_), channel_id=1, source_target_pairs={{0,32},{32,64},{64,96},{96,128},{128,160},{160,192},{192,224},{224... | collective-permute-start | bytes 589832 | tf_op jit(solution)/shard_map/ppermute | solution.py:206
  3.6 4.0 %collective-permute-start.5 = (bf16[48,2048]{1,0:T(8,128)(2,1)S(1)}, bf16[48,2048]{1,0:T(8,128)(2,1)S(1)}, u32[]{:S(2)}, u32[]{:S(2)}) collective-permute-start(bf16[48,2048]{1,0:T(8,128)(2,1)S(1)} %get-tuple-element.45.refs_1_), channel_id=1, source_target_pairs={{0,224},{32,0},{64,32},{96,64},{128,96},{160,128},{192,160},{224,1... | collective-permute-start | bytes 589832 | tf_op jit(solution)/shard_map/ppermute | solution.py:209
  7.6 2.7 %collective-permute-start.3 = (bf16[48,2048]{1,0:T(8,128)(2,1)S(1)}, bf16[48,2048]{1,0:T(8,128)(2,1)S(1)}, u32[]{:S(2)}, u32[]{:S(2)}) collective-permute-start(bf16[48,2048]{1,0:T(8,128)(2,1)S(1)} %get-tuple-element.46.refs_0_), channel_id=1, source_target_pairs={{0,224},{32,0},{64,32},{96,64},{128,96},{160,128},{192,160},{224,1... | collective-permute-start | bytes 589832 | tf_op jit(solution)/shard_map/ppermute | solution.py:208
  10.4 3.3 %shard_map.109 = (bf16[2048,1024]{1,0:T(8,128)(2,1)S(1)}, f32[16,128]{1,0:T(8,128)S(1)}, f32[8,128]{1,0:T(8,128)S(1)}, f32[8,128]{1,0:T(8,128)S(1)}, f32[16,128]{1,0:T(8,128)S(1)}) custom-call(s32[32,128]{1,0:T(8,128)} %bitcast.6, s32[32,128]{1,0:T(8,128)} %bitcast.7, s32[8,128]{1,0:T(8,128)} %bitcast.8, s32[8,128]{1,0:T(8,128)} %bitcast.9, s32[12]{0:T(128)} %occ1.1, ...), custom_call_target="tpu_custom_call" | custom-call | tf_op jit(solution)/shard_map/pallas_call | solution.py:184
  13.7 0.1 collective-permute-start.1
  13.8 2.7 %collective-permute-start.6 = (bf16[48,2048]{1,0:T(8,128)(2,1)S(1)}, bf16[48,2048]{1,0:T(8,128)(2,1)S(1)}, u32[]{:S(2)}, u32[]{:S(2)}) collective-permute-start(bf16[48,2048]{1,0:T(8,128)(2,1)S(1)} %collective-permute-done.5.refs_5_), channel_id=1, source_target_pairs={{0,224},{32,0},{64,32},{96,64},{128,96},{160,128},{192,160},{224,1... | collective-permute-start | bytes 589832 | tf_op jit(solution)/shard_map/ppermute | solution.py:209
  16.5 2.7 %collective-permute-start.9 = (bf16[48,2048]{1,0:T(8,128)(2,1)S(1)}, bf16[48,2048]{1,0:T(8,128)(2,1)S(1)}, u32[]{:S(2)}, u32[]{:S(2)}) collective-permute-start(bf16[48,2048]{1,0:T(8,128)(2,1)S(1)} %collective-permute-done.3.after2.refs_4_), channel_id=1, source_target_pairs={{0,224},{32,0},{64,32},{96,64},{128,96},{160,128},{192,160},{224,1... | collective-permute-start | bytes 589832 | tf_op jit(solution)/shard_map/ppermute | solution.py:208
  19.2 2.5 %shard_map.110 = (bf16[2048,1024]{1,0:T(8,128)(2,1)S(1)}, f32[8,128]{1,0:T(8,128)S(1)}) custom-call(f32[16,128]{1,0:T(8,128)S(1)} %get-tuple-element.28.cd, f32[8,128]{1,0:T(8,128)S(1)} %get-tuple-element.29.ab, bf16[4096,1024]{1,0:T(8,128)(2,1)} %values.3, bf16[48,2048]{1,0:T(8,128)(2,1)S(1)} %collective-permute-done.2.after1.refs_3_, ...), custom_call_target="tpu_custom_call" | custom-call | tf_op jit(solution)/shard_map/pallas_call | solution.py:212
  21.7 0.1 collective-permute-start.4
  21.8 2.7 %collective-permute-start.7 = (bf16[48,2048]{1,0:T(8,128)(2,1)S(1)}, bf16[48,2048]{1,0:T(8,128)(2,1)S(1)}, u32[]{:S(2)}, u32[]{:S(2)}) collective-permute-start(bf16[48,2048]{1,0:T(8,128)(2,1)S(1)} %collective-permute-done.6.refs_9_), channel_id=1, source_target_pairs={{0,224},{32,0},{64,32},{96,64},{128,96},{160,128},{192,160},{224,1... | collective-permute-start | bytes 589832 | tf_op jit(solution)/shard_map/ppermute | solution.py:209
  24.4 0.1 collective-permute-done.8.refs_7_
  24.6 2.7 %collective-permute-start.11 = (bf16[48,2048]{1,0:T(8,128)(2,1)S(1)}, bf16[48,2048]{1,0:T(8,128)(2,1)S(1)}, u32[]{:S(2)}, u32[]{:S(2)}) collective-permute-start(bf16[48,2048]{1,0:T(8,128)(2,1)S(1)} %collective-permute-done.9.refs_8_), channel_id=1, source_target_pairs={{0,224},{32,0},{64,32},{96,64},{128,96},{160,128},{192,160},{224,1... | collective-permute-start | bytes 589832 | tf_op jit(solution)/shard_map/ppermute | solution.py:208
  27.3 0.7 %collective-permute-done.4.after1.refs_0_ = bf16[48,2048]{1,0:T(8,128)(2,1)S(1)} collective-permute-done((bf16[48,2048]{1,0:T(8,128)(2,1)S(1)}, bf16[48,2048]{1,0:T(8,128)(2,1)S(1)}, u32[]{:S(2)}, u32[]{:S(2)}) %collective-permute-start.4) | collective-permute-done | bytes 196640 | tf_op jit(solution)/shard_map/ppermute | solution.py:206
  28.0 2.8 %collective-permute-start.13 = (bf16[48,2048]{1,0:T(8,128)(2,1)S(1)}, bf16[48,2048]{1,0:T(8,128)(2,1)S(1)}, u32[]{:S(2)}, u32[]{:S(2)}) collective-permute-start(bf16[48,2048]{1,0:T(8,128)(2,1)S(1)} %collective-permute-done.7.after2.refs_3_), channel_id=1, source_target_pairs={{0,224},{32,0},{64,32},{96,64},{128,96},{160,128},{192,160},{224,1... | collective-permute-start | bytes 589832 | tf_op jit(solution)/shard_map/ppermute | solution.py:223
  30.8 2.8 %shard_map.111 = (f32[10,96,128]{2,1,0:T(8,128)S(1)}, f32[10,96,128]{2,1,0:T(8,128)S(1)}) custom-call(s32[2]{0:T(128)S(1)} %pad_add_fusion.where, f32[8,128]{1,0:T(8,128)S(1)} %get-tuple-element.31.ready, bf16[2048,1024]{1,0:T(8,128)(2,1)S(1)} %get-tuple-element.32.low, bf16[2048,1024]{1,0:T(8,128)(2,1)S(1)} %get-tuple-element.33.high, ...), custom_call_target="tpu_custom_call" | custom-call | tf_op jit(solution)/shard_map/pallas_call | solution.py:119
  33.6 3.0 %collective-permute-done.12.refs_4_ = bf16[48,2048]{1,0:T(8,128)(2,1)S(1)} collective-permute-done((bf16[48,2048]{1,0:T(8,128)(2,1)S(1)}, bf16[48,2048]{1,0:T(8,128)(2,1)S(1)}, u32[]{:S(2)}, u32[]{:S(2)}) %collective-permute-start.12) | collective-permute-done | bytes 196640 | tf_op jit(solution)/shard_map/ppermute | solution.py:223
  36.7 3.6 %collective-permute-start.14 = (f32[10,96,128]{2,1,0:T(8,128)S(1)}, f32[10,96,128]{2,1,0:T(8,128)S(1)}, u32[]{:S(2)}, u32[]{:S(2)}) collective-permute-start(f32[10,96,128]{2,1,0:T(8,128)S(1)} %get-tuple-element.41), channel_id=1, source_target_pairs={{0,1},{1,0},{2,3},{3,2},{4,5},{5,4},{6,7},{7,6},{8,9},{9,8},{10,11... | collective-permute-start | bytes 1474568 | tf_op jit(solution)/shard_map/ppermute | solution.py:235
  40.3 2.0 %shard_map.113 = (f32[6,96,128]{2,1,0:T(8,128)S(1)}, f32[6,96,128]{2,1,0:T(8,128)S(1)}) custom-call(s32[2]{0:T(128)S(1)} %pad_add_fusion.where, f32[8,128]{1,0:T(8,128)S(1)} %shard_map.112.ready, bf16[2048,1024]{1,0:T(8,128)(2,1)S(1)} %get-tuple-element.32.low, bf16[2048,1024]{1,0:T(8,128)(2,1)S(1)} %get-tuple-element.33.high, ...), custom_call_target="tpu_custom_call" | custom-call | tf_op jit(solution)/shard_map/pallas_call | solution.py:119
  42.3 0.1 collective-permute-start.15
  42.4 1.6 %collective-permute-done.15.last_got = f32[6,96,128]{2,1,0:T(8,128)S(1)} collective-permute-done((f32[6,96,128]{2,1,0:T(8,128)S(1)}, f32[6,96,128]{2,1,0:T(8,128)S(1)}, u32[]{:S(2)}, u32[]{:S(2)}) %collective-permute-start.15) | collective-permute-done | bytes 294944 | tf_op jit(solution)/shard_map/ppermute | solution.py:237
  43.9 0.8 %shard_map.114 = s16[16,112,128]{2,1,0:T(8,128)(2,1)S(1)} custom-call(s32[2]{0:T(128)S(1)} %pad_add_fusion.where, f32[10,96,128]{2,1,0:T(8,128)S(1)} %get-tuple-element.35.after3.first_keep, f32[6,96,128]{2,1,0:T(8,128)S(1)} %get-tuple-element.40.last_keep, f32[10,96,128]{2,1,0:T(8,128)S(1)} %collective-permute-done.14.first_got, ...), custom_call_target="tpu_custom_call" | custom-call | tf_op jit(solution)/shard_map/pallas_call | solution.py:238
  44.7 16.8 %all_to_all.5.parts = s16[16,112,128]{2,1,0:T(8,128)(2,1)S(1)} all-to-all(s16[16,112,128]{2,1,0:T(8,128)(2,1)S(1)} %shard_map.114), channel_id=1, replica_groups=mesh['z'=8,'y'=4,'x'=4,'core'=2] {'y','x'}, dimensions={0} | all-to-all | bytes 917504 | tf_op jit(solution)/shard_map/all_to_all | solution.py:246
  61.5 0.8 %shard_map.115 = f32[12,1024]{1,0:T(8,128)} custom-call(s16[16,112,128]{2,1,0:T(8,128)(2,1)S(1)} %all_to_all.5.parts, f32[8,128]{1,0:T(8,128)S(1)} %get-tuple-element.43.virt, f32[16,128]{1,0:T(8,128)S(1)} %get-tuple-element.44.occ), custom_call_target="tpu_custom_call" | custom-call | tf_op jit(solution)/shard_map/pallas_call | solution.py:247
  (18 shorter events, 0.1 us)
Async XLA Ops:
  1.1 12.7 %collective-permute-start = (bf16[48,2048]{1,0:T(8,128)(2,1)S(1)}, bf16[48,2048]{1,0:T(8,128)(2,1)S(1)}, u32[]{:S(2)}, u32[]{:S(2)}) collective-permute-start(bf16[48,2048]{1,0:T(8,128)(2,1)S(1)} %get-tuple-element.46.refs_0_), channel_id=1, source_target_pairs={{0,32},{32,64},{64,96},{96,128},{128,160},{160,192},{192,224},{224... | collective-permute-start | bytes 589832 | tf_op jit(solution)/shard_map/ppermute | solution.py:206
  3.6 10.2 %collective-permute-start.5 = (bf16[48,2048]{1,0:T(8,128)(2,1)S(1)}, bf16[48,2048]{1,0:T(8,128)(2,1)S(1)}, u32[]{:S(2)}, u32[]{:S(2)}) collective-permute-start(bf16[48,2048]{1,0:T(8,128)(2,1)S(1)} %get-tuple-element.45.refs_1_), channel_id=1, source_target_pairs={{0,224},{32,0},{64,32},{96,64},{128,96},{160,128},{192,160},{224,1... | collective-permute-start | bytes 589832 | tf_op jit(solution)/shard_map/ppermute | solution.py:209
  7.6 8.9 %collective-permute-start.2 = (bf16[48,2048]{1,0:T(8,128)(2,1)S(1)}, bf16[48,2048]{1,0:T(8,128)(2,1)S(1)}, u32[]{:S(2)}, u32[]{:S(2)}) collective-permute-start(bf16[48,2048]{1,0:T(8,128)(2,1)S(1)} %get-tuple-element.45.refs_1_), channel_id=1, source_target_pairs={{0,32},{32,64},{64,96},{96,128},{128,160},{160,192},{192,224},{224... | collective-permute-start | bytes 589832 | tf_op jit(solution)/shard_map/ppermute | solution.py:207
  7.6 8.9 %collective-permute-start.3 = (bf16[48,2048]{1,0:T(8,128)(2,1)S(1)}, bf16[48,2048]{1,0:T(8,128)(2,1)S(1)}, u32[]{:S(2)}, u32[]{:S(2)}) collective-permute-start(bf16[48,2048]{1,0:T(8,128)(2,1)S(1)} %get-tuple-element.46.refs_0_), channel_id=1, source_target_pairs={{0,224},{32,0},{64,32},{96,64},{128,96},{160,128},{192,160},{224,1... | collective-permute-start | bytes 589832 | tf_op jit(solution)/shard_map/ppermute | solution.py:208
  13.7 7.9 %collective-permute-start.1 = (bf16[48,2048]{1,0:T(8,128)(2,1)S(1)}, bf16[48,2048]{1,0:T(8,128)(2,1)S(1)}, u32[]{:S(2)}, u32[]{:S(2)}) collective-permute-start(bf16[48,2048]{1,0:T(8,128)(2,1)S(1)} %collective-permute-done.refs_2_), channel_id=1, source_target_pairs={{0,32},{32,64},{64,96},{96,128},{128,160},{160,192},{192,224},{224... | collective-permute-start | bytes 589832 | tf_op jit(solution)/shard_map/ppermute | solution.py:206
  13.8 7.9 %collective-permute-start.6 = (bf16[48,2048]{1,0:T(8,128)(2,1)S(1)}, bf16[48,2048]{1,0:T(8,128)(2,1)S(1)}, u32[]{:S(2)}, u32[]{:S(2)}) collective-permute-start(bf16[48,2048]{1,0:T(8,128)(2,1)S(1)} %collective-permute-done.5.refs_5_), channel_id=1, source_target_pairs={{0,224},{32,0},{64,32},{96,64},{128,96},{160,128},{192,160},{224,1... | collective-permute-start | bytes 589832 | tf_op jit(solution)/shard_map/ppermute | solution.py:209
  16.5 8.1 %collective-permute-start.8 = (bf16[48,2048]{1,0:T(8,128)(2,1)S(1)}, bf16[48,2048]{1,0:T(8,128)(2,1)S(1)}, u32[]{:S(2)}, u32[]{:S(2)}) collective-permute-start(bf16[48,2048]{1,0:T(8,128)(2,1)S(1)} %collective-permute-done.2.after1.refs_3_), channel_id=1, source_target_pairs={{0,32},{32,64},{64,96},{96,128},{128,160},{160,192},{192,224},{224... | collective-permute-start | bytes 589832 | tf_op jit(solution)/shard_map/ppermute | solution.py:207
  16.5 8.1 %collective-permute-start.9 = (bf16[48,2048]{1,0:T(8,128)(2,1)S(1)}, bf16[48,2048]{1,0:T(8,128)(2,1)S(1)}, u32[]{:S(2)}, u32[]{:S(2)}) collective-permute-start(bf16[48,2048]{1,0:T(8,128)(2,1)S(1)} %collective-permute-done.3.after2.refs_4_), channel_id=1, source_target_pairs={{0,224},{32,0},{64,32},{96,64},{128,96},{160,128},{192,160},{224,1... | collective-permute-start | bytes 589832 | tf_op jit(solution)/shard_map/ppermute | solution.py:208
  21.7 6.3 %collective-permute-start.4 = (bf16[48,2048]{1,0:T(8,128)(2,1)S(1)}, bf16[48,2048]{1,0:T(8,128)(2,1)S(1)}, u32[]{:S(2)}, u32[]{:S(2)}) collective-permute-start(bf16[48,2048]{1,0:T(8,128)(2,1)S(1)} %collective-permute-done.1.refs_6_), channel_id=1, source_target_pairs={{0,32},{32,64},{64,96},{96,128},{128,160},{160,192},{192,224},{224... | collective-permute-start | bytes 589832 | tf_op jit(solution)/shard_map/ppermute | solution.py:206
  21.8 6.2 %collective-permute-start.7 = (bf16[48,2048]{1,0:T(8,128)(2,1)S(1)}, bf16[48,2048]{1,0:T(8,128)(2,1)S(1)}, u32[]{:S(2)}, u32[]{:S(2)}) collective-permute-start(bf16[48,2048]{1,0:T(8,128)(2,1)S(1)} %collective-permute-done.6.refs_9_), channel_id=1, source_target_pairs={{0,224},{32,0},{64,32},{96,64},{128,96},{160,128},{192,160},{224,1... | collective-permute-start | bytes 589832 | tf_op jit(solution)/shard_map/ppermute | solution.py:209
  24.6 9.0 %collective-permute-start.10 = (bf16[48,2048]{1,0:T(8,128)(2,1)S(1)}, bf16[48,2048]{1,0:T(8,128)(2,1)S(1)}, u32[]{:S(2)}, u32[]{:S(2)}) collective-permute-start(bf16[48,2048]{1,0:T(8,128)(2,1)S(1)} %collective-permute-done.8.refs_7_), channel_id=1, source_target_pairs={{0,32},{32,64},{64,96},{96,128},{128,160},{160,192},{192,224},{224... | collective-permute-start | bytes 589832 | tf_op jit(solution)/shard_map/ppermute | solution.py:207
  24.6 9.0 %collective-permute-start.11 = (bf16[48,2048]{1,0:T(8,128)(2,1)S(1)}, bf16[48,2048]{1,0:T(8,128)(2,1)S(1)}, u32[]{:S(2)}, u32[]{:S(2)}) collective-permute-start(bf16[48,2048]{1,0:T(8,128)(2,1)S(1)} %collective-permute-done.9.refs_8_), channel_id=1, source_target_pairs={{0,224},{32,0},{64,32},{96,64},{128,96},{160,128},{192,160},{224,1... | collective-permute-start | bytes 589832 | tf_op jit(solution)/shard_map/ppermute | solution.py:208
  28.0 8.7 %collective-permute-start.12 = (bf16[48,2048]{1,0:T(8,128)(2,1)S(1)}, bf16[48,2048]{1,0:T(8,128)(2,1)S(1)}, u32[]{:S(2)}, u32[]{:S(2)}) collective-permute-start(bf16[48,2048]{1,0:T(8,128)(2,1)S(1)} %collective-permute-done.4.after1.refs_0_), channel_id=1, source_target_pairs={{0,32},{32,64},{64,96},{96,128},{128,160},{160,192},{192,224},{224... | collective-permute-start | bytes 589832 | tf_op jit(solution)/shard_map/ppermute | solution.py:223
  28.0 8.7 %collective-permute-start.13 = (bf16[48,2048]{1,0:T(8,128)(2,1)S(1)}, bf16[48,2048]{1,0:T(8,128)(2,1)S(1)}, u32[]{:S(2)}, u32[]{:S(2)}) collective-permute-start(bf16[48,2048]{1,0:T(8,128)(2,1)S(1)} %collective-permute-done.7.after2.refs_3_), channel_id=1, source_target_pairs={{0,224},{32,0},{64,32},{96,64},{128,96},{160,128},{192,160},{224,1... | collective-permute-start | bytes 589832 | tf_op jit(solution)/shard_map/ppermute | solution.py:223
  36.7 7.3 %collective-permute-start.14 = (f32[10,96,128]{2,1,0:T(8,128)S(1)}, f32[10,96,128]{2,1,0:T(8,128)S(1)}, u32[]{:S(2)}, u32[]{:S(2)}) collective-permute-start(f32[10,96,128]{2,1,0:T(8,128)S(1)} %get-tuple-element.41), channel_id=1, source_target_pairs={{0,1},{1,0},{2,3},{3,2},{4,5},{5,4},{6,7},{7,6},{8,9},{9,8},{10,11... | collective-permute-start | bytes 1474568 | tf_op jit(solution)/shard_map/ppermute | solution.py:235
  42.3 1.7 %collective-permute-start.15 = (f32[6,96,128]{2,1,0:T(8,128)S(1)}, f32[6,96,128]{2,1,0:T(8,128)S(1)}, u32[]{:S(2)}, u32[]{:S(2)}) collective-permute-start(f32[6,96,128]{2,1,0:T(8,128)S(1)} %get-tuple-element.42), channel_id=1, source_target_pairs={{0,1},{1,0},{2,3},{3,2},{4,5},{5,4},{6,7},{7,6},{8,9},{9,8},{10,11... | collective-permute-start | bytes 884744 | tf_op jit(solution)/shard_map/ppermute | solution.py:237

commit v11 on v10

--- a/solution.py
+++ b/solution.py
@@ -209,6 +209,7 @@
         down[1] = lax.ppermute(down[1], "z", backward)
         if hop == 0:
             up[0], cd, where = lax.optimization_barrier((up[0], cd, where))
+        if hop == 1:
             high, ready = pl.pallas_call(
                 high_kernel,
                 out_shape=(half, lines),
@@ -217,7 +218,7 @@
                 scratch_shapes=[pltpu.SemaphoreType.DMA((4,))],
                 compiler_params=pltpu.CompilerParams(vmem_limit_bytes=4 * MIB),
             )(cd, ab, tables[-1], up[1], down[0])
-        if hop == 1:
+        if hop == 2:
             up[0], ready = lax.optimization_barrier((up[0], ready))
         pieces += up + down
     last = [lax.ppermute(up[0], "z", forward), lax.ppermute(down[1], "z", backward)]

time: 62.9 us -> 63.9 us (1.016)
  starting transfers between devices: 26.6 us -> 27.7 us
    ppermute x1, waiting for transfers between devices: 3 us -> 0.86 us  [on_device(): lax.ppermute(up[0], 'z', forward)]
    ppermute x3, waiting for transfers between devices: 0.15 us -> 2.01 us  [on_device(): up[1] = lax.ppermute(up[1], 'z', forward)]
    ppermute x1, starting transfers between devices: 3.6 us -> 4.64 us  [on_device(): got = lax.ppermute(send, 'core', swap)]
where the time goes in v11:
time: 63.9 us; the launch traced here: 63 us
  starting transfers between devices  27.7 us (43%)
  blocking collectives  16.8 us (26%)
  Pallas kernels  12.2 us (19%)
  waiting for transfers between devices  5.19 us (8%)
  local copies, waits for them, and re-layouts  1.05 us (2%)
    all_to_all x1, blocking collectives, on_device(): parts = lax.all_to_all(packed, ('y', 'x'), 0, 0, tiled=True)  16.8 us
    ppermute x3, starting transfers between devices, on_device(): down[1] = lax.ppermute(down[1], 'z', backward)  9.36 us
    ppermute x3, starting transfers between devices, on_device(): down[0] = lax.ppermute(down[0], 'z', backward)  8.02 us
    pallas_call x2, Pallas kernels, ladder(): pl.pallas_call(ladder_kernel, out_shape=(block, block), grid_spec=pltpu.P...  4.81 us
    ppermute x1, starting transfers between devices, on_device(): got = lax.ppermute(send, 'core', swap)  4.64 us
    pallas_call x1, Pallas kernels, on_device(): pl.pallas_call(low_kernel, out_shape=(half, pltpu.VMEM((depth // LANES //...  3.33 us
    ppermute x1, starting transfers between devices, on_device(): lax.ppermute(down[1], 'z', backward)  2.66 us
    ppermute x3, starting transfers between devices, on_device(): up[0] = lax.ppermute(up[0], 'z', forward)  2.63 us
  transfers between devices with their start and end apart: 16, of which 4 were waited for; matrix products, arithmetic and copies ran while one was open for 0% of the time, Pallas kernels for 17%

profile of v11, /device:TPU:1, one launch (start us, length us, event | category | flops | bytes accessed | tf_op | source)
XLA Modules:
  0.0 63.0 jit_solution(10293240351218619547)
XLA Ops:
  0.0 1.0 %fusion = (bf16[48,2048]{1,0:T(8,128)(2,1)S(1)}, bf16[48,2048]{1,0:T(8,128)(2,1)S(1)}) fusion(bf16[48,4096]{1,0:T(8,128)(2,1)} %param.11), kind=kLoop, calls=%fused_computation.1 | loop fusion | bytes 786432 | tf_op jit(solution)/shard_map/slice | solution.py:202
  1.1 2.5 %collective-permute-start = (bf16[48,2048]{1,0:T(8,128)(2,1)S(1)}, bf16[48,2048]{1,0:T(8,128)(2,1)S(1)}, u32[]{:S(2)}, u32[]{:S(2)}) collective-permute-start(bf16[48,2048]{1,0:T(8,128)(2,1)S(1)} %get-tuple-element.46.refs_0_), channel_id=1, source_target_pairs={{0,32},{32,64},{64,96},{96,128},{128,160},{160,192},{192,224},{224... | collective-permute-start | bytes 589832 | tf_op jit(solution)/shard_map/ppermute | solution.py:206
  3.6 4.0 %collective-permute-start.7 = (bf16[48,2048]{1,0:T(8,128)(2,1)S(1)}, bf16[48,2048]{1,0:T(8,128)(2,1)S(1)}, u32[]{:S(2)}, u32[]{:S(2)}) collective-permute-start(bf16[48,2048]{1,0:T(8,128)(2,1)S(1)} %get-tuple-element.45.refs_1_), channel_id=1, source_target_pairs={{0,224},{32,0},{64,32},{96,64},{128,96},{160,128},{192,160},{224,1... | collective-permute-start | bytes 589832 | tf_op jit(solution)/shard_map/ppermute | solution.py:209
  7.6 2.7 %collective-permute-start.5 = (bf16[48,2048]{1,0:T(8,128)(2,1)S(1)}, bf16[48,2048]{1,0:T(8,128)(2,1)S(1)}, u32[]{:S(2)}, u32[]{:S(2)}) collective-permute-start(bf16[48,2048]{1,0:T(8,128)(2,1)S(1)} %get-tuple-element.46.refs_0_), channel_id=1, source_target_pairs={{0,224},{32,0},{64,32},{96,64},{128,96},{160,128},{192,160},{224,1... | collective-permute-start | bytes 589832 | tf_op jit(solution)/shard_map/ppermute | solution.py:208
  10.4 3.3 %shard_map.109 = (bf16[2048,1024]{1,0:T(8,128)(2,1)S(1)}, f32[16,128]{1,0:T(8,128)S(1)}, f32[8,128]{1,0:T(8,128)S(1)}, f32[8,128]{1,0:T(8,128)S(1)}, f32[16,128]{1,0:T(8,128)S(1)}) custom-call(s32[32,128]{1,0:T(8,128)} %bitcast.6, s32[32,128]{1,0:T(8,128)} %bitcast.7, s32[8,128]{1,0:T(8,128)} %bitcast.8, s32[8,128]{1,0:T(8,128)} %bitcast.9, s32[12]{0:T(128)} %occ1.1, ...), custom_call_target="tpu_custom_call" | custom-call | tf_op jit(solution)/shard_map/pallas_call | solution.py:184
  13.7 0.1 collective-permute-start.1
  13.8 2.7 %collective-permute-start.8 = (bf16[48,2048]{1,0:T(8,128)(2,1)S(1)}, bf16[48,2048]{1,0:T(8,128)(2,1)S(1)}, u32[]{:S(2)}, u32[]{:S(2)}) collective-permute-start(bf16[48,2048]{1,0:T(8,128)(2,1)S(1)} %collective-permute-done.7.refs_5_), channel_id=1, source_target_pairs={{0,224},{32,0},{64,32},{96,64},{128,96},{160,128},{192,160},{224,1... | collective-permute-start | bytes 589832 | tf_op jit(solution)/shard_map/ppermute | solution.py:209
  16.5 2.7 %collective-permute-start.6 = (bf16[48,2048]{1,0:T(8,128)(2,1)S(1)}, bf16[48,2048]{1,0:T(8,128)(2,1)S(1)}, u32[]{:S(2)}, u32[]{:S(2)}) collective-permute-start(bf16[48,2048]{1,0:T(8,128)(2,1)S(1)} %collective-permute-done.5.refs_4_), channel_id=1, source_target_pairs={{0,224},{32,0},{64,32},{96,64},{128,96},{160,128},{192,160},{224,1... | collective-permute-start | bytes 589832 | tf_op jit(solution)/shard_map/ppermute | solution.py:208
  19.2 0.7 %collective-permute-done.1.refs_6_ = bf16[48,2048]{1,0:T(8,128)(2,1)S(1)} collective-permute-done((bf16[48,2048]{1,0:T(8,128)(2,1)S(1)}, bf16[48,2048]{1,0:T(8,128)(2,1)S(1)}, u32[]{:S(2)}, u32[]{:S(2)}) %collective-permute-start.1) | collective-permute-done | bytes 196640 | tf_op jit(solution)/shard_map/ppermute | solution.py:206
  19.9 2.7 %collective-permute-start.9 = (bf16[48,2048]{1,0:T(8,128)(2,1)S(1)}, bf16[48,2048]{1,0:T(8,128)(2,1)S(1)}, u32[]{:S(2)}, u32[]{:S(2)}) collective-permute-start(bf16[48,2048]{1,0:T(8,128)(2,1)S(1)} %collective-permute-done.8.refs_9_), channel_id=1, source_target_pairs={{0,224},{32,0},{64,32},{96,64},{128,96},{160,128},{192,160},{224,1... | collective-permute-start | bytes 589832 | tf_op jit(solution)/shard_map/ppermute | solution.py:209
  22.6 2.0 %collective-permute-done.4.after1.refs_7_ = bf16[48,2048]{1,0:T(8,128)(2,1)S(1)} collective-permute-done((bf16[48,2048]{1,0:T(8,128)(2,1)S(1)}, bf16[48,2048]{1,0:T(8,128)(2,1)S(1)}, u32[]{:S(2)}, u32[]{:S(2)}) %collective-permute-start.4) | collective-permute-done | bytes 196640 | tf_op jit(solution)/shard_map/ppermute | solution.py:207
  24.6 2.7 %collective-permute-start.11 = (bf16[48,2048]{1,0:T(8,128)(2,1)S(1)}, bf16[48,2048]{1,0:T(8,128)(2,1)S(1)}, u32[]{:S(2)}, u32[]{:S(2)}) collective-permute-start(bf16[48,2048]{1,0:T(8,128)(2,1)S(1)} %collective-permute-done.6.after2.refs_8_), channel_id=1, source_target_pairs={{0,224},{32,0},{64,32},{96,64},{128,96},{160,128},{192,160},{224,1... | collective-permute-start | bytes 589832 | tf_op jit(solution)/shard_map/ppermute | solution.py:208
  27.3 2.5 %shard_map.110 = (bf16[2048,1024]{1,0:T(8,128)(2,1)S(1)}, f32[8,128]{1,0:T(8,128)S(1)}) custom-call(f32[16,128]{1,0:T(8,128)S(1)} %get-tuple-element.28.cd, f32[8,128]{1,0:T(8,128)S(1)} %get-tuple-element.29.ab, bf16[4096,1024]{1,0:T(8,128)(2,1)} %values.3, bf16[48,2048]{1,0:T(8,128)(2,1)S(1)} %collective-permute-done.4.after1.refs_7_, ...), custom_call_target="tpu_custom_call" | custom-call | tf_op jit(solution)/shard_map/pallas_call | solution.py:213
  29.8 0.3 collective-permute-start.12
  30.0 2.7 %collective-permute-start.13 = (bf16[48,2048]{1,0:T(8,128)(2,1)S(1)}, bf16[48,2048]{1,0:T(8,128)(2,1)S(1)}, u32[]{:S(2)}, u32[]{:S(2)}) collective-permute-start(bf16[48,2048]{1,0:T(8,128)(2,1)S(1)} %collective-permute-done.9.after2.refs_3_), channel_id=1, source_target_pairs={{0,224},{32,0},{64,32},{96,64},{128,96},{160,128},{192,160},{224,1... | collective-permute-start | bytes 589832 | tf_op jit(solution)/shard_map/ppermute | solution.py:224
  32.7 2.8 %shard_map.111 = (f32[10,96,128]{2,1,0:T(8,128)S(1)}, f32[10,96,128]{2,1,0:T(8,128)S(1)}) custom-call(s32[2]{0:T(128)S(1)} %pad_add_fusion.where, f32[8,128]{1,0:T(8,128)S(1)} %get-tuple-element.31.ready, bf16[2048,1024]{1,0:T(8,128)(2,1)S(1)} %get-tuple-element.32.low, bf16[2048,1024]{1,0:T(8,128)(2,1)S(1)} %get-tuple-element.33.high, ...), custom_call_target="tpu_custom_call" | custom-call | tf_op jit(solution)/shard_map/pallas_call | solution.py:119
  35.6 0.9 %collective-permute-done.12.refs_4_ = bf16[48,2048]{1,0:T(8,128)(2,1)S(1)} collective-permute-done((bf16[48,2048]{1,0:T(8,128)(2,1)S(1)}, bf16[48,2048]{1,0:T(8,128)(2,1)S(1)}, u32[]{:S(2)}, u32[]{:S(2)}) %collective-permute-start.12) | collective-permute-done | bytes 196640 | tf_op jit(solution)/shard_map/ppermute | solution.py:224
  36.4 4.6 %collective-permute-start.14 = (f32[10,96,128]{2,1,0:T(8,128)S(1)}, f32[10,96,128]{2,1,0:T(8,128)S(1)}, u32[]{:S(2)}, u32[]{:S(2)}) collective-permute-start(f32[10,96,128]{2,1,0:T(8,128)S(1)} %get-tuple-element.41), channel_id=1, source_target_pairs={{0,1},{1,0},{2,3},{3,2},{4,5},{5,4},{6,7},{7,6},{8,9},{9,8},{10,11... | collective-permute-start | bytes 1474568 | tf_op jit(solution)/shard_map/ppermute | solution.py:236
  41.1 2.0 %shard_map.113 = (f32[6,96,128]{2,1,0:T(8,128)S(1)}, f32[6,96,128]{2,1,0:T(8,128)S(1)}) custom-call(s32[2]{0:T(128)S(1)} %pad_add_fusion.where, f32[8,128]{1,0:T(8,128)S(1)} %shard_map.112.ready, bf16[2048,1024]{1,0:T(8,128)(2,1)S(1)} %get-tuple-element.32.low, bf16[2048,1024]{1,0:T(8,128)(2,1)S(1)} %get-tuple-element.33.high, ...), custom_call_target="tpu_custom_call" | custom-call | tf_op jit(solution)/shard_map/pallas_call | solution.py:119
  43.1 0.1 collective-permute-start.15
  43.2 1.6 %collective-permute-done.15.last_got = f32[6,96,128]{2,1,0:T(8,128)S(1)} collective-permute-done((f32[6,96,128]{2,1,0:T(8,128)S(1)}, f32[6,96,128]{2,1,0:T(8,128)S(1)}, u32[]{:S(2)}, u32[]{:S(2)}) %collective-permute-start.15) | collective-permute-done | bytes 294944 | tf_op jit(solution)/shard_map/ppermute | solution.py:238
  44.7 0.8 %shard_map.114 = s16[16,112,128]{2,1,0:T(8,128)(2,1)S(1)} custom-call(s32[2]{0:T(128)S(1)} %pad_add_fusion.where, f32[10,96,128]{2,1,0:T(8,128)S(1)} %get-tuple-element.35.after3.first_keep, f32[6,96,128]{2,1,0:T(8,128)S(1)} %get-tuple-element.40.last_keep, f32[10,96,128]{2,1,0:T(8,128)S(1)} %collective-permute-done.14.first_got, ...), custom_call_target="tpu_custom_call" | custom-call | tf_op jit(solution)/shard_map/pallas_call | solution.py:239
  45.5 16.8 %all_to_all.5.parts = s16[16,112,128]{2,1,0:T(8,128)(2,1)S(1)} all-to-all(s16[16,112,128]{2,1,0:T(8,128)(2,1)S(1)} %shard_map.114), channel_id=1, replica_groups=mesh['z'=8,'y'=4,'x'=4,'core'=2] {'y','x'}, dimensions={0} | all-to-all | bytes 917504 | tf_op jit(solution)/shard_map/all_to_all | solution.py:247
  62.3 0.8 %shard_map.115 = f32[12,1024]{1,0:T(8,128)} custom-call(s16[16,112,128]{2,1,0:T(8,128)(2,1)S(1)} %all_to_all.5.parts, f32[8,128]{1,0:T(8,128)S(1)} %get-tuple-element.43.virt, f32[16,128]{1,0:T(8,128)S(1)} %get-tuple-element.44.occ), custom_call_target="tpu_custom_call" | custom-call | tf_op jit(solution)/shard_map/pallas_call | solution.py:248
  (18 shorter events, 0.1 us)
Async XLA Ops:
  1.1 12.7 %collective-permute-start = (bf16[48,2048]{1,0:T(8,128)(2,1)S(1)}, bf16[48,2048]{1,0:T(8,128)(2,1)S(1)}, u32[]{:S(2)}, u32[]{:S(2)}) collective-permute-start(bf16[48,2048]{1,0:T(8,128)(2,1)S(1)} %get-tuple-element.46.refs_0_), channel_id=1, source_target_pairs={{0,32},{32,64},{64,96},{96,128},{128,160},{160,192},{192,224},{224... | collective-permute-start | bytes 589832 | tf_op jit(solution)/shard_map/ppermute | solution.py:206
  3.6 10.2 %collective-permute-start.7 = (bf16[48,2048]{1,0:T(8,128)(2,1)S(1)}, bf16[48,2048]{1,0:T(8,128)(2,1)S(1)}, u32[]{:S(2)}, u32[]{:S(2)}) collective-permute-start(bf16[48,2048]{1,0:T(8,128)(2,1)S(1)} %get-tuple-element.45.refs_1_), channel_id=1, source_target_pairs={{0,224},{32,0},{64,32},{96,64},{128,96},{160,128},{192,160},{224,1... | collective-permute-start | bytes 589832 | tf_op jit(solution)/shard_map/ppermute | solution.py:209
  7.6 8.9 %collective-permute-start.3 = (bf16[48,2048]{1,0:T(8,128)(2,1)S(1)}, bf16[48,2048]{1,0:T(8,128)(2,1)S(1)}, u32[]{:S(2)}, u32[]{:S(2)}) collective-permute-start(bf16[48,2048]{1,0:T(8,128)(2,1)S(1)} %get-tuple-element.45.refs_1_), channel_id=1, source_target_pairs={{0,32},{32,64},{64,96},{96,128},{128,160},{160,192},{192,224},{224... | collective-permute-start | bytes 589832 | tf_op jit(solution)/shard_map/ppermute | solution.py:207
  7.6 8.9 %collective-permute-start.5 = (bf16[48,2048]{1,0:T(8,128)(2,1)S(1)}, bf16[48,2048]{1,0:T(8,128)(2,1)S(1)}, u32[]{:S(2)}, u32[]{:S(2)}) collective-permute-start(bf16[48,2048]{1,0:T(8,128)(2,1)S(1)} %get-tuple-element.46.refs_0_), channel_id=1, source_target_pairs={{0,224},{32,0},{64,32},{96,64},{128,96},{160,128},{192,160},{224,1... | collective-permute-start | bytes 589832 | tf_op jit(solution)/shard_map/ppermute | solution.py:208
  13.7 6.2 %collective-permute-start.1 = (bf16[48,2048]{1,0:T(8,128)(2,1)S(1)}, bf16[48,2048]{1,0:T(8,128)(2,1)S(1)}, u32[]{:S(2)}, u32[]{:S(2)}) collective-permute-start(bf16[48,2048]{1,0:T(8,128)(2,1)S(1)} %collective-permute-done.refs_2_), channel_id=1, source_target_pairs={{0,32},{32,64},{64,96},{96,128},{128,160},{160,192},{192,224},{224... | collective-permute-start | bytes 589832 | tf_op jit(solution)/shard_map/ppermute | solution.py:206
  13.8 6.1 %collective-permute-start.8 = (bf16[48,2048]{1,0:T(8,128)(2,1)S(1)}, bf16[48,2048]{1,0:T(8,128)(2,1)S(1)}, u32[]{:S(2)}, u32[]{:S(2)}) collective-permute-start(bf16[48,2048]{1,0:T(8,128)(2,1)S(1)} %collective-permute-done.7.refs_5_), channel_id=1, source_target_pairs={{0,224},{32,0},{64,32},{96,64},{128,96},{160,128},{192,160},{224,1... | collective-permute-start | bytes 589832 | tf_op jit(solution)/shard_map/ppermute | solution.py:209
  16.5 8.1 %collective-permute-start.4 = (bf16[48,2048]{1,0:T(8,128)(2,1)S(1)}, bf16[48,2048]{1,0:T(8,128)(2,1)S(1)}, u32[]{:S(2)}, u32[]{:S(2)}) collective-permute-start(bf16[48,2048]{1,0:T(8,128)(2,1)S(1)} %collective-permute-done.3.refs_3_), channel_id=1, source_target_pairs={{0,32},{32,64},{64,96},{96,128},{128,160},{160,192},{192,224},{224... | collective-permute-start | bytes 589832 | tf_op jit(solution)/shard_map/ppermute | solution.py:207
  16.5 8.1 %collective-permute-start.6 = (bf16[48,2048]{1,0:T(8,128)(2,1)S(1)}, bf16[48,2048]{1,0:T(8,128)(2,1)S(1)}, u32[]{:S(2)}, u32[]{:S(2)}) collective-permute-start(bf16[48,2048]{1,0:T(8,128)(2,1)S(1)} %collective-permute-done.5.refs_4_), channel_id=1, source_target_pairs={{0,224},{32,0},{64,32},{96,64},{128,96},{160,128},{192,160},{224,1... | collective-permute-start | bytes 589832 | tf_op jit(solution)/shard_map/ppermute | solution.py:208
  19.9 9.9 %collective-permute-start.2 = (bf16[48,2048]{1,0:T(8,128)(2,1)S(1)}, bf16[48,2048]{1,0:T(8,128)(2,1)S(1)}, u32[]{:S(2)}, u32[]{:S(2)}) collective-permute-start(bf16[48,2048]{1,0:T(8,128)(2,1)S(1)} %collective-permute-done.1.refs_6_), channel_id=1, source_target_pairs={{0,32},{32,64},{64,96},{96,128},{128,160},{160,192},{192,224},{224... | collective-permute-start | bytes 589832 | tf_op jit(solution)/shard_map/ppermute | solution.py:206
  19.9 10.1 %collective-permute-start.9 = (bf16[48,2048]{1,0:T(8,128)(2,1)S(1)}, bf16[48,2048]{1,0:T(8,128)(2,1)S(1)}, u32[]{:S(2)}, u32[]{:S(2)}) collective-permute-start(bf16[48,2048]{1,0:T(8,128)(2,1)S(1)} %collective-permute-done.8.refs_9_), channel_id=1, source_target_pairs={{0,224},{32,0},{64,32},{96,64},{128,96},{160,128},{192,160},{224,1... | collective-permute-start | bytes 589832 | tf_op jit(solution)/shard_map/ppermute | solution.py:209
  24.6 10.9 %collective-permute-start.10 = (bf16[48,2048]{1,0:T(8,128)(2,1)S(1)}, bf16[48,2048]{1,0:T(8,128)(2,1)S(1)}, u32[]{:S(2)}, u32[]{:S(2)}) collective-permute-start(bf16[48,2048]{1,0:T(8,128)(2,1)S(1)} %collective-permute-done.4.after1.refs_7_), channel_id=1, source_target_pairs={{0,32},{32,64},{64,96},{96,128},{128,160},{160,192},{192,224},{224... | collective-permute-start | bytes 589832 | tf_op jit(solution)/shard_map/ppermute | solution.py:207
  24.6 10.9 %collective-permute-start.11 = (bf16[48,2048]{1,0:T(8,128)(2,1)S(1)}, bf16[48,2048]{1,0:T(8,128)(2,1)S(1)}, u32[]{:S(2)}, u32[]{:S(2)}) collective-permute-start(bf16[48,2048]{1,0:T(8,128)(2,1)S(1)} %collective-permute-done.6.after2.refs_8_), channel_id=1, source_target_pairs={{0,224},{32,0},{64,32},{96,64},{128,96},{160,128},{192,160},{224,1... | collective-permute-start | bytes 589832 | tf_op jit(solution)/shard_map/ppermute | solution.py:208
  29.8 6.7 %collective-permute-start.12 = (bf16[48,2048]{1,0:T(8,128)(2,1)S(1)}, bf16[48,2048]{1,0:T(8,128)(2,1)S(1)}, u32[]{:S(2)}, u32[]{:S(2)}) collective-permute-start(bf16[48,2048]{1,0:T(8,128)(2,1)S(1)} %collective-permute-done.2.after1.refs_0_), channel_id=1, source_target_pairs={{0,32},{32,64},{64,96},{96,128},{128,160},{160,192},{192,224},{224... | collective-permute-start | bytes 589832 | tf_op jit(solution)/shard_map/ppermute | solution.py:224
  30.0 6.4 %collective-permute-start.13 = (bf16[48,2048]{1,0:T(8,128)(2,1)S(1)}, bf16[48,2048]{1,0:T(8,128)(2,1)S(1)}, u32[]{:S(2)}, u32[]{:S(2)}) collective-permute-start(bf16[48,2048]{1,0:T(8,128)(2,1)S(1)} %collective-permute-done.9.after2.refs_3_), channel_id=1, source_target_pairs={{0,224},{32,0},{64,32},{96,64},{128,96},{160,128},{192,160},{224,1... | collective-permute-start | bytes 589832 | tf_op jit(solution)/shard_map/ppermute | solution.py:224
  36.4 8.3 %collective-permute-start.14 = (f32[10,96,128]{2,1,0:T(8,128)S(1)}, f32[10,96,128]{2,1,0:T(8,128)S(1)}, u32[]{:S(2)}, u32[]{:S(2)}) collective-permute-start(f32[10,96,128]{2,1,0:T(8,128)S(1)} %get-tuple-element.41), channel_id=1, source_target_pairs={{0,1},{1,0},{2,3},{3,2},{4,5},{5,4},{6,7},{7,6},{8,9},{9,8},{10,11... | collective-permute-start | bytes 1474568 | tf_op jit(solution)/shard_map/ppermute | solution.py:236
  43.1 1.7 %collective-permute-start.15 = (f32[6,96,128]{2,1,0:T(8,128)S(1)}, f32[6,96,128]{2,1,0:T(8,128)S(1)}, u32[]{:S(2)}, u32[]{:S(2)}) collective-permute-start(f32[6,96,128]{2,1,0:T(8,128)S(1)} %get-tuple-element.42), channel_id=1, source_target_pairs={{0,1},{1,0},{2,3},{3,2},{4,5},{5,4},{6,7},{7,6},{8,9},{9,8},{10,11... | collective-permute-start | bytes 884744 | tf_op jit(solution)/shard_map/ppermute | solution.py:238
